TPU v7x, 32 devices: a whole 2x2x4 slice. The times are simulated.
32 devices in a mesh: wide: 8 (over y, x, core), narrow: 4 (over z).
Axes of the slice: x: 2, y: 2, z: 4, core: 2. Of those that a mesh axis runs over, the one named last changes fastest.
Arguments:
- tokens: bfloat16 [32768, 512], P('wide'), may hold values from -6 to 6
- cotangent: bfloat16 [32768, 512], P('wide'), may hold values from -6 to 6
- segment_ids: int32 [8, 4096], P('wide'), may hold values from 0 to 3, never falling along the last dimension, each value on 1 to 2560 neighbouring positions
- pad_mask: int32 [8, 4096], P('wide'), may hold values 0 or 1
- owner_order: int32 [192], replicated, may hold values from 0 to 191, as said below
- weights: float32 [4, 192, 64, 64], P('narrow', 'wide')
- first_moment: float32 [4, 192, 64, 64], P('narrow', 'wide')
- second_moment: float32 [4, 192, 64, 64], P('narrow', 'wide'), as said below
- average: float32 [4, 192, 64, 64], P('narrow', 'wide')
- stats: float32 [4, 192, 2, 64, 64], P('narrow', 'wide'), as said below
- bases: float32 [4, 192, 2, 64, 64], P('narrow', 'wide'), as said below
- gains: float32 [1024], P('wide'), may hold values from 0.5 to 1.5
- gain_first: float32 [1024], P('wide'), may hold values from -128 to 128
- gain_second: float32 [1024], P('wide'), may hold values from 1723.5968 to 6881.28
- gain_average: float32 [1024], P('wide'), may hold values from 0.5 to 1.5
Outputs:
- output: bfloat16 [32768, 512], P('wide')
- input_grad: float32 [32768, 512], P('wide')
- new_weights: float32 [4, 192, 64, 64], P('narrow', 'wide')
- new_first: float32 [4, 192, 64, 64], P('narrow', 'wide')
- new_second: float32 [4, 192, 64, 64], P('narrow', 'wide')
- new_average: float32 [4, 192, 64, 64], P('narrow', 'wide')
- new_stats: float32 [4, 192, 2, 64, 64], P('narrow', 'wide')
- new_bases: float32 [4, 192, 2, 64, 64], P('narrow', 'wide')
- new_gains: float32 [1024], P('wide')
- gain_moment: float32 [1024], P('wide')
- gain_square: float32 [1024], P('wide')
- gain_mean: float32 [1024], P('wide')
Inputs may be any that keep to these rules, and one draw needn't show every extreme that they name: `segment_ids`: within a row segment numbers never fall; a segment holds at most 2560 positions. `owner_order`: each block number appears exactly once. `second_moment`: Positive. `stats`: each matrix is symmetric positive definite. `bases`: each matrix is orthogonal.
All inputs are finite; a program needn't handle non-finite values. No bound on the sum of `pad_mask` on one device may be relied on, other than what follows from the above.
Results may differ from a plain program's by a relative error of at most 0.025.
Values may be sent and summed in bfloat16 or wider, within the bound.
A program may use at most 192 MiB of HBM per device.

v0:
```python
from functools import partial

import jax
import jax.numpy as jnp
from jax import lax
from jax.sharding import PartitionSpec as P

HEADS = 8
HD = 64
FF = 2048


beta_one = 0.9
beta_two = 0.95
step_rate = 0.1
gain_rate = 0.75
weight_decay = 0.01
average_keep = 0.5
norm_eps = 1e-05
step_eps = 1e-08
masked_score = -1e30
highest = lax.Precision.HIGHEST


def normalize(values):
    center = jnp.mean(values, axis=-1, keepdims=True)
    centered = values - center
    variance = jnp.mean(centered * centered, axis=-1, keepdims=True)
    return centered * lax.rsqrt(variance + norm_eps)


def scaled_norm(values, gain):
    return normalize(values) * gain


def exact_gelu(values):
    return jax.nn.gelu(values, approximate=False)


def assemble(blocks, rows, cols):
    size = blocks.shape[-1]
    grid = blocks.reshape(rows // size, cols // size, size, size)
    return grid.transpose(0, 2, 1, 3).reshape(rows, cols)


def to_blocks(matrix, size):
    rows, cols = matrix.shape
    return (
        matrix.reshape(rows // size, size, cols // size, size)
        .transpose(0, 2, 1, 3)
        .reshape(-1, size, size)
    )


def masked_scores(query_rows, key_rows, seg_row, pad_row, block, scale, index):
    start = index * block
    query_block = lax.dynamic_slice_in_dim(query_rows, start, block, 0)
    query_pos = start + jnp.arange(block, dtype=jnp.int32)
    query_seg = lax.dynamic_slice_in_dim(seg_row, start, block, 0)
    positions = jnp.arange(seg_row.shape[0], dtype=jnp.int32)
    allowed = (query_seg[:, None] == seg_row[None, :]) & (
        (pad_row[None, :] == 1) | (query_pos[:, None] == positions[None, :])
    )
    scores = (
        jnp.einsum("qhd,khd->hqk", query_block, key_rows, preferred_element_type=jnp.float32)
        * scale
    )
    return (query_block, jnp.where(allowed[None], scores, masked_score))


def attend_forward(query_rows, key_rows, value_rows, seg_row, pad_row, block, scale, index):
    _, masked = masked_scores(query_rows, key_rows, seg_row, pad_row, block, scale, index)
    peak = jnp.max(masked, axis=-1, keepdims=True)
    total = peak + jnp.log(jnp.sum(jnp.exp(masked - peak), axis=-1, keepdims=True))
    probs = jnp.exp(masked - total).astype(jnp.bfloat16)
    attended = jnp.einsum("hqk,khd->qhd", probs, value_rows, preferred_element_type=jnp.float32)
    return (attended, total[..., 0])


def attend_backward(
    query_rows,
    key_rows,
    value_rows,
    seg_row,
    pad_row,
    back_attended,
    block,
    scale,
    carry,
    step_inputs,
):
    back_keys, back_values = carry
    index, total = step_inputs
    query_block, masked = masked_scores(query_rows, key_rows, seg_row, pad_row, block, scale, index)
    probs = jnp.exp(masked - total[:, :, None])
    probs_low = probs.astype(jnp.bfloat16)
    back_block = lax.dynamic_slice_in_dim(back_attended, index * block, block, 0)
    back_values = back_values + jnp.einsum(
        "hqk,qhd->khd", probs_low, back_block, preferred_element_type=jnp.float32
    )
    back_probs = jnp.einsum(
        "qhd,khd->hqk", back_block, value_rows, preferred_element_type=jnp.float32
    )
    back_scores = (
        probs * (back_probs - jnp.sum(probs * back_probs, axis=-1, keepdims=True))
    ).astype(jnp.bfloat16)
    back_query = (
        jnp.einsum("hqk,khd->qhd", back_scores, key_rows, preferred_element_type=jnp.float32)
        * scale
    )
    back_keys = (
        back_keys
        + jnp.einsum("hqk,qhd->khd", back_scores, query_block, preferred_element_type=jnp.float32)
        * scale
    )
    return ((back_keys, back_values), back_query)


def orthonormal(matrix):
    gram = jnp.einsum("...ji,...jk->...ik", matrix, matrix, precision=highest)
    lower = jnp.linalg.cholesky(gram)
    solved = jax.scipy.linalg.solve_triangular(lower, jnp.swapaxes(matrix, -1, -2), lower=True)
    return jnp.swapaxes(solved, -1, -2)


def soap_update(grad, weight, first, second, average, stats, bases):
    left = bases[..., 0, :, :]
    right = bases[..., 1, :, :]
    new_first = beta_one * first + (1.0 - beta_one) * grad
    rotated = jnp.einsum(
        "...ji,...jk->...ik",
        left,
        jnp.einsum("...jk,...kl->...jl", grad, right, precision=highest),
        precision=highest,
    )
    new_second = beta_two * second + (1.0 - beta_two) * rotated * rotated
    moment_rot = jnp.einsum(
        "...ji,...jk->...ik",
        left,
        jnp.einsum("...jk,...kl->...jl", new_first, right, precision=highest),
        precision=highest,
    )
    scaled = moment_rot / (jnp.sqrt(new_second) + step_eps)
    direction = jnp.einsum(
        "...ij,...jk->...ik",
        left,
        jnp.einsum("...jk,...lk->...jl", scaled, right, precision=highest),
        precision=highest,
    )
    new_weight = weight - step_rate * (direction + weight_decay * weight)
    new_average = average_keep * average + (1.0 - average_keep) * new_weight
    left_stat = beta_two * stats[..., 0, :, :] + (1.0 - beta_two) * jnp.einsum(
        "...ik,...jk->...ij", grad, grad, precision=highest
    )
    right_stat = beta_two * stats[..., 1, :, :] + (1.0 - beta_two) * jnp.einsum(
        "...ki,...kj->...ij", grad, grad, precision=highest
    )
    new_left = orthonormal(jnp.einsum("...ij,...jk->...ik", left_stat, left, precision=highest))
    new_right = orthonormal(jnp.einsum("...ij,...jk->...ik", right_stat, right, precision=highest))
    return (
        new_weight,
        new_first,
        new_second,
        new_average,
        jnp.stack([left_stat, right_stat], axis=-3),
        jnp.stack([new_left, new_right], axis=-3),
    )


def adam_gains(grad, gain, first, second, average):
    new_first = beta_one * first + (1.0 - beta_one) * grad
    new_second = beta_two * second + (1.0 - beta_two) * grad * grad
    new_gain = gain - gain_rate * new_first / (jnp.sqrt(new_second) + step_eps)
    new_average = average_keep * average + (1.0 - average_keep) * new_gain
    return (new_gain, new_first, new_second, new_average)


def body(
    tokens,
    cotangent,
    segment_ids,
    pad_mask,
    owner_order,
    weights,
    first_moment,
    second_moment,
    average,
    stats,
    bases,
    gains,
    gain_first,
    gain_second,
    gain_average,
):
    narrow = lax.axis_size("narrow")
    heads_here = HEADS // narrow
    units_here = FF // narrow
    span = heads_here * HD
    size = weights.shape[-1]
    width = tokens.shape[1]
    rows = tokens.shape[0]
    block_count = owner_order.shape[0]
    gathered, gain_all = (
        lax.all_gather(weights.astype(jnp.bfloat16), "wide", axis=1, tiled=True),
        lax.all_gather(gains.astype(jnp.bfloat16), "wide", axis=0, tiled=True),
    )
    slot_of = (
        jnp.zeros((block_count,), jnp.int32)
        .at[owner_order]
        .set(jnp.arange(block_count, dtype=jnp.int32))
    )
    blocks = gathered[0][slot_of]
    first_end = width // size * (3 * span // size)
    second_end = first_end + span // size * (width // size)
    third_end = second_end + width // size * (units_here // size)
    mixing = assemble(blocks[:first_end], width, 3 * span)
    out_weight = assemble(blocks[first_end:second_end], span, width)
    up_weight = assemble(blocks[second_end:third_end], width, units_here)
    down_weight = assemble(blocks[third_end:], units_here, width)
    gain_values = gain_all.astype(jnp.float32)
    gain_one = gain_values[:width]
    gain_two = gain_values[width:]
    seg_row = segment_ids[0]
    pad_row = pad_mask[0]
    pad_float = pad_row.astype(jnp.float32)
    inputs = tokens.astype(jnp.float32)
    normed_one = scaled_norm(inputs, gain_one).astype(jnp.bfloat16)
    mixed = jnp.dot(normed_one, mixing, preferred_element_type=jnp.float32).astype(jnp.bfloat16)
    query_rows = mixed[:, :span].reshape(rows, heads_here, HD)
    key_rows = mixed[:, span : 2 * span].reshape(rows, heads_here, HD)
    value_rows = mixed[:, 2 * span :].reshape(rows, heads_here, HD)
    block = min(512, rows)
    count = rows // block
    scale = HD ** (-0.5)
    forward_fn = partial(
        attend_forward, query_rows, key_rows, value_rows, seg_row, pad_row, block, scale
    )
    attended, totals = lax.map(forward_fn, jnp.arange(count, dtype=jnp.int32))
    attended = (
        (attended.reshape(rows, heads_here, HD) * pad_float[:, None, None])
        .astype(jnp.bfloat16)
        .reshape(rows, span)
    )
    branch_part = jnp.dot(attended, out_weight, preferred_element_type=jnp.float32)
    residual = inputs + lax.psum(branch_part.astype(jnp.bfloat16), "narrow").astype(jnp.float32)
    normed_full, second_back = jax.vjp(scaled_norm, residual, gain_two)
    normed_two = normed_full.astype(jnp.bfloat16)
    up = jnp.dot(normed_two, up_weight, preferred_element_type=jnp.float32)
    active_full, gelu_back = jax.vjp(exact_gelu, up)
    active = active_full.astype(jnp.bfloat16)
    down_part = jnp.dot(active, down_weight, preferred_element_type=jnp.float32)
    output = (
        residual + lax.psum(down_part.astype(jnp.bfloat16), "narrow").astype(jnp.float32)
    ).astype(jnp.bfloat16)
    grad_down = jnp.einsum("tf,td->fd", active, cotangent, preferred_element_type=jnp.float32)
    back_active = jnp.einsum(
        "td,fd->tf", cotangent, down_weight, preferred_element_type=jnp.float32
    )
    back_up = gelu_back(back_active)[0].astype(jnp.bfloat16)
    grad_up = jnp.einsum("td,tf->df", normed_two, back_up, preferred_element_type=jnp.float32)
    back_normed_two = jnp.einsum(
        "tf,df->td", back_up, up_weight, preferred_element_type=jnp.float32
    )
    back_two_full = lax.psum(back_normed_two.astype(jnp.bfloat16), "narrow").astype(jnp.float32)
    from_norm, grad_gain_two = second_back(back_two_full)
    back_residual = cotangent.astype(jnp.float32) + from_norm
    back_branch = back_residual.astype(jnp.bfloat16)
    grad_out = jnp.einsum("tc,td->cd", attended, back_branch, preferred_element_type=jnp.float32)
    back_attended = jnp.einsum(
        "td,cd->tc", back_branch, out_weight, preferred_element_type=jnp.float32
    ).astype(jnp.bfloat16)
    back_attended = (back_attended * pad_row.astype(jnp.bfloat16)[:, None]).reshape(
        rows, heads_here, HD
    )
    backward_fn = partial(
        attend_backward,
        query_rows,
        key_rows,
        value_rows,
        seg_row,
        pad_row,
        back_attended,
        block,
        scale,
    )
    zeros_rows = jnp.zeros((rows, heads_here, HD), jnp.float32)
    (back_keys, back_values), back_queries = lax.scan(
        backward_fn, (zeros_rows, zeros_rows), (jnp.arange(count, dtype=jnp.int32), totals)
    )
    back_mixed = jnp.concatenate(
        [
            back_queries.reshape(rows, span),
            back_keys.reshape(rows, span),
            back_values.reshape(rows, span),
        ],
        axis=1,
    ).astype(jnp.bfloat16)
    grad_mixing = jnp.einsum(
        "td,tc->dc", normed_one, back_mixed, preferred_element_type=jnp.float32
    )
    back_normed_one = jnp.einsum(
        "tc,dc->td", back_mixed, mixing, preferred_element_type=jnp.float32
    )
    back_one_full = lax.psum(back_normed_one.astype(jnp.bfloat16), "narrow").astype(jnp.float32)
    _, first_back = jax.vjp(scaled_norm, inputs, gain_one)
    from_first, grad_gain_one = first_back(back_one_full)
    input_grad = back_residual + from_first
    gain_grad = jnp.concatenate([grad_gain_one, grad_gain_two])
    grad_blocks = jnp.concatenate(
        [
            to_blocks(grad_mixing, size),
            to_blocks(grad_out, size),
            to_blocks(grad_up, size),
            to_blocks(grad_down, size),
        ],
        axis=0,
    )
    slot_grads = grad_blocks[owner_order]
    own_grad, own_gain_grad = (
        lax.psum_scatter(
            slot_grads.astype(jnp.bfloat16), "wide", scatter_dimension=0, tiled=True
        ).astype(jnp.float32),
        lax.psum_scatter(
            gain_grad.astype(jnp.bfloat16), "wide", scatter_dimension=0, tiled=True
        ).astype(jnp.float32),
    )
    new_weight, new_first, new_second, new_average, new_stats, new_bases = soap_update(
        own_grad[None], weights, first_moment, second_moment, average, stats, bases
    )
    new_gains, gain_moment, gain_square, gain_mean = adam_gains(
        own_gain_grad, gains, gain_first, gain_second, gain_average
    )
    return (
        output,
        input_grad,
        new_weight,
        new_first,
        new_second,
        new_average,
        new_stats,
        new_bases,
        new_gains,
        gain_moment,
        gain_square,
        gain_mean,
    )


def solution(mesh):
    placed = (
        P("wide", None),
        P("wide", None),
        P("wide", None),
        P("wide", None),
        P(),
        P("narrow", "wide", None, None),
        P("narrow", "wide", None, None),
        P("narrow", "wide", None, None),
        P("narrow", "wide", None, None),
        P("narrow", "wide", None, None, None),
        P("narrow", "wide", None, None, None),
        P("wide"),
        P("wide"),
        P("wide"),
        P("wide"),
    )
    return jax.shard_map(
        body,
        mesh=mesh,
        in_specs=placed,
        out_specs=(
            P("wide", None),
            P("wide", None),
            P("narrow", "wide", None, None),
            P("narrow", "wide", None, None),
            P("narrow", "wide", None, None),
            P("narrow", "wide", None, None),
            P("narrow", "wide", None, None, None),
            P("narrow", "wide", None, None, None),
            P("wide"),
            P("wide"),
            P("wide"),
            P("wide"),
        ),
        check_vma=False,
    )
```

profile of v0, /device:TPU:0, one launch (start us, length us, event | category | flops | bytes accessed | tf_op | source)
XLA Modules:
  0.0 1682.4 jit_solution(14273510150274380255)
XLA Ops:
  29.7 15.9 all-gather.3.cloned.1.call-done
  60.9 140.6 %while.29 = (s32[]{:T(128)}, f32[8,512,2,64]{1,3,2,0:T(8,128)}, f32[8,2,512]{2,1,0:T(2,128)S(1)}, s32[8]{0:T(128)S(1)}, s32[4096]{0:T(1024)S(1)}, /*index=5*/s32...) while((s32[]{:T(128)}, f32[8,512,2,64]{1,3,2,0:T(8,128)}, ...), condition=%wide.region_6.7_spmd.clone, body=%wide.region_3.6_spmd.sunk.clone | while | flops 1128271360 | bytes 61294784 | solution.py:238
  214.2 149.3 %all-reduce.6.cloned.1.call-done = bf16[4096,512]{1,0:T(8,128)(2,1)} async-done(((bf16[4096,512]{1,0:T(8,128)(2,1)}), bf16[4096,512]{1,0:T(8,128)(2,1)}) %all-reduce.6.cloned.1.call-update) | async-done | bytes 4194320 | tf_op jit(solution)/shard_map/psum | solution.py:245
  374.0 20.7 %multiply_convert_fusion.1 = (bf16[4096,512]{1,0:T(8,128)(2,1)}, f32[4096,512]{1,0:T(8,128)S(1)}, f32[4096,512]{1,0:T(8,128)}) fusion(bf16[4096,512]{1,0:T(8,128)(2,1)S(1)} %multiply_convert_fusion.2, bf16[512,512]{1,0:T(8,128)(2,1)S(1)} %reshape.466), kind=kOutput, calls=%fused_computation.92 | convolution fusion | flops 2283798528 | bytes 25690112 | tf_op jit(solution)/shard_map/dot_general | solution.py:248
  435.5 126.2 %all-reduce.8.cloned.1.call-done = bf16[4096,512]{1,0:T(8,128)(2,1)} async-done(((bf16[4096,512]{1,0:T(8,128)(2,1)}), bf16[4096,512]{1,0:T(8,128)(2,1)}) %all-reduce.8.cloned.1.call-update) | async-done | bytes 4194320 | tf_op jit(solution)/shard_map/psum | solution.py:264
  581.1 416.0 %while.30 = (s32[]{:T(128)}, f32[4096,2,64]{0,2,1:T(8,128)S(1)}, f32[4096,2,64]{0,2,1:T(8,128)}, bf16[8,512,2,64]{1,3,2,0:T(8,128)(2,1)}, s32[8]{0:T(128)S(1)}, ...) while((s32[]{:T(128)}, f32[4096,2,64]{0,2,1:T(8,128)S(1)}, ...), condition=%wide.region_16.17_spmd.clone.clone, body=%wide.region_14.16_spmd.clone.sunk.clone | while | flops 2758348288 | bytes 217921824 | solution.py:287
  602.0 12.7 multiply_reduce_fusion.4
  614.7 12.3 multiply_convert_fusion.7
  654.0 12.7 multiply_reduce_fusion.4
  706.0 12.7 multiply_reduce_fusion.4
  757.9 12.7 multiply_reduce_fusion.4
  770.7 12.3 multiply_convert_fusion.7
  809.9 12.7 multiply_reduce_fusion.4
  822.6 12.3 multiply_convert_fusion.7
  861.9 12.7 multiply_reduce_fusion.4
  913.9 12.7 multiply_reduce_fusion.4
  965.8 12.7 multiply_reduce_fusion.4
  1045.6 19.3 %reduce-scatter.2.cloned.1.call-done = bf16[24,64,64]{2,1,0:T(8,128)(2,1)} async-done(((bf16[192,64,64]{2,1,0:T(8,128)(2,1)}), bf16[24,64,64]{2,1,0:T(8,128)(2,1)}) %reduce-scatter.2.cloned.1.call-update) | async-done | bytes 196624 | tf_op jit(solution)/shard_map/reduce_scatter | solution.py:320
  1094.8 142.1 %custom-call.12 = f32[1,24,64,64]{3,2,1,0:T(8,128)} custom-call(f32[1,24,64,64]{3,2,1,0:T(8,128)} %fusion.96), custom_call_target="Cholesky" | custom-call | tf_op jit(solution)/shard_map/jit(cholesky)/cholesky | solution.py:121
  1242.5 142.3 %custom-call.10 = f32[1,24,64,64]{3,2,1,0:T(8,128)} custom-call(f32[1,24,64,64]{3,2,1,0:T(8,128)} %fusion.98), custom_call_target="Cholesky" | custom-call | tf_op jit(solution)/shard_map/jit(cholesky)/cholesky | solution.py:121
  1389.2 119.3 %custom-call.11 = f32[24,1,64,64]{2,3,1,0:T(8,128)} custom-call(f32[24,1,64,64]{3,2,1,0:T(8,128)} %get-tuple-element.308), custom_call_target="InvertDiagBlocksLowerTriangular" | custom-call | tf_op jit(solution)/shard_map/jit(_solve_triangular)/vmap()/triangular_solve | solution.py:122
  1508.6 119.3 %custom-call.13 = f32[24,1,64,64]{2,3,1,0:T(8,128)} custom-call(f32[24,1,64,64]{3,2,1,0:T(8,128)} %get-tuple-element.309), custom_call_target="InvertDiagBlocksLowerTriangular" | custom-call | tf_op jit(solution)/shard_map/jit(_solve_triangular)/vmap()/triangular_solve | solution.py:122
  1647.6 12.8 all-reduce
  1661.0 14.7 add_add_fusion.2
  (450 shorter events, 634.2 us)
Async XLA Ops:
  7.2 38.3 %all-gather.3.cloned.1.call-start = ((), (), s32[]{:S(2)}) async-start(), calls=%async_computation.1 | async-start | bytes 3538944 | tf_op jit(solution)/shard_map/all_gather | solution.py:204
  9.2 354.4 %all-reduce.6.cloned.1.call-start = ((), (), s32[]{:S(2)}) async-start(), calls=%async_computation.2 | async-start | bytes 8388608 | tf_op jit(solution)/shard_map/psum | solution.py:245
  10.7 12.1 copy-start.57
  22.8 33.7 %copy-start.51 = (f32[4,1,128]{2,1,0:T(1,128)}, f32[4,1,128]{2,1,0:T(1,128)S(1)}, u32[]{:S(2)}) copy-start(f32[4,1,128]{2,1,0:T(1,128)S(1)} %get-tuple-element.311) | copy-start | bytes 6148
  25.7 35.0 %copy-start.41 = (f32[4096]{0:T(1024)}, f32[4096]{0:T(1024)S(1)}, u32[]{:S(2)}) copy-start(f32[4096]{0:T(1024)S(1)} %broadcast_multiply_fusion.1) | copy-start | bytes 49156
  29.6 31.0 %copy-start.44 = (f32[4096]{0:T(1024)}, f32[4096]{0:T(1024)S(1)}, u32[]{:S(2)}) copy-start(f32[4096]{0:T(1024)S(1)} %fusion.110) | copy-start | bytes 49156
  208.5 353.2 %all-reduce.8.cloned.1.call-start = ((), (), s32[]{:S(2)}) async-start(), calls=%async_computation.3 | async-start | bytes 8388608 | tf_op jit(solution)/shard_map/psum | solution.py:264
  374.0 20.7 %copy-start.23 = (bf16[4096,512]{1,0:T(8,128)(2,1)}, bf16[4096,512]{1,0:T(8,128)(2,1)S(1)}, u32[]{:S(2)}) copy-start(bf16[4096,512]{1,0:T(8,128)(2,1)S(1)} %multiply_convert_fusion.2) | copy-start | bytes 12582916
  374.0 20.7 %copy-start.13 = (bf16[4096,512]{1,0:T(8,128)(2,1)S(1)}, bf16[4096,512]{1,0:T(8,128)(2,1)}, u32[]{:S(2)}) copy-start(bf16[4096,512]{1,0:T(8,128)(2,1)} %param.23) | copy-start | bytes 12582916
  374.0 20.7 %copy-start.40 = (bf16[512,512]{1,0:T(8,128)(2,1)S(1)}, bf16[512,512]{1,0:T(8,128)(2,1)}, u32[]{:S(2)}) copy-start(bf16[512,512]{1,0:T(8,128)(2,1)} %reshape.468) | copy-start | bytes 1572868
  407.6 657.4 %reduce-scatter.2.cloned.1.call-start = ((), (), s32[]{:S(2)}) async-start(), calls=%async_computation.4 | async-start | bytes 3538944 | tf_op jit(solution)/shard_map/reduce_scatter | solution.py:320
  1019.5 617.2 %all-reduce.10.cloned.1.call-start = ((), (), s32[]{:S(2)}) async-start(), calls=%async_computation.5 | async-start | bytes 16777216 | tf_op jit(solution)/shard_map/psum | solution.py:253
  1030.8 12.4 copy-start.63
  1030.8 34.2 %copy-start.12 = (f32[1,24,2,64,64]{4,3,2,1,0:T(8,128)S(1)}, f32[1,24,2,64,64]{4,3,2,1,0:T(8,128)}, u32[]{:S(2)}) copy-start(f32[1,24,2,64,64]{4,3,2,1,0:T(8,128)} %param.32) | copy-start | bytes 2359300
  1074.3 12.0 copy-start.16
  1238.4 146.4 %copy-start.55 = (pred[64,64]{1,0:T(8,128)(4,1)S(1)}, pred[64,64]{1,0:T(8,128)(4,1)}, u32[]{:S(2)}) copy-start(pred[64,64]{1,0:T(8,128)(4,1)} %iota_compare_fusion.3) | copy-start | bytes 12292
  1238.4 148.1 %copy-start.54 = (pred[64,64]{1,0:T(8,128)(4,1)S(1)}, pred[64,64]{1,0:T(8,128)(4,1)}, u32[]{:S(2)}) copy-start(pred[64,64]{1,0:T(8,128)(4,1)} %iota_compare_fusion.2) | copy-start | bytes 12292
  1242.5 392.4 %copy-start.19 = (f32[24,64,64]{1,2,0:T(8,128)S(1)}, f32[24,64,64]{1,2,0:T(8,128)}, u32[]{:S(2)}) copy-start(f32[24,64,64]{1,2,0:T(8,128)} %copy-done.18) | copy-start | bytes 1179652
  1242.5 392.4 %copy-start.21 = (f32[24,64,64]{1,2,0:T(8,128)S(1)}, f32[24,64,64]{1,2,0:T(8,128)}, u32[]{:S(2)}) copy-start(f32[24,64,64]{1,2,0:T(8,128)} %copy-done.20) | copy-start | bytes 1179652
  1636.8 23.6 %copy-start.59 = (f32[128]{0:T(128)S(1)}, f32[128]{0:T(128)}, u32[]{:S(2)}) copy-start(f32[128]{0:T(128)} %param.33) | copy-start | bytes 1540
  1636.8 23.6 %copy-start.60 = (f32[128]{0:T(128)S(1)}, f32[128]{0:T(128)}, u32[]{:S(2)}) copy-start(f32[128]{0:T(128)} %param.36) | copy-start | bytes 1540
  1636.8 23.6 %copy-start.61 = (f32[128]{0:T(128)S(1)}, f32[128]{0:T(128)}, u32[]{:S(2)}) copy-start(f32[128]{0:T(128)} %param.34) | copy-start | bytes 1540
  1636.8 23.6 %copy-start.62 = (f32[128]{0:T(128)S(1)}, f32[128]{0:T(128)}, u32[]{:S(2)}) copy-start(f32[128]{0:T(128)} %param.35) | copy-start | bytes 1540
  1636.8 24.2 %copy-start.48 = (f32[4096]{0:T(1024)S(1)}, f32[4096]{0:T(1024)}, u32[]{:S(2)}) copy-start(f32[4096]{0:T(1024)} %copy-done.47) | copy-start | bytes 49156
  (61 other events, 333.0 us)
Sparse Core Ops, SparseCore 0:
  10.5 35.0 all-gather.2
  208.6 154.9 all-reduce.5
  407.7 153.9 all-reduce.7
  1019.6 45.2 reduce-scatter.1
  1068.1 291.6 all-reduce.9
where the time goes:
time: 1690 us; the launch traced here: 1680 us
  other arithmetic  782 us (46%)
  matrix products  401 us (24%)
  waiting for transfers between devices  311 us (18%)
  local copies, waits for them, and re-layouts  137 us (8%)
  blocking collectives  23 us (1%)
    another operation x5, other arithmetic, orthonormal(): lower = jnp.linalg.cholesky(gram)  287 us
    another operation x4, other arithmetic, orthonormal(): jax.scipy.linalg.solve_triangular(lower, jnp.swapaxes(matrix, -1, -2), lo...  242 us
    psum x1, waiting for transfers between devices, body(): lax.psum(branch_part.astype(jnp.bfloat16), 'narrow').astype(jnp.float32)  149 us
    psum x1, waiting for transfers between devices, body(): lax.psum(back_normed_two.astype(jnp.bfloat16), 'narrow').astype(jnp.float32)  126 us
    dot_general x8, matrix products, attend_backward(): jnp.einsum('qhd,khd->hqk', back_block, value_rows, preferred_element_type...  102 us
    convert_element_type x8, other arithmetic, attend_backward(): back_scores = (probs * (back_probs - jnp.sum(probs * back_probs, axis=-1,...  98.3 us
    dot_general x8, matrix products, attend_backward(): jnp.einsum('hqk,qhd->khd', probs_low, back_block, preferred_element_type=...  60.8 us
    dot_general x16, matrix products, masked_scores(): jnp.einsum('qhd,khd->hqk', query_block, key_rows, preferred_element_type=...  56.2 us
  transfers between devices with their start and end apart: 5, of which 4 were waited for; matrix products, arithmetic and copies ran while one was open for 38% of the time, Pallas kernels for 0%

commit v1 on v0

v1 whole, which is shorter than its diff:
```python
import functools

import jax
import jax.numpy as jnp
from jax import lax
from jax.experimental import pallas as pl
from jax.experimental.pallas import tpu as pltpu
from jax.sharding import PartitionSpec as P

HEADS = 8
HD = 64
FF = 2048
LANES = 128
SEGS = 4
NEG = -1e30
F32 = jnp.float32
BF = jnp.bfloat16
highest = lax.Precision.HIGHEST

beta_one = 0.9
beta_two = 0.95
step_rate = 0.1
gain_rate = 0.75
weight_decay = 0.01
average_keep = 0.5
norm_eps = 1e-05
step_eps = 1e-08


def nt(a, b):
    return lax.dot_general(a, b, (((1,), (1,)), ((), ())), preferred_element_type=F32)


def nn(a, b):
    return lax.dot_general(a, b, (((1,), (0,)), ((), ())), preferred_element_type=F32)


def tn(a, b):
    return lax.dot_general(a, b, (((0,), (0,)), ((), ())), preferred_element_type=F32)


def split3(x):
    hi = x.astype(BF)
    r = x - hi.astype(F32)
    mid = r.astype(BF)
    lo = (r - mid.astype(F32)).astype(BF)
    return hi, mid, lo


def put3(base, x, lane0):
    lane = lax.broadcasted_iota(jnp.int32, base.shape, 1)
    hi, mid, lo = split3(x)
    out = jnp.where(lane == lane0, hi.astype(F32), base.astype(F32))
    out = jnp.where(lane == lane0 + 1, mid.astype(F32), out)
    out = jnp.where(lane == lane0 + 2, lo.astype(F32), out)
    return out.astype(BF)


VT = 80
QC, AHEAD, QB, BAHEAD = 512, 1, 256, 1


def fwd_kernel(heads, bq, bk, lo_ref, hi_ref, qe_ref, ke_ref, vt_ref, pad_ref, att_ref, qb_ref, m_ref, acc_ref):
    i = pl.program_id(0)
    row0 = pl.multiple_of(i * bq, bq)
    real = pad_ref[...] > 0.5
    for h in range(heads):
        qt = qe_ref[h].astype(F32).T[:HD]
        kt = ke_ref[h, pl.ds(row0, bq), :].astype(F32).T[:HD]
        own = jnp.sum(qt * kt, axis=0, keepdims=True)
        m_ref[h] = jnp.where(real, NEG, own)
        acc_ref[h] = jnp.where(real, 0.0, vt_ref[h, :, pl.ds(row0, bq)].astype(F32))

    def step(j, _):
        col0 = pl.multiple_of(j * bk, bk)
        work = [(h, slice(c, c + QC)) for c in range(0, bq, QC) for h in range(heads)]
        score = lambda h, c: nt(ke_ref[h, pl.ds(col0, bk), :], qe_ref[h, c, :])
        ss = [score(*w) for w in work[:AHEAD]]
        for n, (h, c) in enumerate(work):
            if n + AHEAD < len(work):
                ss.append(score(*work[n + AHEAD]))
            s = ss[n]
            m_old = m_ref[h, :, c]
            m_new = jnp.maximum(m_old, jnp.max(s, axis=0, keepdims=True))
            p = jnp.exp(s - m_new).astype(BF)
            alpha = jnp.exp(m_old - m_new)
            acc_ref[h, :, c] = acc_ref[h, :, c] * alpha + nn(vt_ref[h, :, pl.ds(col0, bk)], p)
            m_ref[h, :, c] = m_new
        return 0

    lax.fori_loop(lo_ref[i], hi_ref[i], step, 0)
    outs = []
    for h in range(heads):
        acc = acc_ref[h]
        total = acc[HD : HD + 1]
        outs.append(jnp.where(real, acc[:HD] / total, 0.0))
        lse = jnp.broadcast_to(m_ref[h] + jnp.log(total), (8, bq)).T[:, :1]
        qb_ref[h] = put3(qe_ref[h], -lse, HD + 4)
    att_ref[...] = (jnp.concatenate(outs, axis=0) if heads > 1 else outs[0]).T.astype(BF)


def attend(qe, ke, vt, padw, lo, hi, bq, bk):
    heads, rows, _ = qe.shape
    full = lambda i, lo, hi: (0, 0, 0)
    return pl.pallas_call(
        functools.partial(fwd_kernel, heads, bq, bk),
        grid_spec=pltpu.PrefetchScalarGridSpec(
            num_scalar_prefetch=2,
            grid=(rows // bq,),
            in_specs=[
                pl.BlockSpec((heads, bq, LANES), lambda i, lo, hi: (0, i, 0)),
                pl.BlockSpec((heads, rows, LANES), full),
                pl.BlockSpec((heads, VT, rows), full),
                pl.BlockSpec((1, bq), lambda i, lo, hi: (0, i)),
            ],
            out_specs=[
                pl.BlockSpec((bq, heads * HD), lambda i, lo, hi: (i, 0)),
                pl.BlockSpec((heads, bq, LANES), lambda i, lo, hi: (0, i, 0)),
            ],
            scratch_shapes=[
                pltpu.VMEM((heads, 1, bq), F32),
                pltpu.VMEM((heads, VT, bq), F32),
            ],
        ),
        out_shape=[
            jax.ShapeDtypeStruct((rows, heads * HD), BF),
            jax.ShapeDtypeStruct((heads, rows, LANES), BF),
        ],
        compiler_params=pltpu.CompilerParams(vmem_limit_bytes=48 << 20),
        name="attend",
    )(lo, hi, qe, ke, vt, padw)


def bwd_kernel(heads, bq, bk, lo_ref, hi_ref, qb_ref, ke_ref, ve_ref, go_ref, att_ref, dq_ref, dk_ref, dv_ref, ge_ref, dqt_ref, kt_ref, qt_ref, got_ref, dkt_ref, dvt_ref):
    j = pl.program_id(0)
    rows = qb_ref.shape[1]

    @pl.when(j == 0)
    def _():
        for h in range(heads):
            dqt_ref[h] = jnp.zeros_like(dqt_ref[h])
            for c in range(rows // 512):
                sl = pl.ds(c * 512, 512)
                go = go_ref[sl, h * HD : (h + 1) * HD]
                at = att_ref[sl, h * HD : (h + 1) * HD]
                delta = jnp.sum(go.astype(F32) * at.astype(F32), axis=1, keepdims=True)
                wide = jnp.concatenate([go, jnp.zeros_like(go)], axis=1)
                ge_ref[h, sl, :] = put3(wide, -delta, HD)
                got_ref[h, :, c * 512 : (c + 1) * 512] = wide.T[:HD]
                qt_ref[h, :, c * 512 : (c + 1) * 512] = qb_ref[h, sl, :].T[:HD]

    for h in range(heads):
        kt_ref[h] = ke_ref[h].T[:HD]

    zero = jnp.zeros((HD, bk), F32)

    def step(i, carry):
        row0 = pl.multiple_of(i * bq, bq)
        work = [(h, pl.ds(row0 + c, QB)) for c in range(0, bq, QB) for h in range(heads)]
        score = lambda h, c: (nt(ke_ref[h], qb_ref[h, c, :]), nt(ve_ref[h], ge_ref[h, c, :]))
        ss = [score(*w) for w in work[:BAHEAD]]
        for n, (h, c) in enumerate(work):
            if n + BAHEAD < len(work):
                ss.append(score(*work[n + BAHEAD]))
            st, dt = ss[n]
            p = jnp.exp(st)
            ds = (p * dt).astype(BF)
            pb = p.astype(BF)
            dvt_ref[h] += nt(got_ref[h, :, c], pb)
            dkt_ref[h] += nt(qt_ref[h, :, c], ds)
            dqt_ref[h, :, c] += nn(kt_ref[h], ds)
        return 0

    for h in range(heads):
        dkt_ref[h] = zero
        dvt_ref[h] = zero
    lax.fori_loop(lo_ref[j], hi_ref[j], step, 0)
    for h in range(heads):
        dk_ref[:, h * HD : (h + 1) * HD] = dkt_ref[h].T.astype(BF)
        dv_ref[:, h * HD : (h + 1) * HD] = dvt_ref[h].T.astype(BF)

    @pl.when(j == pl.num_programs(0) - 1)
    def _():
        for h in range(heads):
            for c in range(rows // 512):
                sl = pl.ds(c * 512, 512)
                dq_ref[sl, h * HD : (h + 1) * HD] = (dqt_ref[h, :, c * 512 : (c + 1) * 512].T * (HD ** -0.5)).astype(BF)


def attend_back(qb, ke, ve, go, att, lo, hi, bq, bk):
    heads, rows, _ = qb.shape
    full3 = lambda i, lo, hi: (0, 0, 0)
    full2 = lambda i, lo, hi: (0, 0)
    blk3 = lambda i, lo, hi: (0, i, 0)
    blk2 = lambda i, lo, hi: (i, 0)
    wide = heads * HD
    return pl.pallas_call(
        functools.partial(bwd_kernel, heads, bq, bk),
        grid_spec=pltpu.PrefetchScalarGridSpec(
            num_scalar_prefetch=2,
            grid=(rows // bk,),
            in_specs=[
                pl.BlockSpec((heads, rows, LANES), full3),
                pl.BlockSpec((heads, bk, LANES), blk3),
                pl.BlockSpec((heads, bk, LANES), blk3),
                pl.BlockSpec((rows, wide), full2),
                pl.BlockSpec((rows, wide), full2),
            ],
            out_specs=[
                pl.BlockSpec((rows, wide), full2),
                pl.BlockSpec((bk, wide), blk2),
                pl.BlockSpec((bk, wide), blk2),
            ],
            scratch_shapes=[
                pltpu.VMEM((heads, rows, LANES), BF),
                pltpu.VMEM((heads, HD, rows), F32),
                pltpu.VMEM((heads, HD, bk), BF),
                pltpu.VMEM((heads, HD, rows), BF),
                pltpu.VMEM((heads, HD, rows), BF),
                pltpu.VMEM((heads, HD, bk), F32),
                pltpu.VMEM((heads, HD, bk), F32),
            ],
        ),
        out_shape=[jax.ShapeDtypeStruct((rows, wide), BF)] * 3,
        compiler_params=pltpu.CompilerParams(vmem_limit_bytes=48 << 20),
        name="attend_back",
    )(lo, hi, qb, ke, ve, go, att)


def dot_f32(a, b, dims):
    return lax.dot_general(a, b, ((dims[:1], dims[1:]), ((), ())), precision=highest, preferred_element_type=F32)


def soap_kernel(group, ga_ref, gb_ref, w_ref, m1_ref, m2_ref, av_ref, st_ref, ba_ref,
                nw_ref, n1_ref, n2_ref, na_ref, ns_ref, nb_ref, aug_ref):
    size = w_ref.shape[-1]
    half = size // 2
    panel = 8
    for s in range(group):
        wire = ga_ref[s * half : (s + 1) * half, :].astype(F32) + gb_ref[s * half : (s + 1) * half, :].astype(F32)
        grad = jnp.concatenate([wire[:, :size], wire[:, size:]], axis=0)
        left, right = ba_ref[0, s, 0], ba_ref[0, s, 1]
        weight = w_ref[0, s]
        first = beta_one * m1_ref[0, s] + (1.0 - beta_one) * grad
        n1_ref[0, s] = first
        both = dot_f32(jnp.concatenate([grad, first], axis=0), right, (1, 0))
        pair = dot_f32(left, jnp.concatenate([both[:size], both[size:]], axis=1), (0, 0))
        rotated, moment = pair[:, :size], pair[:, size:]
        second = beta_two * m2_ref[0, s] + (1.0 - beta_two) * rotated * rotated
        n2_ref[0, s] = second
        scaled = moment / (jnp.sqrt(second) + step_eps)
        direction = dot_f32(left, dot_f32(scaled, right, (1, 1)), (1, 0))
        fresh = weight - step_rate * (direction + weight_decay * weight)
        nw_ref[0, s] = fresh
        na_ref[0, s] = average_keep * av_ref[0, s] + (1.0 - average_keep) * fresh
        for side, base in ((0, left), (1, right)):
            outer = dot_f32(grad, grad, (1, 1) if side == 0 else (0, 0))
            stat = beta_two * st_ref[0, s, side] + (1.0 - beta_two) * outer
            ns_ref[0, s, side] = stat
            mt = dot_f32(base, stat, (0, 1))
            gram = dot_f32(mt, mt, (1, 1))
            aug_ref[2 * s + side] = jnp.concatenate([gram, mt], axis=1)
    count = 2 * group
    row = lax.broadcasted_iota(jnp.int32, (count, panel, LANES), 1)
    for p in range(size // panel):
        top = p * panel
        part = aug_ref[:, top : top + panel, :]
        for r in range(panel):
            pivot = lax.rsqrt(part[:, r : r + 1, top + r : top + r + 1])
            lead = part[:, r : r + 1, :] * pivot
            column = jnp.where(row > r, part[:, :, top + r : top + r + 1] * pivot, 0.0)
            part = jnp.where(row == r, lead, part - column * lead)
        aug_ref[:, top : top + panel, :] = part
        below = top + panel
        if below < size:
            for m in range(count):
                one = part[m]
                aug_ref[m, below:, :] -= dot_f32(one[:, below:size], one, (0, 0))
    for s in range(group):
        for side in range(2):
            nb_ref[0, s, side] = aug_ref[2 * s + side][:, size:].T


def soap(ga, gb, weights, first, second, average, stats, bases, group):
    _, slots, size, _ = weights.shape
    wire = pl.BlockSpec((group * size // 2, LANES), lambda i: (i, 0))
    four = pl.BlockSpec((1, group, size, size), lambda i: (0, i, 0, 0))
    five = pl.BlockSpec((1, group, 2, size, size), lambda i: (0, i, 0, 0, 0))
    like = lambda a: jax.ShapeDtypeStruct(a.shape, a.dtype)
    return pl.pallas_call(
        functools.partial(soap_kernel, group),
        grid=(slots // group,),
        in_specs=[wire, wire, four, four, four, four, five, five],
        out_specs=[four, four, four, four, five, five],
        out_shape=[like(a) for a in (weights, first, second, average, stats, bases)],
        scratch_shapes=[pltpu.VMEM((2 * group, size, LANES), F32)],
        compiler_params=pltpu.CompilerParams(vmem_limit_bytes=48 << 20),
        name="soap",
    )(ga, gb, weights, first, second, average, stats, bases)


def normalize(values):
    center = jnp.mean(values, axis=-1, keepdims=True)
    centered = values - center
    variance = jnp.mean(centered * centered, axis=-1, keepdims=True)
    scale = lax.rsqrt(variance + norm_eps)
    return centered * scale, scale


def norm_back(grad, xhat, scale):
    along = jnp.mean(grad * xhat, axis=-1, keepdims=True)
    return (grad - jnp.mean(grad, axis=-1, keepdims=True) - xhat * along) * scale


TAIL = 0.305
TAIL_FIT = (
    0.1216397411342051,
    0.12246669816059132,
    0.10342157025713879,
    0.1210193967312446,
    -0.037972477455618554,
    0.18571204369074895,
    -0.15298537812807472,
    0.036698452375741396,
)


def gelu_pair(u):
    size = jnp.abs(u)
    bell = jnp.exp(-0.5 * u * u)
    t = 1.0 / (1.0 + TAIL * size)
    poly = jnp.full_like(t, TAIL_FIT[-1])
    for c in TAIL_FIT[-2::-1]:
        poly = poly * t + c
    upper = poly * t * bell
    cdf = jnp.where(u > 0.0, 1.0 - upper, upper)
    return u * cdf, cdf + (0.3989422804014327 * u) * bell


def block_rows(ref, start, half):
    return ref[pl.ds(pl.multiple_of(start, 16), half), :]


def project_kernel(heads, rows_dev, gains_at, row_ref, wire_ref, tok_ref, seg_ref, pad_ref, gain_ref,
                   norm_ref, qe_ref, ke_ref, ve_ref, vt_ref, mix_ref, wide_ref):
    width = tok_ref.shape[1]
    half = HD // 2
    cols = 3 * heads

    @pl.when(pl.program_id(0) == 0)
    def _():
        zero = jnp.zeros((half, HD), BF)

        def fill(r, _):
            low = pl.multiple_of(r * HD, HD)
            for c in range(cols):
                t = block_rows(wire_ref, row_ref[r * cols + c], half)
                for part in range(2):
                    piece = t[:, part * HD : (part + 1) * HD]
                    at = pl.ds(low + part * half, half)
                    wide_ref[at, c * LANES : (c + 1) * LANES] = jnp.concatenate([piece, zero], axis=1)
                    mix_ref[at, c * HD : (c + 1) * HD] = piece
            return 0

        lax.fori_loop(0, width // HD, fill, 0)

    xhat, _ = normalize(tok_ref[...].astype(F32))
    normed = (xhat * gain_ref[...]).astype(BF)
    norm_ref[...] = normed
    count = tok_ref.shape[0]
    lane = lax.broadcasted_iota(jnp.int32, (LANES, count), 0)
    seg = seg_ref[...]
    same = lane - HD == seg
    in_segs = (lane >= HD) & (lane < HD + SEGS)
    ones = (lane >= HD + SEGS) & (lane < HD + SEGS + 3)
    ext_q = jnp.where(same, 1.0, 0.0).T
    ext_k = jnp.where(in_segs, jnp.where(same & (pad_ref[...] > 0.5), 0.0, NEG), jnp.where(ones, 1.0, 0.0)).T
    ext_v = jnp.where((lane >= HD) & (lane < HD + 3), 1.0, 0.0).T
    for h in range(heads):
        for ref, part, scale, ext in ((qe_ref, 0, HD ** -0.5, ext_q), (ke_ref, 1, 1.0, ext_k), (ve_ref, 2, 1.0, ext_v)):
            c = part * heads + h
            mixed = nn(normed, wide_ref[:, c * LANES : (c + 1) * LANES]).astype(BF)
            out = (mixed.astype(F32) * scale + ext).astype(BF)
            ref[h] = out
            if part == 2:
                vt_ref[h] = out.T[:VT]


def project(wire, row_own, tokens, seg, pad, gain_one, heads):
    rows, width = tokens.shape
    tb = min(512, rows)
    full = lambda i, r: (0, 0)
    blk = lambda i, r: (i, 0)
    col = lambda i, r: (0, i)
    ext = lambda i, r: (0, i, 0)
    out = lambda *s: jax.ShapeDtypeStruct(s, BF)
    return pl.pallas_call(
        functools.partial(project_kernel, heads, 0, 0),
        grid_spec=pltpu.PrefetchScalarGridSpec(
            num_scalar_prefetch=1,
            grid=(rows // tb,),
            in_specs=[
                pl.BlockSpec(wire.shape, full),
                pl.BlockSpec((tb, width), blk),
                pl.BlockSpec((1, tb), col),
                pl.BlockSpec((1, tb), col),
                pl.BlockSpec((1, width), full),
            ],
            out_specs=[
                pl.BlockSpec((tb, width), blk),
                pl.BlockSpec((heads, tb, LANES), ext),
                pl.BlockSpec((heads, tb, LANES), ext),
                pl.BlockSpec((heads, tb, LANES), ext),
                pl.BlockSpec((heads, VT, tb), lambda i, r: (0, 0, i)),
                pl.BlockSpec((width, 3 * heads * HD), full),
            ],
            scratch_shapes=[pltpu.VMEM((width, 3 * heads * LANES), BF)],
        ),
        out_shape=[
            out(rows, width),
            out(heads, rows, LANES),
            out(heads, rows, LANES),
            out(heads, rows, LANES),
            out(heads, VT, rows),
            out(width, 3 * heads * HD),
        ],
        compiler_params=pltpu.CompilerParams(vmem_limit_bytes=48 << 20),
        name="project",
    )(row_own, wire, tokens, seg, pad, gain_one)


def middle_kernel(shards, span, units, rows_dev, wide, gain_row, gains_dev,
                  here_ref, row_ref, wire_ref, att_ref, tok_ref, cot_ref, pad_ref, gain_ref,
                  out_ref, res_ref, back_ref, grads_ref, mix_ref,
                  wo_ref, wu_ref, wd_ref, go_ref, gu_ref, gd_ref, gg_ref):
    width = tok_ref.shape[1]
    half = HD // 2
    kinds = (
        (mix_ref, None, width, 3 * span),
        (wo_ref, go_ref, span, width),
        (wu_ref, gu_ref, width, units),
        (wd_ref, gd_ref, units, width),
    )

    @pl.when(pl.program_id(0) == 0)
    def _():
        base = 0
        for ref, acc, rows, cols in kinds:
            grid_cols = cols // HD

            def fill(r, _, ref=ref, base=base, grid_cols=grid_cols):
                low = pl.multiple_of(r * HD, HD)
                for n in range(shards):
                    for c in range(grid_cols):
                        t = block_rows(wire_ref, row_ref[base + r * grid_cols + c] + n * rows_dev, half)
                        for part in range(2):
                            ref[n, pl.ds(low + part * half, half), c * HD : (c + 1) * HD] = t[:, part * HD : (part + 1) * HD]
                return 0

            lax.fori_loop(0, rows // HD, fill, 0)
            base += rows // HD * grid_cols
            if acc is not None:
                acc[...] = jnp.zeros_like(acc)
        gg_ref[...] = jnp.zeros_like(gg_ref)

    tokens = tok_ref[...].astype(F32)
    cot = cot_ref[...]
    branch = nn(att_ref[0], wo_ref[0])
    for n in range(1, shards):
        branch += nn(att_ref[n], wo_ref[n])
    residual = tokens + branch
    xhat, scale = normalize(residual)
    gain = gain_ref[...]
    normed = (xhat * gain).astype(BF)
    mlp = jnp.zeros_like(residual)
    back = jnp.zeros_like(residual)
    for n in range(shards):
        value, slope = gelu_pair(nn(normed, wu_ref[n]))
        active = value.astype(BF)
        mlp += nn(active, wd_ref[n])
        gd_ref[n] += tn(active, cot)
        back_up = (slope * nt(cot, wd_ref[n])).astype(BF)
        gu_ref[n] += tn(normed, back_up)
        back += nt(back_up, wu_ref[n])
    out_ref[...] = (residual + mlp).astype(BF)
    gg_ref[...] += jnp.sum(back * xhat, axis=0, keepdims=True)
    back_res = cot.astype(F32) + norm_back(back * gain, xhat, scale)
    res_ref[...] = back_res
    branch_low = back_res.astype(BF)
    pad = jnp.broadcast_to(pad_ref[...], (8, pad_ref.shape[1])).T[:, :1]
    for n in range(shards):
        go_ref[n] += tn(att_ref[n], branch_low)
        back_ref[n] = (nt(branch_low, wo_ref[n]) * pad).astype(BF)

    @pl.when(pl.program_id(0) == pl.num_programs(0) - 1)
    def _():
        grads_ref[...] = jnp.zeros_like(grads_ref)
        base = 0
        for ref, acc, rows, cols in kinds:
            grid_cols = cols // HD
            if acc is not None:

                def scatter(r, _, acc=acc, base=base, grid_cols=grid_cols):
                    low = pl.multiple_of(r * HD, HD)
                    for n in range(shards):
                        for c in range(grid_cols):
                            at = row_ref[base + r * grid_cols + c] + n * rows_dev
                            cut = slice(c * HD, (c + 1) * HD)
                            value = jnp.concatenate([acc[n, pl.ds(low, half), cut], acc[n, pl.ds(low + half, half), cut]], axis=1)
                            grads_ref[pl.ds(pl.multiple_of(at, 16), half), :] = value.astype(BF)
                    return 0

                lax.fori_loop(0, rows // HD, scatter, 0)
            base += rows // HD * grid_cols
        for w in range(wide):
            piece = w * gains_dev // LANES - width // LANES
            if piece >= 0:
                for n in range(shards):
                    at = (w * shards + n) * rows_dev + gain_row
                    grads_ref[at : at + 1, :] = gg_ref[:, piece * LANES : (piece + 1) * LANES].astype(BF)


def middle(here, row_full, wire, att, tokens, cotangent, pad, gain_two, wide, rows_dev, gain_row, gains_dev):
    shards, own, span = att.shape
    width = tokens.shape[1]
    units = FF // shards
    tb = min(256, own)
    steps = own // tb
    full = lambda i, h, r: (0, 0)
    full3 = lambda i, h, r: (0, 0, 0)
    mine = lambda i, h, r: (h[0] * steps + i, 0)
    blk = lambda i, h, r: (i, 0)
    blk3 = lambda i, h, r: (0, i, 0)
    once = pl.Buffered(1)
    return pl.pallas_call(
        functools.partial(middle_kernel, shards, span, units, rows_dev, wide, gain_row, gains_dev),
        grid_spec=pltpu.PrefetchScalarGridSpec(
            num_scalar_prefetch=2,
            grid=(steps,),
            in_specs=[
                pl.BlockSpec(wire.shape, full, pipeline_mode=once),
                pl.BlockSpec((shards, tb, span), blk3),
                pl.BlockSpec((tb, width), mine),
                pl.BlockSpec((tb, width), mine),
                pl.BlockSpec((1, tb), lambda i, h, r: (0, h[0] * steps + i)),
                pl.BlockSpec((1, width), full),
            ],
            out_specs=[
                pl.BlockSpec((tb, width), blk),
                pl.BlockSpec((tb, width), blk),
                pl.BlockSpec((shards, tb, span), blk3),
                pl.BlockSpec(wire.shape, full, pipeline_mode=once),
                pl.BlockSpec((shards, width, 3 * span), full3, pipeline_mode=once),
            ],
            scratch_shapes=[
                pltpu.VMEM((shards, span, width), BF),
                pltpu.VMEM((shards, width, units), BF),
                pltpu.VMEM((shards, units, width), BF),
                pltpu.VMEM((shards, span, width), F32),
                pltpu.VMEM((shards, width, units), F32),
                pltpu.VMEM((shards, units, width), F32),
                pltpu.VMEM((1, width), F32),
            ],
        ),
        out_shape=[
            jax.ShapeDtypeStruct((own, width), BF),
            jax.ShapeDtypeStruct((own, width), F32),
            jax.ShapeDtypeStruct((shards, own, span), BF),
            jax.ShapeDtypeStruct(wire.shape, BF),
            jax.ShapeDtypeStruct((shards, width, 3 * span), BF),
        ],
        compiler_params=pltpu.CompilerParams(vmem_limit_bytes=56 << 20),
        name="middle",
    )(here, row_full, wire, att, tokens, cotangent, pad, gain_two)


def mixgrad_kernel(heads, rows_dev, wide, gain_row, gains_dev, row_ref, norm_ref, dq_ref, dk_ref, dv_ref, mix_ref, gain_ref, grads_ref, acc_ref):
    width = norm_ref.shape[1]
    span = heads * HD
    half = HD // 2
    cols = 3 * heads

    @pl.when(pl.program_id(0) == 0)
    def _():
        acc_ref[...] = jnp.zeros_like(acc_ref)

    normed = norm_ref[...]
    for part, ref in enumerate((dq_ref, dk_ref, dv_ref)):
        acc_ref[:, part * span : (part + 1) * span] += tn(normed, ref[...])

    @pl.when(pl.program_id(0) == pl.num_programs(0) - 1)
    def _():
        grads_ref[...] = jnp.zeros_like(grads_ref)

        def scatter(r, _):
            low = pl.multiple_of(r * HD, HD)
            for c in range(cols):
                cut = slice(c * HD, (c + 1) * HD)
                value = jnp.concatenate([acc_ref[pl.ds(low, half), cut], acc_ref[pl.ds(low + half, half), cut]], axis=1)
                grads_ref[pl.ds(pl.multiple_of(row_ref[r * cols + c], 16), half), :] = value.astype(BF)
            return 0

        lax.fori_loop(0, width // HD, scatter, 0)
        along = jnp.sum(acc_ref[...] * mix_ref[...].astype(F32), axis=1, keepdims=True)
        line = jnp.broadcast_to(along, (width, LANES)).T[:1] / gain_ref[...]
        for w in range(wide):
            piece = w * gains_dev // LANES
            if piece < width // LANES:
                at = w * rows_dev + gain_row
                grads_ref[at : at + 1, :] = line[:, piece * LANES : (piece + 1) * LANES].astype(BF)


def mixgrad(row_own, normed, dq, dk, dv, mix, gain_one, wire_shape, wide, rows_dev, gain_row, gains_dev):
    rows, width = normed.shape
    span = dq.shape[1]
    tb = min(512, rows)
    full = lambda i, r: (0, 0)
    blk = lambda i, r: (i, 0)
    return pl.pallas_call(
        functools.partial(mixgrad_kernel, span // HD, rows_dev, wide, gain_row, gains_dev),
        grid_spec=pltpu.PrefetchScalarGridSpec(
            num_scalar_prefetch=1,
            grid=(rows // tb,),
            in_specs=[
                pl.BlockSpec((tb, width), blk),
                pl.BlockSpec((tb, span), blk),
                pl.BlockSpec((tb, span), blk),
                pl.BlockSpec((tb, span), blk),
                pl.BlockSpec((width, 3 * span), full),
                pl.BlockSpec((1, width), full),
            ],
            out_specs=pl.BlockSpec(wire_shape, full),
            scratch_shapes=[pltpu.VMEM((width, 3 * span), F32)],
        ),
        out_shape=jax.ShapeDtypeStruct(wire_shape, BF),
        compiler_params=pltpu.CompilerParams(vmem_limit_bytes=48 << 20),
        name="mixgrad",
    )(row_own, normed, dq, dk, dv, mix, gain_one)


def tail_kernel(shards, here_ref, bm_ref, mix_ref, tok_ref, res_ref, gain_ref, out_ref):
    back = nt(bm_ref[0], mix_ref[0])
    for n in range(1, shards):
        back += nt(bm_ref[n], mix_ref[n])
    xhat, scale = normalize(tok_ref[...].astype(F32))
    out_ref[...] = (res_ref[...] + norm_back(back * gain_ref[...], xhat, scale)).astype(BF)


def tail(here, bm, mix, tokens, res, gain_one):
    shards, own, cols = bm.shape
    width = tokens.shape[1]
    tb = min(256, own)
    steps = own // tb
    full3 = lambda i, h: (0, 0, 0)
    return pl.pallas_call(
        functools.partial(tail_kernel, shards),
        grid_spec=pltpu.PrefetchScalarGridSpec(
            num_scalar_prefetch=1,
            grid=(steps,),
            in_specs=[
                pl.BlockSpec((shards, tb, cols), lambda i, h: (0, i, 0)),
                pl.BlockSpec(mix.shape, full3),
                pl.BlockSpec((tb, width), lambda i, h: (h[0] * steps + i, 0)),
                pl.BlockSpec((tb, width), lambda i, h: (i, 0)),
                pl.BlockSpec((1, width), lambda i, h: (0, 0)),
            ],
            out_specs=pl.BlockSpec((tb, width), lambda i, h: (i, 0)),
        ),
        out_shape=jax.ShapeDtypeStruct((own, width), BF),
        compiler_params=pltpu.CompilerParams(vmem_limit_bytes=48 << 20),
        name="tail",
    )(here, bm, mix, tokens, res, gain_one)


def adam_gains(grad, gain, first, second, average):
    new_first = beta_one * first + (1.0 - beta_one) * grad
    new_second = beta_two * second + (1.0 - beta_two) * grad * grad
    new_gain = gain - gain_rate * new_first / (jnp.sqrt(new_second) + step_eps)
    new_average = average_keep * average + (1.0 - average_keep) * new_gain
    return (new_gain, new_first, new_second, new_average)


def to_shards(values, shards):
    rows, cols = values.shape
    return lax.all_to_all(values.reshape(shards, rows // shards, cols), "narrow", 0, 0)


def body(
    tokens,
    cotangent,
    segment_ids,
    pad_mask,
    owner_order,
    weights,
    first_moment,
    second_moment,
    average,
    stats,
    bases,
    gains,
    gain_first,
    gain_second,
    gain_average,
):
    narrow = lax.axis_size("narrow")
    wide = lax.axis_size("wide")
    here = lax.axis_index("narrow")
    heads = HEADS // narrow
    rows, width = tokens.shape
    span = heads * HD
    own = rows // narrow
    slots, size = weights.shape[1], weights.shape[2]
    half = size // 2
    block_count = owner_order.shape[0]
    gains_dev = gains.shape[0]
    gain_row = slots * half
    rows_dev = gain_row + 16

    low = weights[0].astype(BF)
    wire = jnp.concatenate([low[:, :half], low[:, half:]], axis=2).reshape(gain_row, 2 * size)
    wire = jnp.concatenate([wire, jnp.pad(gains.astype(BF)[None], ((0, 15), (0, LANES - gains_dev)))], axis=0)
    wire_own = lax.all_gather(wire, "wide", axis=0, tiled=True)
    wire_full = lax.all_gather(lax.all_gather(wire, "narrow", axis=0, tiled=True), "wide", axis=0, tiled=True)

    ids = jnp.arange(block_count, dtype=jnp.int32)
    slot_of = jnp.sum(jnp.where(owner_order[None, :] == ids[:, None], ids[None, :], 0), axis=1)
    device, place = slot_of // slots, slot_of % slots
    row_own = device * rows_dev + place * half
    row_full = device * (narrow * rows_dev) + place * half
    here_of = jnp.full((1,), here, jnp.int32)

    gain_all = wire_own.reshape(wide, rows_dev, LANES)[:, gain_row, :gains_dev].astype(F32).reshape(1, 2 * width)
    gain_one, gain_two = gain_all[:, :width], gain_all[:, width:]
    seg = segment_ids
    seg_row = segment_ids[0]
    pad = pad_mask.astype(F32)
    block = min(512, rows)
    low_seg = seg_row[::block]
    high_seg = seg_row[block - 1 :: block]
    begin = jnp.sum((seg_row[None, :] < low_seg[:, None]).astype(jnp.int32), axis=1) // block
    end = (jnp.sum((seg_row[None, :] <= high_seg[:, None]).astype(jnp.int32), axis=1) + block - 1) // block

    normed, qe, ke, ve, vt, mix = project(wire_own, row_own, tokens, seg, pad, gain_one, heads)
    attended, qb = attend(qe, ke, vt, pad, begin, end, block, block)
    att_own = to_shards(attended, narrow)
    out_own, back_res, back_own, grads, mix_full = middle(
        here_of, row_full, wire_full, att_own, tokens, cotangent, pad, gain_two, wide, rows_dev, gain_row, gains_dev
    )
    output = lax.all_gather(out_own, "narrow", axis=0, tiled=True)
    back_att = lax.all_to_all(back_own, "narrow", 0, 0).reshape(rows, span)
    dq, dk, dv = attend_back(qb, ke, ve, back_att, attended, begin, end, block, block)
    grads_mix = mixgrad(row_own, normed, dq, dk, dv, mix, gain_one, wire_own.shape, wide, rows_dev, gain_row, gains_dev)
    bm = to_shards(jnp.concatenate([dq, dk, dv], axis=1), narrow)
    grad_own = tail(here_of, bm, mix_full, tokens, back_res, gain_one)
    input_grad = lax.all_gather(grad_own, "narrow", axis=0, tiled=True).astype(F32)

    part_a = lax.psum_scatter(grads, "wide", scatter_dimension=0, tiled=True)
    part_a = lax.psum_scatter(part_a, "narrow", scatter_dimension=0, tiled=True)
    part_b = lax.psum_scatter(grads_mix, "wide", scatter_dimension=0, tiled=True)
    group = 8 if slots % 8 == 0 else 1
    new_weight, new_first, new_second, new_average, new_stats, new_bases = soap(
        part_a, part_b, weights, first_moment, second_moment, average, stats, bases, group
    )
    line = part_a[gain_row].astype(F32) + lax.psum(part_b[gain_row].astype(F32), "narrow")
    offset = lax.axis_index("wide") * gains_dev % LANES
    own_gain = lax.dynamic_slice_in_dim(line, offset, gains_dev, 0)
    new_gains, gain_moment, gain_square, gain_mean = adam_gains(own_gain, gains, gain_first, gain_second, gain_average)
    return (
        output,
        input_grad,
        new_weight,
        new_first,
        new_second,
        new_average,
        new_stats,
        new_bases,
        new_gains,
        gain_moment,
        gain_square,
        gain_mean,
    )


def solution(mesh):
    block = P("narrow", "wide", None, None)
    pair = P("narrow", "wide", None, None, None)
    rows = P("wide", None)
    line = P("wide")
    return jax.shard_map(
        body,
        mesh=mesh,
        in_specs=(rows, rows, rows, rows, P(), block, block, block, block, pair, pair, line, line, line, line),
        out_specs=(rows, rows, block, block, block, block, pair, pair, line, line, line, line),
        check_vma=False,
    )
```

time: 1690 us -> 542 us (0.32)
  other arithmetic: 782 us -> 13.9 us
  matrix products: 401 us -> 0 us
  Pallas kernels: 0 us -> 277 us
  waiting for transfers between devices: 311 us -> 157 us
  local copies, waits for them, and re-layouts: 137 us -> 17.9 us
  blocking collectives: 23 us -> 50.7 us
    another operation x14 -> x0, other arithmetic: 529 us -> none  [the longest x5 287 us: orthonormal(): lower = jnp.linalg.cholesky(gram)]
    dot_general x80 -> x0, matrix products: 396 us -> none  [the longest x8 102 us: attend_backward(): jnp.einsum('qhd,khd->hqk', back_block, value_rows, preferred_element_type...]
    pallas_call x0 -> x7, Pallas kernels: none -> 277 us  [the longest x1 79.7 us: soap(): pl.pallas_call(functools.partial(soap_kernel, group), grid=(slots // grou...]
    psum x3 -> x0, waiting for transfers between devices: 276 us -> none  [the longest x1 149 us: body(): lax.psum(branch_part.astype(jnp.bfloat16), 'narrow').astype(jnp.float32)]
    convert_element_type x16 -> x5, other arithmetic: 108 us -> 8.82 us  [the longest x1 6.94 us: body(): lax.all_gather(grad_own, 'narrow', axis=0, tiled=True).astype(F32)]
    reduce_sum x16 -> x2, other arithmetic: 73.7 us -> 0.36 us  [the longest x1 0.24 us: body(): jnp.sum((seg_row[None, :] <= high_seg[:, None]).astype(jnp.int32), axis=1)]
    all_to_all x0 -> x2, waiting for transfers between devices: none -> 56 us  [to_shards(): lax.all_to_all(values.reshape(shards, rows // shards, cols), 'narrow', 0, 0)]
    while x33 -> x0, local copies, waits for them, and re-layouts: 49.3 us -> none
  transfers between devices with their start and end apart: 5 -> 9, of which waited for: 4 -> 5; matrix products, arithmetic and copies ran while one was open for 38% -> 1% of each run, Pallas kernels for 0% -> 43%
where the time goes in v1:
time: 542 us; the launch traced here: 540 us
  Pallas kernels  277 us (51%)
  waiting for transfers between devices  157 us (29%)
  blocking collectives  50.7 us (9%)
  local copies, waits for them, and re-layouts  17.9 us (3%)
  between operations  14.3 us (3%)
  other arithmetic  13.9 us (3%)
  starting transfers between devices  9.71 us (2%)
    pallas_call x1, Pallas kernels, soap(): pl.pallas_call(functools.partial(soap_kernel, group), grid=(slots // grou...  79.7 us
    pallas_call x1, Pallas kernels, attend_back(): pl.pallas_call(functools.partial(bwd_kernel, heads, bq, bk), grid_spec=pl...  71.6 us
    all_to_all x2, waiting for transfers between devices, to_shards(): lax.all_to_all(values.reshape(shards, rows // shards, cols), 'narrow', 0, 0)  56 us
    all_gather x1, waiting for transfers between devices, body(): output = lax.all_gather(out_own, 'narrow', axis=0, tiled=True)  51.9 us
    pallas_call x1, Pallas kernels, attend(): pl.pallas_call(functools.partial(fwd_kernel, heads, bq, bk), grid_spec=pl...  49 us
    pallas_call x1, Pallas kernels, middle(): pl.pallas_call(functools.partial(middle_kernel, shards, span, units, rows...  46.1 us
    reduce_scatter x1, waiting for transfers between devices, body(): part_a = lax.psum_scatter(part_a, 'narrow', scatter_dimension=0, tiled=True)  41.6 us
    all_gather x1, blocking collectives, body(): lax.all_gather(wire, 'narrow', axis=0, tiled=True)  21.9 us
  transfers between devices with their start and end apart: 9, of which 5 were waited for; matrix products, arithmetic and copies ran while one was open for 1% of the time, Pallas kernels for 43%

profile of v1, /device:TPU:0, one launch (start us, length us, event | category | flops | bytes accessed | tf_op | source)
XLA Modules:
  0.0 540.4 jit_solution(15622906098204861849)
XLA Ops:
  10.1 21.9 %all_gather.15 = bf16[3136,128]{1,0:T(8,128)(2,1)} all-gather(bf16[784,128]{1,0:T(8,128)(2,1)} %fusion.1), channel_id=1, replica_groups=mesh['wide'=8,'narrow'=4] {'narrow'}, dimensions={0}, use_global_device_ids=true | all-gather | bytes 1003520 | tf_op jit(solution)/shard_map/all_gather | solution.py:723
  32.7 6.4 %all-gather.7.cloned.1.call-done.wire_ref = bf16[6272,128]{1,0:T(8,128)(2,1)} async-done(((bf16[784,128]{1,0:T(8,128)(2,1)}), bf16[6272,128]{1,0:T(8,128)(2,1)}) %all-gather.7.cloned.1.call-update) | async-done | bytes 1605648 | tf_op jit(solution)/shard_map/all_gather | solution.py:722
  40.4 1.4 copy-done.4
  41.8 14.2 %project.1 = (bf16[4096,512]{1,0:T(8,128)(2,1)}, bf16[2,4096,128]{2,1,0:T(8,128)(2,1)S(1)}, bf16[2,4096,128]{2,1,0:T(8,128)(2,1)}, bf16[2,4096,128]{2,1,0:T(8,12...) custom-call(s32[192]{0:T(256)S(1)} %get-tuple-element.62.row_ref, ...), custom_call_target="tpu_custom_call" | custom-call | tf_op jit(solution)/shard_map/project/pallas_call | solution.py:397
  57.4 49.0 %attend.1 = (bf16[4096,128]{1,0:T(8,128)(2,1)}, bf16[2,4096,128]{2,1,0:T(8,128)(2,1)S(1)}) custom-call(s32[8]{0:T(128)S(1)} %get-tuple-element.69.lo_ref, s32[8]{0:T(128)S(1)} %get-tuple-element.68.hi_ref, bf16[2,4096,128]{2,1,0:T(8,128)(2,1)} %copy-done.3, bf16[2,4096,128]{2,1,0:T(8,128)(2,1)} %get-tuple-element.35.ke_ref, ...), custom_call_target="tpu_custom_call" | custom-call | tf_op jit(solution)/shard_map/attend/pallas_call | solution.py:105
  106.3 1.4 copy-done.2
  107.7 4.6 all-to-all-start
  112.9 15.3 %all-to-all-done.att_ref = bf16[4,1024,128]{2,1,0:T(8,128)(2,1)S(1)} async-done(((bf16[4,1024,128]{2,1,0:T(8,128)(2,1)}), bf16[4,1024,128]{2,1,0:T(8,128)(2,1)S(1)}, u32[]{:S(2)}, u32[]{:S(2)}) %all-to-all-start) | async-done | bytes 1048608 | tf_op jit(solution)/shard_map/all_to_all | solution.py:685
  129.2 46.1 %middle.1 = (bf16[1024,512]{1,0:T(8,128)(2,1)}, f32[1024,512]{1,0:T(8,128)}, bf16[4,1024,128]{2,1,0:T(8,128)(2,1)}, bf16[25088,128]{1,0:T(8,128)(2,1)}, bf16[4,512,384]{2,1,0:T(8,128)(2,1)}) custom-call(s32[1]{0:T(128)} %bitcast.here_ref, s32[192]{0:T(256)} %multiply_add_fusion.1.row_ref, bf16[25088,128]{1,0:T(8,128)(2,1)} %all-gather.5.cloned.1.call-done.wire_ref, ...), custom_call_target="tpu_custom_call" | custom-call | tf_op jit(solution)/shard_map/middle/pallas_call | solution.py:535
  176.5 18.4 %all_to_all.15 = bf16[4,1024,128]{2,1,0:T(8,128)(2,1)S(1)} all-to-all(bf16[4,1024,128]{2,1,0:T(8,128)(2,1)S(1)} %copy-done.16), channel_id=1, replica_groups=mesh['wide'=8,'narrow'=4] {'narrow'}, dimensions={0} | all-to-all | bytes 2097152 | tf_op jit(solution)/shard_map/all_to_all | solution.py:750
  194.9 71.6 %attend_back.1 = (bf16[4096,128]{1,0:T(8,128)(2,1)S(1)}, bf16[4096,128]{1,0:T(8,128)(2,1)S(1)}, bf16[4096,128]{1,0:T(8,128)(2,1)S(1)}) custom-call(s32[8]{0:T(128)S(1)} %get-tuple-element.69.lo_ref, s32[8]{0:T(128)S(1)} %get-tuple-element.68.hi_ref, bf16[2,4096,128]{2,1,0:T(8,128)(2,1)} %copy-done.2, bf16[2,4096,128]{2,1,0:T(8,128)(2,1)} %get-tuple-element.35.ke_ref, ...), custom_call_target="tpu_custom_call" | custom-call | tf_op jit(solution)/shard_map/attend_back/pallas_call | solution.py:197
  266.5 10.3 %mixgrad.1 = bf16[6272,128]{1,0:T(8,128)(2,1)} custom-call(s32[192]{0:T(256)S(1)} %get-tuple-element.62.row_ref, bf16[4096,512]{1,0:T(8,128)(2,1)} %get-tuple-element.48.norm_ref, bf16[4096,128]{1,0:T(8,128)(2,1)S(1)} %get-tuple-element.42.dq_ref, bf16[4096,128]{1,0:T(8,128)(2,1)S(1)} %get-tuple-element.43.dk_ref, ...), custom_call_target="tpu_custom_call" | custom-call | tf_op jit(solution)/shard_map/mixgrad/pallas_call | solution.py:619
  277.4 2.1 pad_maximum_fusion
  279.5 4.8 all-to-all-start.2
  285.0 40.7 %all-to-all-done.2.bm_ref = bf16[4,1024,384]{2,1,0:T(8,128)(2,1)} async-done(((bf16[4,1024,384]{2,1,0:T(8,128)(2,1)}), bf16[4,1024,384]{2,1,0:T(8,128)(2,1)}, u32[]{:S(2)}, u32[]{:S(2)}) %all-to-all-start.2) | async-done | bytes 3145760 | tf_op jit(solution)/shard_map/all_to_all | solution.py:685
  325.7 1.4 copy-done.5
  327.1 6.0 %tail.1 = bf16[1024,512]{1,0:T(8,128)(2,1)} custom-call(s32[1]{0:T(128)} %bitcast.here_ref, bf16[4,1024,384]{2,1,0:T(8,128)(2,1)} %all-to-all-done.2.bm_ref, bf16[4,512,384]{2,1,0:T(8,128)(2,1)S(1)} %copy-done.5, bf16[4096,512]{1,0:T(8,128)(2,1)} %tok_ref.5, f32[1024,512]{1,0:T(8,128)S(1)} %copy-done.1, f32[1,512]{1,0:T(1,128)S(1)} %get-tuple-element.67.gain_ref), custom_call_target="tpu_custom_call" | custom-call | tf_op jit(solution)/shard_map/tail/pallas_call | solution.py:655
  333.8 10.4 %psum.7 = f32[128]{0:T(128)S(1)} all-reduce(f32[128]{0:T(128)S(1)} %fusion.4), channel_id=1, replica_groups=mesh['wide'=8,'narrow'=4] {'narrow'}, use_global_device_ids=true, to_apply=%region_6.7 | all-reduce | flops 128 | bytes 1024 | tf_op jit(solution)/shard_map/psum | solution.py:764
  344.2 51.9 %all-gather.9.cloned.1.call-done = bf16[4096,512]{1,0:T(8,128)(2,1)} async-done(((bf16[1024,512]{1,0:T(8,128)(2,1)}), bf16[4096,512]{1,0:T(8,128)(2,1)}) %all-gather.9.cloned.1.call-update) | async-done | bytes 4194320 | tf_op jit(solution)/shard_map/all_gather | solution.py:749
  396.1 41.6 %reduce-scatter.6.cloned.1.call-done.ga_ref = bf16[784,128]{1,0:T(8,128)(2,1)} async-done(((bf16[3136,128]{1,0:T(8,128)(2,1)}), bf16[784,128]{1,0:T(8,128)(2,1)}) %reduce-scatter.6.cloned.1.call-update) | async-done | bytes 200720 | tf_op jit(solution)/shard_map/reduce_scatter | solution.py:758
  437.7 1.4 copy-done.6
  444.3 79.7 %soap.1 = (f32[1,24,64,64]{3,2,1,0:T(8,128)}, f32[1,24,64,64]{3,2,1,0:T(8,128)}, f32[1,24,64,64]{3,2,1,0:T(8,128)}, f32[1,24,64,64]{3,2,1,0:T(8,128)}, f32[1,24,...) custom-call(bf16[784,128]{1,0:T(8,128)(2,1)S(1)} %copy-done.11, bf16[784,128]{1,0:T(8,128)(2,1)S(1)} %copy-done.12, ...), custom_call_target="tpu_custom_call" | custom-call | tf_op jit(solution)/shard_map/soap/pallas_call | solution.py:290
  524.6 6.9 %convert_element_type.56 = f32[4096,512]{1,0:T(8,128)} convert(bf16[4096,512]{1,0:T(8,128)(2,1)} %all-gather.11.cloned.1.call-done) | non-fusion elementwise | flops 2097152 | bytes 12582912 | tf_op jit(solution)/shard_map/convert_element_type | solution.py:755
  531.6 2.0 copy.32
  (78 shorter events, 16.5 us)
Async XLA Ops:
  7.2 24.8 %copy-start.13 = (s32[1,4096]{1,0:T(1,128)S(1)}, s32[1,4096]{1,0:T(1,128)}, u32[]{:S(2)}) copy-start(s32[1,4096]{1,0:T(1,128)} %seg_ref.1) | copy-start | bytes 49156
  7.2 25.0 %copy-start.17 = (s32[1,4096]{1,0:T(1,128)S(1)}, s32[1,4096]{1,0:T(1,128)}, u32[]{:S(2)}) copy-start(s32[1,4096]{1,0:T(1,128)} %param.18) | copy-start | bytes 49156
  7.2 25.3 %copy-start.18 = (s32[192]{0:T(256)S(1)}, s32[192]{0:T(256)}, u32[]{:S(2)}) copy-start(s32[192]{0:T(256)} %param.19) | copy-start | bytes 2308
  7.2 31.9 %all-gather.7.cloned.1.call-start = ((), (), s32[]{:S(2)}) async-start(), calls=%async_computation.7 | async-start | bytes 1806336 | tf_op jit(solution)/shard_map/all_gather | solution.py:722
  10.0 118.2 %all-gather.5.cloned.1.call-start = ((), (), s32[]{:S(2)}) async-start(), calls=%async_computation.6 | async-start | bytes 7225344 | tf_op jit(solution)/shard_map/all_gather | solution.py:723
  32.2 74.1 %copy-start.10 = (f32[1,4096]{1,0:T(1,128)}, f32[1,4096]{1,0:T(1,128)S(1)}, u32[]{:S(2)}) copy-start(f32[1,4096]{1,0:T(1,128)S(1)} %convert_element_type.53.pad_ref) | copy-start | bytes 49156
  40.4 1.4 copy-start.4
  106.3 1.4 copy-start.2
  107.7 20.5 %all-to-all-start = ((bf16[4,1024,128]{2,1,0:T(8,128)(2,1)}), bf16[4,1024,128]{2,1,0:T(8,128)(2,1)S(1)}, u32[]{:S(2)}, u32[]{:S(2)}) async-start(bf16[4,1024,128]{2,1,0:T(8,128)(2,1)} %bitcast.7), calls=%async_computation | async-start | bytes 2097152 | tf_op jit(solution)/shard_map/all_to_all | solution.py:685
  112.3 172.1 %reduce-scatter.4.cloned.1.call-start = ((), (), s32[]{:S(2)}) async-start(), calls=%async_computation.10 | async-start | bytes 7225344 | tf_op jit(solution)/shard_map/reduce_scatter | solution.py:757
  175.3 157.8 %reduce-scatter.8.cloned.1.call-start = ((), (), s32[]{:S(2)}) async-start(), calls=%async_computation.12 | async-start | bytes 1806336 | tf_op jit(solution)/shard_map/reduce_scatter | solution.py:759
  276.8 119.2 %all-gather.9.cloned.1.call-start = ((), (), s32[]{:S(2)}) async-start(), calls=%async_computation.8 | async-start | bytes 5242880 | tf_op jit(solution)/shard_map/all_gather | solution.py:749
  279.5 46.1 %copy-start.1 = (f32[1024,512]{1,0:T(8,128)S(1)}, f32[1024,512]{1,0:T(8,128)}, u32[]{:S(2)}) copy-start(f32[1024,512]{1,0:T(8,128)} %get-tuple-element.46.res_ref) | copy-start | bytes 6291460
  279.5 46.1 %all-to-all-start.2 = ((bf16[4,1024,384]{2,1,0:T(8,128)(2,1)}), bf16[4,1024,384]{2,1,0:T(8,128)(2,1)}, u32[]{:S(2)}, u32[]{:S(2)}) async-start(bf16[4,1024,384]{2,1,0:T(8,128)(2,1)} %bitcast.35), calls=%async_computation.2 | async-start | bytes 6291456 | tf_op jit(solution)/shard_map/all_to_all | solution.py:685
  284.4 153.3 %reduce-scatter.6.cloned.1.call-start = ((), (), s32[]{:S(2)}) async-start(), calls=%async_computation.11 | async-start | bytes 1003520 | tf_op jit(solution)/shard_map/reduce_scatter | solution.py:758
  284.9 239.7 %all-gather.11.cloned.1.call-start = ((), (), s32[]{:S(2)}) async-start(), calls=%async_computation.9 | async-start | bytes 5242880 | tf_op jit(solution)/shard_map/all_gather | solution.py:755
  325.7 1.4 copy-start.5
  327.1 110.6 %copy-start = (f32[1,24,64,64]{3,2,1,0:T(8,128)S(1)}, f32[1,24,64,64]{3,2,1,0:T(8,128)}, u32[]{:S(2)}) copy-start(f32[1,24,64,64]{3,2,1,0:T(8,128)} %w_ref.1) | copy-start | bytes 1179652
  333.8 190.3 %copy-start.19 = (f32[128]{0:T(128)S(1)}, f32[128]{0:T(128)}, u32[]{:S(2)}) copy-start(f32[128]{0:T(128)} %param.26) | copy-start | bytes 1540
  333.8 190.3 %copy-start.20 = (f32[128]{0:T(128)S(1)}, f32[128]{0:T(128)}, u32[]{:S(2)}) copy-start(f32[128]{0:T(128)} %param.29) | copy-start | bytes 1540
  333.8 190.3 %copy-start.21 = (f32[128]{0:T(128)S(1)}, f32[128]{0:T(128)}, u32[]{:S(2)}) copy-start(f32[128]{0:T(128)} %param.27) | copy-start | bytes 1540
  437.7 1.4 copy-start.6
  444.3 79.7 %copy-start.22 = (f32[128]{0:T(128)S(1)}, f32[128]{0:T(128)}, u32[]{:S(2)}) copy-start(f32[128]{0:T(128)} %param.28) | copy-start | bytes 1540
  524.6 6.9 %copy-start.15 = (bf16[4096,512]{1,0:T(8,128)(2,1)S(1)}, bf16[4096,512]{1,0:T(8,128)(2,1)}, u32[]{:S(2)}) copy-start(bf16[4096,512]{1,0:T(8,128)(2,1)} %all-gather.9.cloned.1.call-done) | copy-start | bytes 12582916
  (8 other events, 8.8 us)
Sparse Core Ops, SparseCore 0:
  10.5 28.5 all-gather.6
  40.9 46.1 all-gather.4
  175.4 60.5 reduce-scatter.3
  277.0 36.6 reduce-scatter.7
  315.2 80.8 all-gather.8
  398.4 39.2 reduce-scatter.5
  439.9 80.1 all-gather.10

commit v2 on v1

--- a/solution.py
+++ b/solution.py
@@ -126,12 +126,12 @@
             jax.ShapeDtypeStruct((rows, heads * HD), BF),
             jax.ShapeDtypeStruct((heads, rows, LANES), BF),
         ],
-        compiler_params=pltpu.CompilerParams(vmem_limit_bytes=48 << 20),
+        compiler_params=pltpu.CompilerParams(vmem_limit_bytes=60 << 20),
         name="attend",
     )(lo, hi, qe, ke, vt, padw)
 
 
-def bwd_kernel(heads, bq, bk, lo_ref, hi_ref, qb_ref, ke_ref, ve_ref, go_ref, att_ref, dq_ref, dk_ref, dv_ref, ge_ref, dqt_ref, kt_ref, qt_ref, got_ref, dkt_ref, dvt_ref):
+def bwd_kernel(heads, bq, bk, lo_ref, hi_ref, qb_ref, ke_ref, ve_ref, go_ref, att_ref, out_ref, ge_ref, dqt_ref, kt_ref, qt_ref, got_ref, dkt_ref, dvt_ref):
     j = pl.program_id(0)
     rows = qb_ref.shape[1]
 
@@ -176,15 +176,16 @@
         dvt_ref[h] = zero
     lax.fori_loop(lo_ref[j], hi_ref[j], step, 0)
     for h in range(heads):
-        dk_ref[:, h * HD : (h + 1) * HD] = dkt_ref[h].T.astype(BF)
-        dv_ref[:, h * HD : (h + 1) * HD] = dvt_ref[h].T.astype(BF)
+        for part, ref in ((1, dkt_ref), (2, dvt_ref)):
+            at = (part * heads + h) * HD
+            out_ref[pl.ds(pl.multiple_of(j * bk, bk), bk), at : at + HD] = ref[h].T.astype(BF)
 
     @pl.when(j == pl.num_programs(0) - 1)
     def _():
         for h in range(heads):
             for c in range(rows // 512):
                 sl = pl.ds(c * 512, 512)
-                dq_ref[sl, h * HD : (h + 1) * HD] = (dqt_ref[h, :, c * 512 : (c + 1) * 512].T * (HD ** -0.5)).astype(BF)
+                out_ref[sl, h * HD : (h + 1) * HD] = (dqt_ref[h, :, c * 512 : (c + 1) * 512].T * (HD ** -0.5)).astype(BF)
 
 
 def attend_back(qb, ke, ve, go, att, lo, hi, bq, bk):
@@ -192,7 +193,6 @@
     full3 = lambda i, lo, hi: (0, 0, 0)
     full2 = lambda i, lo, hi: (0, 0)
     blk3 = lambda i, lo, hi: (0, i, 0)
-    blk2 = lambda i, lo, hi: (i, 0)
     wide = heads * HD
     return pl.pallas_call(
         functools.partial(bwd_kernel, heads, bq, bk),
@@ -206,11 +206,7 @@
                 pl.BlockSpec((rows, wide), full2),
                 pl.BlockSpec((rows, wide), full2),
             ],
-            out_specs=[
-                pl.BlockSpec((rows, wide), full2),
-                pl.BlockSpec((bk, wide), blk2),
-                pl.BlockSpec((bk, wide), blk2),
-            ],
+            out_specs=pl.BlockSpec((rows, 3 * wide), full2),
             scratch_shapes=[
                 pltpu.VMEM((heads, rows, LANES), BF),
                 pltpu.VMEM((heads, HD, rows), F32),
@@ -221,8 +217,8 @@
                 pltpu.VMEM((heads, HD, bk), F32),
             ],
         ),
-        out_shape=[jax.ShapeDtypeStruct((rows, wide), BF)] * 3,
-        compiler_params=pltpu.CompilerParams(vmem_limit_bytes=48 << 20),
+        out_shape=jax.ShapeDtypeStruct((rows, 3 * wide), BF),
+        compiler_params=pltpu.CompilerParams(vmem_limit_bytes=60 << 20),
         name="attend_back",
     )(lo, hi, qb, ke, ve, go, att)
 
@@ -294,7 +290,7 @@
         out_specs=[four, four, four, four, five, five],
         out_shape=[like(a) for a in (weights, first, second, average, stats, bases)],
         scratch_shapes=[pltpu.VMEM((2 * group, size, LANES), F32)],
-        compiler_params=pltpu.CompilerParams(vmem_limit_bytes=48 << 20),
+        compiler_params=pltpu.CompilerParams(vmem_limit_bytes=60 << 20),
         name="soap",
     )(ga, gb, weights, first, second, average, stats, bases)
 
@@ -424,7 +420,7 @@
             out(heads, VT, rows),
             out(width, 3 * heads * HD),
         ],
-        compiler_params=pltpu.CompilerParams(vmem_limit_bytes=48 << 20),
+        compiler_params=pltpu.CompilerParams(vmem_limit_bytes=60 << 20),
         name="project",
     )(row_own, wire, tokens, seg, pad, gain_one)
 
@@ -569,14 +565,13 @@
             jax.ShapeDtypeStruct(wire.shape, BF),
             jax.ShapeDtypeStruct((shards, width, 3 * span), BF),
         ],
-        compiler_params=pltpu.CompilerParams(vmem_limit_bytes=56 << 20),
+        compiler_params=pltpu.CompilerParams(vmem_limit_bytes=60 << 20),
         name="middle",
     )(here, row_full, wire, att, tokens, cotangent, pad, gain_two)
 
 
-def mixgrad_kernel(heads, rows_dev, wide, gain_row, gains_dev, row_ref, norm_ref, dq_ref, dk_ref, dv_ref, mix_ref, gain_ref, grads_ref, acc_ref):
+def mixgrad_kernel(heads, rows_dev, wide, gain_row, gains_dev, row_ref, norm_ref, bm_ref, mix_ref, gain_ref, grads_ref, acc_ref):
     width = norm_ref.shape[1]
-    span = heads * HD
     half = HD // 2
     cols = 3 * heads
 
@@ -584,9 +579,7 @@
     def _():
         acc_ref[...] = jnp.zeros_like(acc_ref)
 
-    normed = norm_ref[...]
-    for part, ref in enumerate((dq_ref, dk_ref, dv_ref)):
-        acc_ref[:, part * span : (part + 1) * span] += tn(normed, ref[...])
+    acc_ref[...] += tn(norm_ref[...], bm_ref[...])
 
     @pl.when(pl.program_id(0) == pl.num_programs(0) - 1)
     def _():
@@ -610,9 +603,9 @@
                 grads_ref[at : at + 1, :] = line[:, piece * LANES : (piece + 1) * LANES].astype(BF)
 
 
-def mixgrad(row_own, normed, dq, dk, dv, mix, gain_one, wire_shape, wide, rows_dev, gain_row, gains_dev):
+def mixgrad(row_own, normed, bm, mix, gain_one, wire_shape, wide, rows_dev, gain_row, gains_dev):
     rows, width = normed.shape
-    span = dq.shape[1]
+    span = bm.shape[1] // 3
     tb = min(512, rows)
     full = lambda i, r: (0, 0)
     blk = lambda i, r: (i, 0)
@@ -623,9 +616,7 @@
             grid=(rows // tb,),
             in_specs=[
                 pl.BlockSpec((tb, width), blk),
-                pl.BlockSpec((tb, span), blk),
-                pl.BlockSpec((tb, span), blk),
-                pl.BlockSpec((tb, span), blk),
+                pl.BlockSpec((tb, 3 * span), blk),
                 pl.BlockSpec((width, 3 * span), full),
                 pl.BlockSpec((1, width), full),
             ],
@@ -633,27 +624,34 @@
             scratch_shapes=[pltpu.VMEM((width, 3 * span), F32)],
         ),
         out_shape=jax.ShapeDtypeStruct(wire_shape, BF),
-        compiler_params=pltpu.CompilerParams(vmem_limit_bytes=48 << 20),
+        compiler_params=pltpu.CompilerParams(vmem_limit_bytes=60 << 20),
         name="mixgrad",
-    )(row_own, normed, dq, dk, dv, mix, gain_one)
-
-
-def tail_kernel(shards, here_ref, bm_ref, mix_ref, tok_ref, res_ref, gain_ref, out_ref):
+    )(row_own, normed, bm, mix, gain_one)
+
+
+def tail_kernel(shards, tb, gain_row, here_ref, bm_ref, mix_ref, tok_ref, res_ref, gain_ref, part_ref, out_ref):
     back = nt(bm_ref[0], mix_ref[0])
     for n in range(1, shards):
         back += nt(bm_ref[n], mix_ref[n])
     xhat, scale = normalize(tok_ref[...].astype(F32))
-    out_ref[...] = (res_ref[...] + norm_back(back * gain_ref[...], xhat, scale)).astype(BF)
-
-
-def tail(here, bm, mix, tokens, res, gain_one):
+    grad = res_ref[...] + norm_back(back * gain_ref[...], xhat, scale)
+    at = pl.multiple_of(pl.program_id(0) * tb, tb)
+    out_ref[pl.ds(at, tb), :] = grad.astype(BF)
+
+    @pl.when(pl.program_id(0) == pl.num_programs(0) - 1)
+    def _():
+        out_ref[-16:, :] = jnp.zeros((16, out_ref.shape[1]), BF)
+        out_ref[-16:, :LANES] = part_ref[gain_row : gain_row + 16, :]
+
+
+def tail(here, bm, mix, tokens, res, gain_one, part, gain_row):
     shards, own, cols = bm.shape
     width = tokens.shape[1]
     tb = min(256, own)
     steps = own // tb
     full3 = lambda i, h: (0, 0, 0)
     return pl.pallas_call(
-        functools.partial(tail_kernel, shards),
+        functools.partial(tail_kernel, shards, tb, gain_row),
         grid_spec=pltpu.PrefetchScalarGridSpec(
             num_scalar_prefetch=1,
             grid=(steps,),
@@ -663,13 +661,14 @@
                 pl.BlockSpec((tb, width), lambda i, h: (h[0] * steps + i, 0)),
                 pl.BlockSpec((tb, width), lambda i, h: (i, 0)),
                 pl.BlockSpec((1, width), lambda i, h: (0, 0)),
-            ],
-            out_specs=pl.BlockSpec((tb, width), lambda i, h: (i, 0)),
+                pl.BlockSpec(part.shape, lambda i, h: (0, 0)),
+            ],
+            out_specs=pl.BlockSpec((own + 16, width), lambda i, h: (0, 0)),
         ),
-        out_shape=jax.ShapeDtypeStruct((own, width), BF),
-        compiler_params=pltpu.CompilerParams(vmem_limit_bytes=48 << 20),
+        out_shape=jax.ShapeDtypeStruct((own + 16, width), BF),
+        compiler_params=pltpu.CompilerParams(vmem_limit_bytes=60 << 20),
         name="tail",
-    )(here, bm, mix, tokens, res, gain_one)
+    )(here, bm, mix, tokens, res, gain_one, part)
 
 
 def adam_gains(grad, gain, first, second, average):
@@ -746,22 +745,25 @@
     out_own, back_res, back_own, grads, mix_full = middle(
         here_of, row_full, wire_full, att_own, tokens, cotangent, pad, gain_two, wide, rows_dev, gain_row, gains_dev
     )
-    output = lax.all_gather(out_own, "narrow", axis=0, tiled=True)
+    part_a = lax.psum_scatter(grads, "wide", scatter_dimension=0, tiled=True)
     back_att = lax.all_to_all(back_own, "narrow", 0, 0).reshape(rows, span)
-    dq, dk, dv = attend_back(qb, ke, ve, back_att, attended, begin, end, block, block)
-    grads_mix = mixgrad(row_own, normed, dq, dk, dv, mix, gain_one, wire_own.shape, wide, rows_dev, gain_row, gains_dev)
-    bm = to_shards(jnp.concatenate([dq, dk, dv], axis=1), narrow)
-    grad_own = tail(here_of, bm, mix_full, tokens, back_res, gain_one)
-    input_grad = lax.all_gather(grad_own, "narrow", axis=0, tiled=True).astype(F32)
-
-    part_a = lax.psum_scatter(grads, "wide", scatter_dimension=0, tiled=True)
+    out_own, back_att = lax.optimization_barrier((out_own, back_att))
+    output = lax.all_to_all(jnp.broadcast_to(out_own, (narrow, own, width)), "narrow", 0, 0).reshape(rows, width)
+    bm = attend_back(qb, ke, ve, back_att, attended, begin, end, block, block)
+    bm_own = to_shards(bm, narrow)
+    bm, part_a, output = lax.optimization_barrier((bm, part_a, output))
     part_a = lax.psum_scatter(part_a, "narrow", scatter_dimension=0, tiled=True)
+    grads_mix = mixgrad(row_own, normed, bm, mix, gain_one, wire_own.shape, wide, rows_dev, gain_row, gains_dev)
     part_b = lax.psum_scatter(grads_mix, "wide", scatter_dimension=0, tiled=True)
+    grad_own = tail(here_of, bm_own, mix_full, tokens, back_res, gain_one, part_b, gain_row)
+    grad_all = lax.all_gather(grad_own, "narrow", axis=0, tiled=False)
+    input_grad = grad_all[:, :own].reshape(rows, width).astype(F32)
+    part_a, part_b, _ = lax.optimization_barrier((part_a, part_b, grad_own))
     group = 8 if slots % 8 == 0 else 1
     new_weight, new_first, new_second, new_average, new_stats, new_bases = soap(
         part_a, part_b, weights, first_moment, second_moment, average, stats, bases, group
     )
-    line = part_a[gain_row].astype(F32) + lax.psum(part_b[gain_row].astype(F32), "narrow")
+    line = part_a[gain_row].astype(F32) + jnp.sum(grad_all[:, own, :LANES].astype(F32), axis=0)
     offset = lax.axis_index("wide") * gains_dev % LANES
     own_gain = lax.dynamic_slice_in_dim(line, offset, gains_dev, 0)
     new_gains, gain_moment, gain_square, gain_mean = adam_gains(own_gain, gains, gain_first, gain_second, gain_average)

time: 542 us -> 518 us (0.956); the launches traced: 540 us -> 511 us
  waiting for transfers between devices: 157 us -> 134 us
  blocking collectives: 50.7 us -> 43.3 us
    all_gather x2 -> x1, waiting for transfers between devices: 51.9 us -> 15.8 us  [body(): grad_all = lax.all_gather(grad_own, 'narrow', axis=0, tiled=False)]
    reduce_scatter x1, waiting for transfers between devices: 41.6 us -> 18.3 us  [body(): part_a = lax.psum_scatter(part_a, 'narrow', scatter_dimension=0, tiled=True)]
    all_to_all x2, waiting for transfers between devices: 56 us -> 75.2 us  [to_shards(): lax.all_to_all(values.reshape(shards, rows // shards, cols), 'narrow', 0, 0)]
    all_to_all x0 -> x1, waiting for transfers between devices: none -> 18.6 us  [body(): lax.all_to_all(jnp.broadcast_to(out_own, (narrow, own, width)), 'narrow',...]
    psum x1 -> x0, blocking collectives: 10.4 us -> none  [body(): lax.psum(part_b[gain_row].astype(F32), 'narrow')]
    unnamed x47 -> x23, local copies, waits for them, and re-layouts: 16.4 us -> 7.14 us
  transfers between devices with their start and end apart: 9 -> 9, of which waited for: 5 -> 7; matrix products, arithmetic and copies ran while one was open for 1% -> 1% of each run, Pallas kernels for 43% -> 46%
where the time goes in v2:
time: 518 us; the launch traced here: 511 us
  Pallas kernels  279 us (54%)
  waiting for transfers between devices  134 us (26%)
  blocking collectives  43.3 us (8%)
  between operations  14.5 us (3%)
  starting transfers between devices  14 us (3%)
  local copies, waits for them, and re-layouts  13.4 us (3%)
  other arithmetic  12.1 us (2%)
    pallas_call x1, Pallas kernels, soap(): pl.pallas_call(functools.partial(soap_kernel, group), grid=(slots // grou...  80.8 us
    all_to_all x2, waiting for transfers between devices, to_shards(): lax.all_to_all(values.reshape(shards, rows // shards, cols), 'narrow', 0, 0)  75.2 us
    pallas_call x1, Pallas kernels, attend_back(): pl.pallas_call(functools.partial(bwd_kernel, heads, bq, bk), grid_spec=pl...  71.6 us
    pallas_call x1, Pallas kernels, attend(): pl.pallas_call(functools.partial(fwd_kernel, heads, bq, bk), grid_spec=pl...  48 us
    pallas_call x1, Pallas kernels, middle(): pl.pallas_call(functools.partial(middle_kernel, shards, span, units, rows...  46 us
    all_gather x1, blocking collectives, body(): lax.all_gather(wire, 'narrow', axis=0, tiled=True)  21.9 us
    all_to_all x1, blocking collectives, body(): back_att = lax.all_to_all(back_own, 'narrow', 0, 0).reshape(rows, span)  21.4 us
    all_to_all x1, waiting for transfers between devices, body(): lax.all_to_all(jnp.broadcast_to(out_own, (narrow, own, width)), 'narrow',...  18.6 us
  transfers between devices with their start and end apart: 9, of which 7 were waited for; matrix products, arithmetic and copies ran while one was open for 1% of the time, Pallas kernels for 46%

profile of v2, /device:TPU:0, one launch (start us, length us, event | category | flops | bytes accessed | tf_op | source)
XLA Modules:
  0.0 510.6 jit_solution(11648633757904901214)
XLA Ops:
  7.9 1.2 convert_bitcast_fusion
  10.1 21.9 %all_gather.16 = bf16[3136,128]{1,0:T(8,128)(2,1)} all-gather(bf16[784,128]{1,0:T(8,128)(2,1)} %fusion.1), channel_id=1, replica_groups=mesh['wide'=8,'narrow'=4] {'narrow'}, dimensions={0}, use_global_device_ids=true | all-gather | bytes 1003520 | tf_op jit(solution)/shard_map/all_gather | solution.py:722
  34.8 4.2 all-gather.5.cloned.1.call-done.wire_ref
  40.4 15.3 %project.1 = (bf16[4096,512]{1,0:T(8,128)(2,1)}, bf16[2,4096,128]{2,1,0:T(8,128)(2,1)}, bf16[2,4096,128]{2,1,0:T(8,128)(2,1)}, bf16[2,4096,128]{2,1,0:T(8,128)(2...) custom-call(s32[192]{0:T(256)} %multiply_add_fusion.1.row_ref, ...), custom_call_target="tpu_custom_call" | custom-call | tf_op jit(solution)/shard_map/project/pallas_call | solution.py:393
  55.7 48.0 %attend.1 = (bf16[4096,128]{1,0:T(8,128)(2,1)}, bf16[2,4096,128]{2,1,0:T(8,128)(2,1)}) custom-call(s32[8]{0:T(128)} %get-tuple-element.77.lo_ref, s32[8]{0:T(128)} %get-tuple-element.76.hi_ref, bf16[2,4096,128]{2,1,0:T(8,128)(2,1)} %get-tuple-element.38.qe_ref, bf16[2,4096,128]{2,1,0:T(8,128)(2,1)} %get-tuple-element.39.ke_ref, ...), custom_call_target="tpu_custom_call" | custom-call | tf_op jit(solution)/shard_map/attend/pallas_call | solution.py:105
  103.7 4.7 all-to-all-start
  108.9 16.2 %all-to-all-done.att_ref = bf16[4,1024,128]{2,1,0:T(8,128)(2,1)S(1)} async-done(((bf16[4,1024,128]{2,1,0:T(8,128)(2,1)}), bf16[4,1024,128]{2,1,0:T(8,128)(2,1)S(1)}, u32[]{:S(2)}, u32[]{:S(2)}) %all-to-all-start) | async-done | bytes 1048608 | tf_op jit(solution)/shard_map/all_to_all | solution.py:684
  126.1 46.0 %middle.1 = (bf16[1024,512]{1,0:T(8,128)(2,1)}, f32[1024,512]{1,0:T(8,128)}, bf16[4,1024,128]{2,1,0:T(8,128)(2,1)}, bf16[25088,128]{1,0:T(8,128)(2,1)}, bf16[4,512,384]{2,1,0:T(8,128)(2,1)}) custom-call(s32[1]{0:T(128)} %bitcast.6.here_ref, s32[192]{0:T(256)} %get-tuple-element.70.row_ref, bf16[25088,128]{1,0:T(8,128)(2,1)} %all-gather.7.cloned.1.call-done.wire_ref, ...), custom_call_target="tpu_custom_call" | custom-call | tf_op jit(solution)/shard_map/middle/pallas_call | solution.py:531
  173.3 21.4 %all_to_all.20 = bf16[4,1024,128]{2,1,0:T(8,128)(2,1)} all-to-all(bf16[4,1024,128]{2,1,0:T(8,128)(2,1)S(1)} %copy-done.3), channel_id=1, replica_groups=mesh['wide'=8,'narrow'=4] {'narrow'}, dimensions={0} | all-to-all | bytes 2097152 | tf_op jit(solution)/shard_map/all_to_all | solution.py:749
  194.7 2.3 broadcast_in_dim.30
  197.0 5.0 all-to-all-start.2
  202.0 71.6 %attend_back.1.bm_ref = bf16[4096,384]{1,0:T(8,128)(2,1)} custom-call(s32[8]{0:T(128)} %get-tuple-element.77.lo_ref, s32[8]{0:T(128)} %get-tuple-element.76.hi_ref, bf16[2,4096,128]{2,1,0:T(8,128)(2,1)} %get-tuple-element.41.qb_ref, bf16[2,4096,128]{2,1,0:T(8,128)(2,1)} %get-tuple-element.39.ke_ref, bf16[2,4096,128]{2,1,0:T(8,128)(2,1)} %get-tuple-element.42.ve_ref, ...), custom_call_target="tpu_custom_call" | custom-call | tf_op jit(solution)/shard_map/attend_back/pallas_call | solution.py:197
  273.6 18.6 %all-to-all-done.2 = bf16[4,1024,512]{2,1,0:T(8,128)(2,1)} async-done(((bf16[4,1024,512]{2,1,0:T(8,128)(2,1)}), bf16[4,1024,512]{2,1,0:T(8,128)(2,1)}, u32[]{:S(2)}, u32[]{:S(2)}) %all-to-all-start.2) | async-done | bytes 4194336 | tf_op jit(solution)/shard_map/all_to_all | solution.py:751
  292.2 3.7 all-to-all-start.3
  296.0 10.4 %mixgrad.1 = bf16[6272,128]{1,0:T(8,128)(2,1)} custom-call(s32[192]{0:T(256)} %multiply_add_fusion.1.row_ref, bf16[4096,512]{1,0:T(8,128)(2,1)} %get-tuple-element.52.norm_ref, bf16[4096,384]{1,0:T(8,128)(2,1)} %attend_back.1.bm_ref, bf16[512,384]{1,0:T(8,128)(2,1)} %get-tuple-element.54.mix_ref, f32[1,512]{1,0:T(1,128)} %get-tuple-element.75.gain_ref), custom_call_target="tpu_custom_call" | custom-call | tf_op jit(solution)/shard_map/mixgrad/pallas_call | solution.py:612
  307.0 59.0 %all-to-all-done.3.bm_ref = bf16[4,1024,384]{2,1,0:T(8,128)(2,1)S(1)} async-done(((bf16[4,1024,384]{2,1,0:T(8,128)(2,1)}), bf16[4,1024,384]{2,1,0:T(8,128)(2,1)S(1)}, u32[]{:S(2)}, u32[]{:S(2)}) %all-to-all-start.3) | async-done | bytes 3145760 | tf_op jit(solution)/shard_map/all_to_all | solution.py:684
  367.7 7.0 %tail.1 = bf16[1040,512]{1,0:T(8,128)(2,1)} custom-call(s32[1]{0:T(128)} %bitcast.6.here_ref, bf16[4,1024,384]{2,1,0:T(8,128)(2,1)} %copy-done, bf16[4,512,384]{2,1,0:T(8,128)(2,1)} %get-tuple-element.50.mix_ref, bf16[4096,512]{1,0:T(8,128)(2,1)} %tok_ref.5, f32[1024,512]{1,0:T(8,128)} %get-tuple-element.51.res_ref, f32[1,512]{1,0:T(1,128)} %get-tuple-element.75.gain_ref, ...), custom_call_target="tpu_custom_call" | custom-call | tf_op jit(solution)/shard_map/tail/pallas_call | solution.py:653
  374.8 18.3 %reduce-scatter.8.cloned.1.call-done.ga_ref = bf16[784,128]{1,0:T(8,128)(2,1)} async-done(((bf16[3136,128]{1,0:T(8,128)(2,1)}), bf16[784,128]{1,0:T(8,128)(2,1)}) %reduce-scatter.8.cloned.1.call-update) | async-done | bytes 200720 | tf_op jit(solution)/shard_map/reduce_scatter | solution.py:755
  393.1 80.8 %soap.1 = (f32[1,24,64,64]{3,2,1,0:T(8,128)}, f32[1,24,64,64]{3,2,1,0:T(8,128)}, f32[1,24,64,64]{3,2,1,0:T(8,128)}, f32[1,24,64,64]{3,2,1,0:T(8,128)}, f32[1,24,...) custom-call(bf16[784,128]{1,0:T(8,128)(2,1)} %reduce-scatter.8.cloned.1.call-done.ga_ref, ...), custom_call_target="tpu_custom_call" | custom-call | tf_op jit(solution)/shard_map/soap/pallas_call | solution.py:286
  473.8 15.8 %all-gather.9.cloned.1.call-done = bf16[4160,512]{1,0:T(8,128)(2,1)} async-done(((bf16[1040,512]{1,0:T(8,128)(2,1)}), bf16[4160,512]{1,0:T(8,128)(2,1)}) %all-gather.9.cloned.1.call-update) | async-done | bytes 4259856 | tf_op jit(solution)/shard_map/all_gather | solution.py:759
  490.4 2.5 slice.45
  492.9 4.9 bitcast_convert_fusion
  497.8 1.2 add_multiply_fusion
  499.0 4.5 copy.32
  (53 shorter events, 11.5 us)
Async XLA Ops:
  7.2 24.8 %copy-start.4 = (s32[1,4096]{1,0:T(1,128)S(1)}, s32[1,4096]{1,0:T(1,128)}, u32[]{:S(2)}) copy-start(s32[1,4096]{1,0:T(1,128)} %seg_ref.1) | copy-start | bytes 49156
  7.2 25.0 %copy-start.5 = (s32[1,4096]{1,0:T(1,128)S(1)}, s32[1,4096]{1,0:T(1,128)}, u32[]{:S(2)}) copy-start(s32[1,4096]{1,0:T(1,128)} %param.18) | copy-start | bytes 49156
  7.2 25.9 %copy-start.6 = (s32[192]{0:T(256)S(1)}, s32[192]{0:T(256)}, u32[]{:S(2)}) copy-start(s32[192]{0:T(256)} %param.19) | copy-start | bytes 2308
  7.2 31.9 %all-gather.5.cloned.1.call-start = ((), (), s32[]{:S(2)}) async-start(), calls=%async_computation.7 | async-start | bytes 1806336 | tf_op jit(solution)/shard_map/all_gather | solution.py:721
  10.0 115.1 %all-gather.7.cloned.1.call-start = ((), (), s32[]{:S(2)}) async-start(), calls=%async_computation.8 | async-start | bytes 7225344 | tf_op jit(solution)/shard_map/all_gather | solution.py:722
  103.7 21.3 %all-to-all-start = ((bf16[4,1024,128]{2,1,0:T(8,128)(2,1)}), bf16[4,1024,128]{2,1,0:T(8,128)(2,1)S(1)}, u32[]{:S(2)}, u32[]{:S(2)}) async-start(bf16[4,1024,128]{2,1,0:T(8,128)(2,1)} %bitcast.27), calls=%async_computation | async-start | bytes 2097152 | tf_op jit(solution)/shard_map/all_to_all | solution.py:684
  108.4 187.6 %reduce-scatter.4.cloned.1.call-start = ((), (), s32[]{:S(2)}) async-start(), calls=%async_computation.9 | async-start | bytes 7225344 | tf_op jit(solution)/shard_map/reduce_scatter | solution.py:748
  125.1 1.0 copy-start.1
  172.1 1.2 copy-start.3
  172.1 22.6 %copy-start.2 = (bf16[1024,512]{1,0:T(8,128)(2,1)S(1)}, bf16[1024,512]{1,0:T(8,128)(2,1)}, u32[]{:S(2)}) copy-start(bf16[1024,512]{1,0:T(8,128)(2,1)} %get-tuple-element.48) | copy-start | bytes 3145732
  197.0 95.2 %all-to-all-start.2 = ((bf16[4,1024,512]{2,1,0:T(8,128)(2,1)}), bf16[4,1024,512]{2,1,0:T(8,128)(2,1)}, u32[]{:S(2)}, u32[]{:S(2)}) async-start(bf16[4,1024,512]{2,1,0:T(8,128)(2,1)} %broadcast_in_dim.30), calls=%async_computation.3 | async-start | bytes 8388608 | tf_op jit(solution)/shard_map/all_to_all | solution.py:751
  292.2 73.8 %all-to-all-start.3 = ((bf16[4,1024,384]{2,1,0:T(8,128)(2,1)}), bf16[4,1024,384]{2,1,0:T(8,128)(2,1)S(1)}, u32[]{:S(2)}, u32[]{:S(2)}) async-start(bf16[4,1024,384]{2,1,0:T(8,128)(2,1)} %bitcast.26), calls=%async_computation.4 | async-start | bytes 6291456 | tf_op jit(solution)/shard_map/all_to_all | solution.py:684
  295.9 71.3 %reduce-scatter.6.cloned.1.call-start = ((), (), s32[]{:S(2)}) async-start(), calls=%async_computation.10 | async-start | bytes 1806336 | tf_op jit(solution)/shard_map/reduce_scatter | solution.py:757
  306.4 86.7 %reduce-scatter.8.cloned.1.call-start = ((), (), s32[]{:S(2)}) async-start(), calls=%async_computation.11 | async-start | bytes 1003520 | tf_op jit(solution)/shard_map/reduce_scatter | solution.py:755
  307.0 182.7 %all-gather.9.cloned.1.call-start = ((), (), s32[]{:S(2)}) async-start(), calls=%async_computation.12 | async-start | bytes 5324800 | tf_op jit(solution)/shard_map/all_gather | solution.py:759
  366.1 1.7 copy-start
  492.9 4.9 copy-start.7
  492.9 4.9 copy-start.8
  492.9 4.9 copy-start.9
  492.9 4.9 copy-start.10
Sparse Core Ops, SparseCore 0:
  10.5 28.5 all-gather.4
  40.9 46.1 all-gather.6
  172.3 70.4 reduce-scatter.3
  306.5 60.7 reduce-scatter.5
  369.5 23.5 reduce-scatter.7
  395.1 94.4 all-gather.8

commit v3 on v2

--- a/solution.py
+++ b/solution.py
@@ -232,30 +232,38 @@
     size = w_ref.shape[-1]
     half = size // 2
     panel = 8
-    for s in range(group):
+    every = range(group)
+    grads, firsts = [], []
+    for s in every:
         wire = ga_ref[s * half : (s + 1) * half, :].astype(F32) + gb_ref[s * half : (s + 1) * half, :].astype(F32)
-        grad = jnp.concatenate([wire[:, :size], wire[:, size:]], axis=0)
-        left, right = ba_ref[0, s, 0], ba_ref[0, s, 1]
-        weight = w_ref[0, s]
-        first = beta_one * m1_ref[0, s] + (1.0 - beta_one) * grad
-        n1_ref[0, s] = first
-        both = dot_f32(jnp.concatenate([grad, first], axis=0), right, (1, 0))
-        pair = dot_f32(left, jnp.concatenate([both[:size], both[size:]], axis=1), (0, 0))
-        rotated, moment = pair[:, :size], pair[:, size:]
+        grads.append(jnp.concatenate([wire[:, :size], wire[:, size:]], axis=0))
+        firsts.append(beta_one * m1_ref[0, s] + (1.0 - beta_one) * grads[s])
+        n1_ref[0, s] = firsts[s]
+    sides = [(s, side) for s in every for side in range(2)]
+    outers = [dot_f32(grads[s], grads[s], (1, 1) if side == 0 else (0, 0)) for s, side in sides]
+    both = [dot_f32(jnp.concatenate([grads[s], firsts[s]], axis=0), ba_ref[0, s, 1], (1, 0)) for s in every]
+    stats = []
+    for (s, side), outer in zip(sides, outers):
+        stats.append(beta_two * st_ref[0, s, side] + (1.0 - beta_two) * outer)
+        ns_ref[0, s, side] = stats[-1]
+    pairs = [dot_f32(ba_ref[0, s, 0], jnp.concatenate([both[s][:size], both[s][size:]], axis=1), (0, 0)) for s in every]
+    mts = [dot_f32(ba_ref[0, s, side], stat, (0, 1)) for (s, side), stat in zip(sides, stats)]
+    scaled = []
+    for s in every:
+        rotated, moment = pairs[s][:, :size], pairs[s][:, size:]
         second = beta_two * m2_ref[0, s] + (1.0 - beta_two) * rotated * rotated
         n2_ref[0, s] = second
-        scaled = moment / (jnp.sqrt(second) + step_eps)
-        direction = dot_f32(left, dot_f32(scaled, right, (1, 1)), (1, 0))
-        fresh = weight - step_rate * (direction + weight_decay * weight)
+        scaled.append(moment / (jnp.sqrt(second) + step_eps))
+    grams = [dot_f32(mt, mt, (1, 1)) for mt in mts]
+    inner = [dot_f32(scaled[s], ba_ref[0, s, 1], (1, 1)) for s in every]
+    for m, (gram, mt) in enumerate(zip(grams, mts)):
+        aug_ref[m] = jnp.concatenate([gram, mt], axis=1)
+    directions = [dot_f32(ba_ref[0, s, 0], inner[s], (1, 0)) for s in every]
+    for s in every:
+        weight = w_ref[0, s]
+        fresh = weight - step_rate * (directions[s] + weight_decay * weight)
         nw_ref[0, s] = fresh
         na_ref[0, s] = average_keep * av_ref[0, s] + (1.0 - average_keep) * fresh
-        for side, base in ((0, left), (1, right)):
-            outer = dot_f32(grad, grad, (1, 1) if side == 0 else (0, 0))
-            stat = beta_two * st_ref[0, s, side] + (1.0 - beta_two) * outer
-            ns_ref[0, s, side] = stat
-            mt = dot_f32(base, stat, (0, 1))
-            gram = dot_f32(mt, mt, (1, 1))
-            aug_ref[2 * s + side] = jnp.concatenate([gram, mt], axis=1)
     count = 2 * group
     row = lax.broadcasted_iota(jnp.int32, (count, panel, LANES), 1)
     for p in range(size // panel):
@@ -269,9 +277,16 @@
         aug_ref[:, top : top + panel, :] = part
         below = top + panel
         if below < size:
+            high = part.astype(BF).astype(F32)
+            rest = part - high
+            mid = rest.astype(BF).astype(F32)
+            low = rest - mid
+            first = jnp.concatenate([high, high, mid, high, mid, low], axis=1).astype(BF)
+            other = jnp.concatenate([high, mid, high, low, mid, high], axis=1).astype(BF)
             for m in range(count):
-                one = part[m]
-                aug_ref[m, below:, :] -= dot_f32(one[:, below:size], one, (0, 0))
+                aug_ref[m, below:, :] -= lax.dot_general(
+                    first[m][:, below:size], other[m], (((0,), (0,)), ((), ())), preferred_element_type=F32
+                )
     for s in range(group):
         for side in range(2):
             nb_ref[0, s, side] = aug_ref[2 * s + side][:, size:].T
@@ -682,6 +697,13 @@
 def to_shards(values, shards):
     rows, cols = values.shape
     return lax.all_to_all(values.reshape(shards, rows // shards, cols), "narrow", 0, 0)
+
+
+def spread(values, shards, own):
+    cut = own // 2
+    first = lax.all_gather(jnp.concatenate([values[:cut], values[own:]], axis=0), "narrow", axis=0, tiled=False)
+    rest = lax.all_to_all(jnp.broadcast_to(values[cut:own], (shards, own - cut, values.shape[1])), "narrow", 0, 0)
+    return jnp.concatenate([first[:, :cut], rest, first[:, cut:]], axis=1)
 
 
 def body(
@@ -748,7 +770,7 @@
     part_a = lax.psum_scatter(grads, "wide", scatter_dimension=0, tiled=True)
     back_att = lax.all_to_all(back_own, "narrow", 0, 0).reshape(rows, span)
     out_own, back_att = lax.optimization_barrier((out_own, back_att))
-    output = lax.all_to_all(jnp.broadcast_to(out_own, (narrow, own, width)), "narrow", 0, 0).reshape(rows, width)
+    output = spread(out_own, narrow, own).reshape(rows, width)
     bm = attend_back(qb, ke, ve, back_att, attended, begin, end, block, block)
     bm_own = to_shards(bm, narrow)
     bm, part_a, output = lax.optimization_barrier((bm, part_a, output))
@@ -756,10 +778,10 @@
     grads_mix = mixgrad(row_own, normed, bm, mix, gain_one, wire_own.shape, wide, rows_dev, gain_row, gains_dev)
     part_b = lax.psum_scatter(grads_mix, "wide", scatter_dimension=0, tiled=True)
     grad_own = tail(here_of, bm_own, mix_full, tokens, back_res, gain_one, part_b, gain_row)
-    grad_all = lax.all_gather(grad_own, "narrow", axis=0, tiled=False)
+    grad_all = spread(grad_own, narrow, own)
     input_grad = grad_all[:, :own].reshape(rows, width).astype(F32)
     part_a, part_b, _ = lax.optimization_barrier((part_a, part_b, grad_own))
-    group = 8 if slots % 8 == 0 else 1
+    group = next(g for g in range(min(12, slots), 0, -1) if slots % g == 0)
     new_weight, new_first, new_second, new_average, new_stats, new_bases = soap(
         part_a, part_b, weights, first_moment, second_moment, average, stats, bases, group
     )

time: 518 us -> 531 us (1.025)
  Pallas kernels: 279 us -> 202 us
  waiting for transfers between devices: 134 us -> 205 us
  blocking collectives: 43.3 us -> 53.3 us
  other arithmetic: 12.1 us -> 20.1 us
    pallas_call x1, Pallas kernels: 80.8 us -> 28.3 us  [soap(): pl.pallas_call(functools.partial(soap_kernel, group), grid=(slots // grou...]
    reduce_scatter x1, waiting for transfers between devices: 0.02 us -> 49.5 us  [body(): part_a = lax.psum_scatter(grads, 'wide', scatter_dimension=0, tiled=True)]
    all_to_all x2, waiting for transfers between devices: 75.2 us -> 31.5 us  [to_shards(): lax.all_to_all(values.reshape(shards, rows // shards, cols), 'narrow', 0, 0)]
    reduce_scatter x1, waiting for transfers between devices: 1.19 us -> 33 us  [body(): lax.psum_scatter(grads_mix, 'wide', scatter_dimension=0, tiled=True)]
    all_gather x1 -> x2, waiting for transfers between devices: 15.8 us -> 38.3 us  [spread(): lax.all_gather(jnp.concatenate([values[:cut], values[own:]], axis=0), 'na...]
    pallas_call x1, Pallas kernels: 71.6 us -> 56.9 us  [attend_back(): pl.pallas_call(functools.partial(bwd_kernel, heads, bq, bk), grid_spec=pl...]
    all_to_all x1, blocking collectives: 21.4 us -> 31.4 us  [body(): back_att = lax.all_to_all(back_own, 'narrow', 0, 0).reshape(rows, span)]
    pallas_call x1, Pallas kernels: 48 us -> 38.5 us  [attend(): pl.pallas_call(functools.partial(fwd_kernel, heads, bq, bk), grid_spec=pl...]
  transfers between devices with their start and end apart: 9 -> 11, of which waited for: 7 -> 8; matrix products, arithmetic and copies ran while one was open for 1% -> 3% of each run, Pallas kernels for 46% -> 30%
where the time goes in v3:
time: 531 us; the launch traced here: 524 us
  waiting for transfers between devices  205 us (39%)
  Pallas kernels  202 us (38%)
  blocking collectives  53.3 us (10%)
  other arithmetic  20.1 us (4%)
  starting transfers between devices  17 us (3%)
  between operations  14.3 us (3%)
  local copies, waits for them, and re-layouts  12 us (2%)
    pallas_call x1, Pallas kernels, attend_back(): pl.pallas_call(functools.partial(bwd_kernel, heads, bq, bk), grid_spec=pl...  56.9 us
    reduce_scatter x1, waiting for transfers between devices, body(): part_a = lax.psum_scatter(grads, 'wide', scatter_dimension=0, tiled=True)  49.5 us
    pallas_call x1, Pallas kernels, middle(): pl.pallas_call(functools.partial(middle_kernel, shards, span, units, rows...  46 us
    pallas_call x1, Pallas kernels, attend(): pl.pallas_call(functools.partial(fwd_kernel, heads, bq, bk), grid_spec=pl...  38.5 us
    all_gather x2, waiting for transfers between devices, spread(): lax.all_gather(jnp.concatenate([values[:cut], values[own:]], axis=0), 'na...  38.3 us
    reduce_scatter x1, waiting for transfers between devices, body(): lax.psum_scatter(grads_mix, 'wide', scatter_dimension=0, tiled=True)  33 us
    all_to_all x2, waiting for transfers between devices, to_shards(): lax.all_to_all(values.reshape(shards, rows // shards, cols), 'narrow', 0, 0)  31.5 us
    all_to_all x1, blocking collectives, body(): back_att = lax.all_to_all(back_own, 'narrow', 0, 0).reshape(rows, span)  31.4 us
  transfers between devices with their start and end apart: 11, of which 8 were waited for; matrix products, arithmetic and copies ran while one was open for 3% of the time, Pallas kernels for 30%

profile of v3, /device:TPU:0, one launch (start us, length us, event | category | flops | bytes accessed | tf_op | source)
XLA Modules:
  0.0 524.5 jit_solution(13629736274711158265)
XLA Ops:
  10.1 21.9 %all_gather.22 = bf16[3136,128]{1,0:T(8,128)(2,1)} all-gather(bf16[784,128]{1,0:T(8,128)(2,1)} %fusion.1), channel_id=1, replica_groups=mesh['wide'=8,'narrow'=4] {'narrow'}, dimensions={0}, use_global_device_ids=true | all-gather | bytes 1003520 | tf_op jit(solution)/shard_map/all_gather | solution.py:744
  34.9 4.1 all-gather.7.cloned.1.call-done.wire_ref
  40.4 15.3 %project.1 = (bf16[4096,512]{1,0:T(8,128)(2,1)}, bf16[2,4096,128]{2,1,0:T(8,128)(2,1)}, bf16[2,4096,128]{2,1,0:T(8,128)(2,1)}, bf16[2,4096,128]{2,1,0:T(8,128)(2...) custom-call(s32[192]{0:T(256)} %multiply_add_fusion.1.row_ref, ...), custom_call_target="tpu_custom_call" | custom-call | tf_op jit(solution)/shard_map/project/pallas_call | solution.py:408
  55.7 38.5 %attend.1 = (bf16[4096,128]{1,0:T(8,128)(2,1)}, bf16[2,4096,128]{2,1,0:T(8,128)(2,1)}) custom-call(s32[8]{0:T(128)} %get-tuple-element.81.lo_ref, s32[8]{0:T(128)} %get-tuple-element.80.hi_ref, bf16[2,4096,128]{2,1,0:T(8,128)(2,1)} %get-tuple-element.38.qe_ref, bf16[2,4096,128]{2,1,0:T(8,128)(2,1)} %get-tuple-element.39.ke_ref, ...), custom_call_target="tpu_custom_call" | custom-call | tf_op jit(solution)/shard_map/attend/pallas_call | solution.py:105
  94.2 4.6 all-to-all-start
  98.8 26.2 %all-to-all-done.att_ref = bf16[4,1024,128]{2,1,0:T(8,128)(2,1)S(1)} async-done(((bf16[4,1024,128]{2,1,0:T(8,128)(2,1)}), bf16[4,1024,128]{2,1,0:T(8,128)(2,1)S(1)}, u32[]{:S(2)}, u32[]{:S(2)}) %all-to-all-start) | async-done | bytes 1048608 | tf_op jit(solution)/shard_map/all_to_all | solution.py:699
  126.0 46.0 %middle.1 = (bf16[1024,512]{1,0:T(8,128)(2,1)}, f32[1024,512]{1,0:T(8,128)}, bf16[4,1024,128]{2,1,0:T(8,128)(2,1)}, bf16[25088,128]{1,0:T(8,128)(2,1)}, bf16[4,512,384]{2,1,0:T(8,128)(2,1)}) custom-call(s32[1]{0:T(128)} %bitcast.6.here_ref, s32[192]{0:T(256)} %get-tuple-element.70.row_ref, bf16[25088,128]{1,0:T(8,128)(2,1)} %all-gather.9.cloned.1.call-done.wire_ref, ...), custom_call_target="tpu_custom_call" | custom-call | tf_op jit(solution)/shard_map/middle/pallas_call | solution.py:546
  172.1 31.4 %all_to_all.25 = bf16[4,1024,128]{2,1,0:T(8,128)(2,1)} all-to-all(bf16[4,1024,128]{2,1,0:T(8,128)(2,1)} %get-tuple-element.45), channel_id=1, replica_groups=mesh['wide'=8,'narrow'=4] {'narrow'}, dimensions={0} | all-to-all | bytes 2097152 | tf_op jit(solution)/shard_map/all_to_all | solution.py:771
  206.4 3.9 all-to-all-start.2
  210.3 56.9 %attend_back.1.bm_ref = bf16[4096,384]{1,0:T(8,128)(2,1)} custom-call(s32[8]{0:T(128)} %get-tuple-element.81.lo_ref, s32[8]{0:T(128)} %get-tuple-element.80.hi_ref, bf16[2,4096,128]{2,1,0:T(8,128)(2,1)} %get-tuple-element.41.qb_ref, bf16[2,4096,128]{2,1,0:T(8,128)(2,1)} %get-tuple-element.39.ke_ref, bf16[2,4096,128]{2,1,0:T(8,128)(2,1)} %get-tuple-element.42.ve_ref, ...), custom_call_target="tpu_custom_call" | custom-call | tf_op jit(solution)/shard_map/attend_back/pallas_call | solution.py:197
  267.2 24.8 %all-to-all-done.2 = bf16[4,512,512]{2,1,0:T(8,128)(2,1)S(1)} async-done(((bf16[4,512,512]{2,1,0:T(8,128)(2,1)}), bf16[4,512,512]{2,1,0:T(8,128)(2,1)S(1)}, u32[]{:S(2)}, u32[]{:S(2)}) %all-to-all-start.2) | async-done | bytes 2097184 | tf_op jit(solution)/shard_map/all_to_all | solution.py:705
  293.3 3.7 all-to-all-start.3
  297.1 5.2 pad_maximum_fusion
  302.3 49.5 %reduce-scatter.4.cloned.1.call-done = bf16[3136,128]{1,0:T(8,128)(2,1)} async-done(((bf16[25088,128]{1,0:T(8,128)(2,1)}), bf16[3136,128]{1,0:T(8,128)(2,1)}) %reduce-scatter.4.cloned.1.call-update) | async-done | bytes 802832 | tf_op jit(solution)/shard_map/reduce_scatter | solution.py:770
  351.9 10.3 %mixgrad.1 = bf16[6272,128]{1,0:T(8,128)(2,1)} custom-call(s32[192]{0:T(256)} %multiply_add_fusion.1.row_ref, bf16[4096,512]{1,0:T(8,128)(2,1)} %get-tuple-element.52.norm_ref, bf16[4096,384]{1,0:T(8,128)(2,1)} %attend_back.1.bm_ref, bf16[512,384]{1,0:T(8,128)(2,1)} %get-tuple-element.54.mix_ref, f32[1,512]{1,0:T(1,128)} %get-tuple-element.79.gain_ref), custom_call_target="tpu_custom_call" | custom-call | tf_op jit(solution)/shard_map/mixgrad/pallas_call | solution.py:627
  362.8 5.3 %all-to-all-done.3.bm_ref = bf16[4,1024,384]{2,1,0:T(8,128)(2,1)S(1)} async-done(((bf16[4,1024,384]{2,1,0:T(8,128)(2,1)}), bf16[4,1024,384]{2,1,0:T(8,128)(2,1)S(1)}, u32[]{:S(2)}, u32[]{:S(2)}) %all-to-all-start.3) | async-done | bytes 3145760 | tf_op jit(solution)/shard_map/all_to_all | solution.py:699
  368.1 33.0 %reduce-scatter.6.cloned.1.call-done.part_ref.gb_ref = bf16[784,128]{1,0:T(8,128)(2,1)} async-done(((bf16[6272,128]{1,0:T(8,128)(2,1)}), bf16[784,128]{1,0:T(8,128)(2,1)}) %reduce-scatter.6.cloned.1.call-update) | async-done | bytes 200720 | tf_op jit(solution)/shard_map/reduce_scatter | solution.py:779
  401.1 7.0 %tail.1 = bf16[1040,512]{1,0:T(8,128)(2,1)} custom-call(s32[1]{0:T(128)} %bitcast.6.here_ref, bf16[4,1024,384]{2,1,0:T(8,128)(2,1)} %copy-done, bf16[4,512,384]{2,1,0:T(8,128)(2,1)} %get-tuple-element.50.mix_ref, bf16[4096,512]{1,0:T(8,128)(2,1)} %tok_ref.5, f32[1024,512]{1,0:T(8,128)} %get-tuple-element.51.res_ref, f32[1,512]{1,0:T(1,128)} %get-tuple-element.79.gain_ref, ...), custom_call_target="tpu_custom_call" | custom-call | tf_op jit(solution)/shard_map/tail/pallas_call | solution.py:668
  411.8 4.6 all-to-all-start.4
  416.4 22.8 %reduce-scatter.8.cloned.1.call-done.ga_ref = bf16[784,128]{1,0:T(8,128)(2,1)} async-done(((bf16[3136,128]{1,0:T(8,128)(2,1)}), bf16[784,128]{1,0:T(8,128)(2,1)}) %reduce-scatter.8.cloned.1.call-update) | async-done | bytes 200720 | tf_op jit(solution)/shard_map/reduce_scatter | solution.py:777
  439.2 28.3 %soap.1 = (f32[1,24,64,64]{3,2,1,0:T(8,128)}, f32[1,24,64,64]{3,2,1,0:T(8,128)}, f32[1,24,64,64]{3,2,1,0:T(8,128)}, f32[1,24,64,64]{3,2,1,0:T(8,128)}, f32[1,24,...) custom-call(bf16[784,128]{1,0:T(8,128)(2,1)} %reduce-scatter.8.cloned.1.call-done.ga_ref, ...), custom_call_target="tpu_custom_call" | custom-call | tf_op jit(solution)/shard_map/soap/pallas_call | solution.py:301
  467.5 38.3 %all-gather.13.cloned.1.call-done = bf16[2112,512]{1,0:T(8,128)(2,1)} async-done(((bf16[528,512]{1,0:T(8,128)(2,1)}), bf16[2112,512]{1,0:T(8,128)(2,1)}) %all-gather.13.cloned.1.call-update) | async-done | bytes 2162704 | tf_op jit(solution)/shard_map/all_gather | solution.py:704
  505.8 3.1 slice.69
  511.5 4.9 bitcast_convert_fusion
  (65 shorter events, 20.4 us)
Async XLA Ops:
  7.2 31.9 %all-gather.7.cloned.1.call-start = ((), (), s32[]{:S(2)}) async-start(), calls=%async_computation.8 | async-start | bytes 1806336 | tf_op jit(solution)/shard_map/all_gather | solution.py:743
  9.1 22.9 %copy-start.4 = (s32[1,4096]{1,0:T(1,128)S(1)}, s32[1,4096]{1,0:T(1,128)}, u32[]{:S(2)}) copy-start(s32[1,4096]{1,0:T(1,128)} %seg_ref.1) | copy-start | bytes 49156
  9.1 23.1 %copy-start.5 = (s32[1,4096]{1,0:T(1,128)S(1)}, s32[1,4096]{1,0:T(1,128)}, u32[]{:S(2)}) copy-start(s32[1,4096]{1,0:T(1,128)} %param.18) | copy-start | bytes 49156
  9.1 24.0 %copy-start.6 = (s32[192]{0:T(256)S(1)}, s32[192]{0:T(256)}, u32[]{:S(2)}) copy-start(s32[192]{0:T(256)} %param.19) | copy-start | bytes 2308
  10.0 115.0 %all-gather.9.cloned.1.call-start = ((), (), s32[]{:S(2)}) async-start(), calls=%async_computation.9 | async-start | bytes 7225344 | tf_op jit(solution)/shard_map/all_gather | solution.py:744
  94.2 30.8 %all-to-all-start = ((bf16[4,1024,128]{2,1,0:T(8,128)(2,1)}), bf16[4,1024,128]{2,1,0:T(8,128)(2,1)S(1)}, u32[]{:S(2)}, u32[]{:S(2)}) async-start(bf16[4,1024,128]{2,1,0:T(8,128)(2,1)} %bitcast.28), calls=%async_computation | async-start | bytes 2097152 | tf_op jit(solution)/shard_map/all_to_all | solution.py:699
  98.8 198.3 %all-gather.11.cloned.1.call-start = ((), (), s32[]{:S(2)}) async-start(), calls=%async_computation.13 | async-start | bytes 2621440 | tf_op jit(solution)/shard_map/all_gather | solution.py:704
  125.0 1.0 copy-start.2
  172.1 31.4 %copy-start.3 = (bf16[1024,512]{1,0:T(8,128)(2,1)S(1)}, bf16[1024,512]{1,0:T(8,128)(2,1)}, u32[]{:S(2)}) copy-start(bf16[1024,512]{1,0:T(8,128)(2,1)} %get-tuple-element.48) | copy-start | bytes 3145732
  204.4 147.5 %reduce-scatter.4.cloned.1.call-start = ((), (), s32[]{:S(2)}) async-start(), calls=%async_computation.10 | async-start | bytes 7225344 | tf_op jit(solution)/shard_map/reduce_scatter | solution.py:770
  206.4 85.6 %all-to-all-start.2 = ((bf16[4,512,512]{2,1,0:T(8,128)(2,1)}), bf16[4,512,512]{2,1,0:T(8,128)(2,1)S(1)}, u32[]{:S(2)}, u32[]{:S(2)}) async-start(bf16[4,512,512]{2,1,0:T(8,128)(2,1)} %broadcast_in_dim.33), calls=%async_computation.3 | async-start | bytes 4194304 | tf_op jit(solution)/shard_map/all_to_all | solution.py:705
  292.0 1.3 copy-start.1
  293.3 74.8 %all-to-all-start.3 = ((bf16[4,1024,384]{2,1,0:T(8,128)(2,1)}), bf16[4,1024,384]{2,1,0:T(8,128)(2,1)S(1)}, u32[]{:S(2)}, u32[]{:S(2)}) async-start(bf16[4,1024,384]{2,1,0:T(8,128)(2,1)} %bitcast.27), calls=%async_computation.4 | async-start | bytes 6291456 | tf_op jit(solution)/shard_map/all_to_all | solution.py:699
  297.0 104.1 %reduce-scatter.6.cloned.1.call-start = ((), (), s32[]{:S(2)}) async-start(), calls=%async_computation.11 | async-start | bytes 1806336 | tf_op jit(solution)/shard_map/reduce_scatter | solution.py:779
  362.2 77.0 %reduce-scatter.8.cloned.1.call-start = ((), (), s32[]{:S(2)}) async-start(), calls=%async_computation.12 | async-start | bytes 1003520 | tf_op jit(solution)/shard_map/reduce_scatter | solution.py:777
  362.8 143.0 %all-gather.13.cloned.1.call-start = ((), (), s32[]{:S(2)}) async-start(), calls=%async_computation.14 | async-start | bytes 2703360 | tf_op jit(solution)/shard_map/all_gather | solution.py:704
  368.1 33.0 %copy-start = (bf16[4,1024,384]{2,1,0:T(8,128)(2,1)}, bf16[4,1024,384]{2,1,0:T(8,128)(2,1)S(1)}, u32[]{:S(2)}) copy-start(bf16[4,1024,384]{2,1,0:T(8,128)(2,1)S(1)} %all-to-all-done.3.bm_ref) | copy-start | bytes 9437188
  408.2 1.3 slice-start
  411.8 97.8 %all-to-all-start.4 = ((bf16[4,512,512]{2,1,0:T(8,128)(2,1)}), bf16[4,512,512]{2,1,0:T(8,128)(2,1)S(1)}, u32[]{:S(2)}, u32[]{:S(2)}) async-start(bf16[4,512,512]{2,1,0:T(8,128)(2,1)} %broadcast_in_dim.34), calls=%async_computation.6 | async-start | bytes 4194304 | tf_op jit(solution)/shard_map/all_to_all | solution.py:705
  511.5 4.9 copy-start.7
  511.5 4.9 copy-start.8
  511.5 4.9 copy-start.9
  511.5 4.9 copy-start.10
Sparse Core Ops, SparseCore 0:
  10.5 28.5 all-gather.6
  40.9 46.0 all-gather.8
  204.5 82.1 all-gather.10
  290.5 61.3 reduce-scatter.3
  362.3 38.7 reduce-scatter.5
  403.4 35.7 reduce-scatter.7
  440.8 64.9 all-gather.12

commit v4 on v3

--- a/solution.py
+++ b/solution.py
@@ -310,6 +310,9 @@
     )(ga, gb, weights, first, second, average, stats, bases)
 
 
+MESH = pl.DeviceIdType.MESH
+
+
 def normalize(values):
     center = jnp.mean(values, axis=-1, keepdims=True)
     centered = values - center
@@ -585,105 +588,169 @@
     )(here, row_full, wire, att, tokens, cotangent, pad, gain_two)
 
 
-def mixgrad_kernel(heads, rows_dev, wide, gain_row, gains_dev, row_ref, norm_ref, bm_ref, mix_ref, gain_ref, grads_ref, acc_ref):
+def finish_kernel(shards, wide, gain_row, gains_dev, sel_ref, mix_ref, full_ref, gain_ref, res_ref, bm_ref, norm_ref, tok_ref,
+                  out_ref, part_ref, own_ref, normed_ref, tokens_ref, got_ref, acc_ref, blk_ref, grads_ref, sums_ref,
+                  local_sem, send_z, recv_z, send_w, recv_w):
     width = norm_ref.shape[1]
+    rows, cols = bm_ref.shape
+    own = rows // shards
+    hold = own // 2
     half = HD // 2
-    cols = 3 * heads
-
-    @pl.when(pl.program_id(0) == 0)
-    def _():
-        acc_ref[...] = jnp.zeros_like(acc_ref)
-
-    acc_ref[...] += tn(norm_ref[...], bm_ref[...])
-
-    @pl.when(pl.program_id(0) == pl.num_programs(0) - 1)
-    def _():
-        grads_ref[...] = jnp.zeros_like(grads_ref)
-
-        def scatter(r, _):
-            low = pl.multiple_of(r * HD, HD)
-            for c in range(cols):
-                cut = slice(c * HD, (c + 1) * HD)
-                value = jnp.concatenate([acc_ref[pl.ds(low, half), cut], acc_ref[pl.ds(low + half, half), cut]], axis=1)
-                grads_ref[pl.ds(pl.multiple_of(row_ref[r * cols + c], 16), half), :] = value.astype(BF)
+    grid_cols = cols // HD
+    blocks = width // HD * grid_cols
+    slots = gain_row // half
+    z = lax.axis_index("narrow")
+    w = lax.axis_index("wide")
+
+    barrier = pltpu.get_barrier_semaphore()
+    for d in range(1, shards):
+        pl.semaphore_signal(barrier, inc=1, device_id={"narrow": lax.rem(z + d, shards)}, device_id_type=MESH)
+    for d in range(1, wide):
+        pl.semaphore_signal(barrier, inc=1, device_id={"wide": lax.rem(w + d, wide)}, device_id_type=MESH)
+    pl.semaphore_wait(barrier, shards + wide - 2)
+
+    def to_peer(d, part, mine):
+        peer = lax.rem(z + d, shards)
+        slot = z if mine else peer
+        at = pl.multiple_of(peer * own + part * hold, hold)
+        return pltpu.make_async_remote_copy(
+            src_ref=bm_ref.at[pl.ds(at, hold), :],
+            dst_ref=got_ref.at[slot, pl.ds(part * hold, hold), :],
+            send_sem=send_z.at[d - 1, part],
+            recv_sem=recv_z.at[slot, part],
+            device_id={"narrow": peer},
+            device_id_type=MESH,
+        )
+
+    def to_owner(d, mine):
+        peer = lax.rem(w + d, wide)
+        slot = w if mine else peer
+        return pltpu.make_async_remote_copy(
+            src_ref=grads_ref.at[peer],
+            dst_ref=sums_ref.at[slot],
+            send_sem=send_w.at[d - 1],
+            recv_sem=recv_w.at[slot],
+            device_id={"wide": peer},
+            device_id_type=MESH,
+        )
+
+    for part in range(2):
+        for d in range(1, shards):
+            to_peer(d, part, True).start()
+    mine = pl.ds(pl.multiple_of(z * own, own), own)
+    copies = [
+        pltpu.make_async_copy(bm_ref, own_ref, local_sem.at[0]),
+        pltpu.make_async_copy(norm_ref, normed_ref, local_sem.at[1]),
+        pltpu.make_async_copy(tok_ref.at[mine, :], tokens_ref, local_sem.at[2]),
+        pltpu.make_async_copy(bm_ref.at[mine, :], got_ref.at[z], local_sem.at[3]),
+    ]
+    for copy in copies:
+        copy.start()
+    for copy in copies:
+        copy.wait()
+
+    acc_ref[...] = jnp.zeros_like(acc_ref)
+    tb = min(512, rows)
+
+    def add(i, _):
+        at = pl.ds(pl.multiple_of(i * tb, tb), tb)
+        acc_ref[...] += tn(normed_ref[at, :], own_ref[at, :])
+        return 0
+
+    lax.fori_loop(0, rows // tb, add, 0)
+    blk_ref[blocks] = jnp.zeros((half, LANES), BF)
+
+    def cut(r, _):
+        low = pl.multiple_of(r * HD, HD)
+        for c in range(grid_cols):
+            lanes = slice(c * HD, (c + 1) * HD)
+            value = jnp.concatenate([acc_ref[pl.ds(low, half), lanes], acc_ref[pl.ds(low + half, half), lanes]], axis=1)
+            blk_ref[r * grid_cols + c] = value.astype(BF)
+        return 0
+
+    lax.fori_loop(0, width // HD, cut, 0)
+    along = jnp.sum(acc_ref[...] * mix_ref[...].astype(F32), axis=1, keepdims=True)
+    line = jnp.broadcast_to(along, (width, LANES)).T[:16] / gain_ref[...]
+    top = lax.broadcasted_iota(jnp.int32, (16, LANES), 0) == 0
+    for v in range(wide):
+
+        def place(i, _, v=v):
+            grads_ref[v, pl.ds(pl.multiple_of(i * half, half), half), :] = blk_ref[sel_ref[v * slots + i]]
             return 0
 
-        lax.fori_loop(0, width // HD, scatter, 0)
-        along = jnp.sum(acc_ref[...] * mix_ref[...].astype(F32), axis=1, keepdims=True)
-        line = jnp.broadcast_to(along, (width, LANES)).T[:1] / gain_ref[...]
-        for w in range(wide):
-            piece = w * gains_dev // LANES
-            if piece < width // LANES:
-                at = w * rows_dev + gain_row
-                grads_ref[at : at + 1, :] = line[:, piece * LANES : (piece + 1) * LANES].astype(BF)
-
-
-def mixgrad(row_own, normed, bm, mix, gain_one, wire_shape, wide, rows_dev, gain_row, gains_dev):
-    rows, width = normed.shape
-    span = bm.shape[1] // 3
-    tb = min(512, rows)
-    full = lambda i, r: (0, 0)
-    blk = lambda i, r: (i, 0)
+        lax.fori_loop(0, slots, place, 0)
+        piece = v * gains_dev // LANES
+        if piece < width // LANES:
+            value = jnp.where(top, line[:, piece * LANES : (piece + 1) * LANES], 0.0).astype(BF)
+        else:
+            value = jnp.zeros((16, LANES), BF)
+        grads_ref[v, gain_row : gain_row + 16, :] = value
+    for d in range(1, wide):
+        to_owner(d, True).start()
+    part_ref[...] = grads_ref[w].astype(F32)
+
+    tile = min(256, hold)
+
+    def norm_rows(i, _):
+        at = pl.ds(pl.multiple_of(i * tile, tile), tile)
+        back = nt(got_ref[0, at, :], full_ref[0])
+        for n in range(1, shards):
+            back += nt(got_ref[n, at, :], full_ref[n])
+        xhat, scale = normalize(tokens_ref[at, :].astype(F32))
+        out_ref[at, :] = (res_ref[at, :] + norm_back(back * gain_ref[...], xhat, scale)).astype(BF)
+        return 0
+
+    for part in range(2):
+        for d in range(1, shards):
+            to_peer(d, part, False).wait_recv()
+        lax.fori_loop(part * hold // tile, (part + 1) * hold // tile, norm_rows, 0)
+    for d in range(1, wide):
+        to_owner(d, False).wait_recv()
+    for d in range(1, wide):
+        part_ref[...] += sums_ref[lax.rem(w + d, wide)].astype(F32)
+    out_ref[own:, :] = jnp.zeros((16, width), BF)
+    out_ref[own:, :LANES] = part_ref[gain_row : gain_row + 16, :].astype(BF)
+    for part in range(2):
+        for d in range(1, shards):
+            to_peer(d, part, True).wait_send()
+    for d in range(1, wide):
+        to_owner(d, True).wait_send()
+
+
+def finish(sel, mix, mix_full, gain_one, res, bm, normed, tokens, wide, rows_dev, gain_row, gains_dev):
+    shards = mix_full.shape[0]
+    rows, cols = bm.shape
+    width = normed.shape[1]
+    own = rows // shards
+    half = HD // 2
+    blocks = width // HD * (cols // HD)
+    vmem = pl.BlockSpec(memory_space=pltpu.VMEM)
+    smem = pl.BlockSpec(memory_space=pltpu.SMEM)
+    hbm = pl.BlockSpec(memory_space=pl.ANY)
+    dma = pltpu.SemaphoreType.DMA
     return pl.pallas_call(
-        functools.partial(mixgrad_kernel, span // HD, rows_dev, wide, gain_row, gains_dev),
-        grid_spec=pltpu.PrefetchScalarGridSpec(
-            num_scalar_prefetch=1,
-            grid=(rows // tb,),
-            in_specs=[
-                pl.BlockSpec((tb, width), blk),
-                pl.BlockSpec((tb, 3 * span), blk),
-                pl.BlockSpec((width, 3 * span), full),
-                pl.BlockSpec((1, width), full),
-            ],
-            out_specs=pl.BlockSpec(wire_shape, full),
-            scratch_shapes=[pltpu.VMEM((width, 3 * span), F32)],
-        ),
-        out_shape=jax.ShapeDtypeStruct(wire_shape, BF),
-        compiler_params=pltpu.CompilerParams(vmem_limit_bytes=60 << 20),
-        name="mixgrad",
-    )(row_own, normed, bm, mix, gain_one)
-
-
-def tail_kernel(shards, tb, gain_row, here_ref, bm_ref, mix_ref, tok_ref, res_ref, gain_ref, part_ref, out_ref):
-    back = nt(bm_ref[0], mix_ref[0])
-    for n in range(1, shards):
-        back += nt(bm_ref[n], mix_ref[n])
-    xhat, scale = normalize(tok_ref[...].astype(F32))
-    grad = res_ref[...] + norm_back(back * gain_ref[...], xhat, scale)
-    at = pl.multiple_of(pl.program_id(0) * tb, tb)
-    out_ref[pl.ds(at, tb), :] = grad.astype(BF)
-
-    @pl.when(pl.program_id(0) == pl.num_programs(0) - 1)
-    def _():
-        out_ref[-16:, :] = jnp.zeros((16, out_ref.shape[1]), BF)
-        out_ref[-16:, :LANES] = part_ref[gain_row : gain_row + 16, :]
-
-
-def tail(here, bm, mix, tokens, res, gain_one, part, gain_row):
-    shards, own, cols = bm.shape
-    width = tokens.shape[1]
-    tb = min(256, own)
-    steps = own // tb
-    full3 = lambda i, h: (0, 0, 0)
-    return pl.pallas_call(
-        functools.partial(tail_kernel, shards, tb, gain_row),
-        grid_spec=pltpu.PrefetchScalarGridSpec(
-            num_scalar_prefetch=1,
-            grid=(steps,),
-            in_specs=[
-                pl.BlockSpec((shards, tb, cols), lambda i, h: (0, i, 0)),
-                pl.BlockSpec(mix.shape, full3),
-                pl.BlockSpec((tb, width), lambda i, h: (h[0] * steps + i, 0)),
-                pl.BlockSpec((tb, width), lambda i, h: (i, 0)),
-                pl.BlockSpec((1, width), lambda i, h: (0, 0)),
-                pl.BlockSpec(part.shape, lambda i, h: (0, 0)),
-            ],
-            out_specs=pl.BlockSpec((own + 16, width), lambda i, h: (0, 0)),
-        ),
-        out_shape=jax.ShapeDtypeStruct((own + 16, width), BF),
-        compiler_params=pltpu.CompilerParams(vmem_limit_bytes=60 << 20),
-        name="tail",
-    )(here, bm, mix, tokens, res, gain_one, part)
+        functools.partial(finish_kernel, shards, wide, gain_row, gains_dev),
+        in_specs=[smem, vmem, vmem, vmem, vmem, hbm, hbm, hbm],
+        out_specs=[vmem, vmem],
+        out_shape=[jax.ShapeDtypeStruct((own + 16, width), BF), jax.ShapeDtypeStruct((rows_dev, LANES), F32)],
+        scratch_shapes=[
+            pltpu.VMEM((rows, cols), BF),
+            pltpu.VMEM((rows, width), BF),
+            pltpu.VMEM((own, width), BF),
+            pltpu.VMEM((shards, own, cols), BF),
+            pltpu.VMEM((width, cols), F32),
+            pltpu.VMEM((blocks + 1, half, LANES), BF),
+            pltpu.VMEM((wide, rows_dev, LANES), BF),
+            pltpu.VMEM((wide, rows_dev, LANES), BF),
+            dma((4,)),
+            dma((shards - 1, 2)),
+            dma((shards, 2)),
+            dma((wide - 1,)),
+            dma((wide,)),
+        ],
+        compiler_params=pltpu.CompilerParams(vmem_limit_bytes=60 << 20, collective_id=1, has_side_effects=True),
+        name="finish",
+    )(sel, mix, mix_full, gain_one, res, bm, normed, tokens)
 
 
 def adam_gains(grad, gain, first, second, average):
@@ -770,17 +837,16 @@
     part_a = lax.psum_scatter(grads, "wide", scatter_dimension=0, tiled=True)
     back_att = lax.all_to_all(back_own, "narrow", 0, 0).reshape(rows, span)
     out_own, back_att = lax.optimization_barrier((out_own, back_att))
-    output = spread(out_own, narrow, own).reshape(rows, width)
+    output = lax.all_to_all(jnp.broadcast_to(out_own, (narrow, own, width)), "narrow", 0, 0).reshape(rows, width)
     bm = attend_back(qb, ke, ve, back_att, attended, begin, end, block, block)
-    bm_own = to_shards(bm, narrow)
     bm, part_a, output = lax.optimization_barrier((bm, part_a, output))
     part_a = lax.psum_scatter(part_a, "narrow", scatter_dimension=0, tiled=True)
-    grads_mix = mixgrad(row_own, normed, bm, mix, gain_one, wire_own.shape, wide, rows_dev, gain_row, gains_dev)
-    part_b = lax.psum_scatter(grads_mix, "wide", scatter_dimension=0, tiled=True)
-    grad_own = tail(here_of, bm_own, mix_full, tokens, back_res, gain_one, part_b, gain_row)
+    sel = jnp.minimum(owner_order, width // size * 3 * heads)
+    grad_own, part_b = finish(
+        sel, mix, mix_full, gain_one, back_res, bm, normed, tokens, wide, rows_dev, gain_row, gains_dev
+    )
     grad_all = spread(grad_own, narrow, own)
     input_grad = grad_all[:, :own].reshape(rows, width).astype(F32)
-    part_a, part_b, _ = lax.optimization_barrier((part_a, part_b, grad_own))
     group = next(g for g in range(min(12, slots), 0, -1) if slots % g == 0)
     new_weight, new_first, new_second, new_average, new_stats, new_bases = soap(
         part_a, part_b, weights, first_moment, second_moment, average, stats, bases, group

time: 531 us -> 516 us (0.972)
  waiting for transfers between devices: 205 us -> 90.3 us
  Pallas kernels: 202 us -> 310 us
  blocking collectives: 53.3 us -> 43.3 us
    pallas_call x2 -> x1, Pallas kernels: 17.4 us -> 101 us  [finish(): pl.pallas_call(functools.partial(finish_kernel, shards, wide, gain_row, g...]
    reduce_scatter x1, waiting for transfers between devices: 49.5 us -> 0.01 us  [body(): part_a = lax.psum_scatter(grads, 'wide', scatter_dimension=0, tiled=True)]
    reduce_scatter x1 -> x0, waiting for transfers between devices: 33 us -> none  [body(): lax.psum_scatter(grads_mix, 'wide', scatter_dimension=0, tiled=True)]
    all_to_all x2 -> x1, waiting for transfers between devices: 24.8 us -> 0.01 us  [spread(): lax.all_to_all(jnp.broadcast_to(values[cut:own], (shards, own - cut, valu...]
    reduce_scatter x1, waiting for transfers between devices: 22.8 us -> 0.02 us  [body(): part_a = lax.psum_scatter(part_a, 'narrow', scatter_dimension=0, tiled=True)]
    all_to_all x0 -> x1, waiting for transfers between devices: none -> 19.2 us  [body(): lax.all_to_all(jnp.broadcast_to(out_own, (narrow, own, width)), 'narrow',...]
    all_to_all x2 -> x1, waiting for transfers between devices: 31.5 us -> 16.5 us  [to_shards(): lax.all_to_all(values.reshape(shards, rows // shards, cols), 'narrow', 0, 0)]
    pallas_call x1, Pallas kernels: 56.9 us -> 70.9 us  [attend_back(): pl.pallas_call(functools.partial(bwd_kernel, heads, bq, bk), grid_spec=pl...]
  transfers between devices with their start and end apart: 11 -> 8, of which waited for: 8 -> 4; matrix products, arithmetic and copies ran while one was open for 3% -> 3% of each run, Pallas kernels for 30% -> 52%
where the time goes in v4:
time: 516 us; the launch traced here: 512 us
  Pallas kernels  310 us (60%)
  waiting for transfers between devices  90.3 us (18%)
  blocking collectives  43.3 us (8%)
  starting transfers between devices  20.9 us (4%)
  local copies, waits for them, and re-layouts  17.1 us (3%)
  other arithmetic  15.4 us (3%)
  between operations  14.4 us (3%)
    pallas_call x1, Pallas kernels, finish(): pl.pallas_call(functools.partial(finish_kernel, shards, wide, gain_row, g...  101 us
    pallas_call x1, Pallas kernels, attend_back(): pl.pallas_call(functools.partial(bwd_kernel, heads, bq, bk), grid_spec=pl...  70.9 us
    all_gather x1, waiting for transfers between devices, spread(): lax.all_gather(jnp.concatenate([values[:cut], values[own:]], axis=0), 'na...  50.4 us
    pallas_call x1, Pallas kernels, attend(): pl.pallas_call(functools.partial(fwd_kernel, heads, bq, bk), grid_spec=pl...  48 us
    pallas_call x1, Pallas kernels, middle(): pl.pallas_call(functools.partial(middle_kernel, shards, span, units, rows...  46.1 us
    pallas_call x1, Pallas kernels, soap(): pl.pallas_call(functools.partial(soap_kernel, group), grid=(slots // grou...  28.6 us
    all_gather x1, blocking collectives, body(): lax.all_gather(wire, 'narrow', axis=0, tiled=True)  21.9 us
    all_to_all x1, blocking collectives, body(): back_att = lax.all_to_all(back_own, 'narrow', 0, 0).reshape(rows, span)  21.4 us
  transfers between devices with their start and end apart: 8, of which 4 were waited for; matrix products, arithmetic and copies ran while one was open for 3% of the time, Pallas kernels for 52%

profile of v4, /device:TPU:0, one launch (start us, length us, event | category | flops | bytes accessed | tf_op | source)
XLA Modules:
  0.0 511.7 jit_solution(16577850409438633662)
XLA Ops:
  7.9 1.2 convert_bitcast_fusion
  10.1 21.9 %all_gather.16 = bf16[3136,128]{1,0:T(8,128)(2,1)} all-gather(bf16[784,128]{1,0:T(8,128)(2,1)} %fusion.1), channel_id=1, replica_groups=mesh['wide'=8,'narrow'=4] {'narrow'}, dimensions={0}, use_global_device_ids=true | all-gather | bytes 1003520 | tf_op jit(solution)/shard_map/all_gather | solution.py:811
  34.9 4.1 all-gather.5.cloned.1.call-done.wire_ref
  40.4 15.3 %project.1 = (bf16[4096,512]{1,0:T(8,128)(2,1)}, bf16[2,4096,128]{2,1,0:T(8,128)(2,1)}, bf16[2,4096,128]{2,1,0:T(8,128)(2,1)}, bf16[2,4096,128]{2,1,0:T(8,128)(2...) custom-call(s32[192]{0:T(256)} %multiply_add_fusion.1.row_ref, ...), custom_call_target="tpu_custom_call" | custom-call | tf_op jit(solution)/shard_map/project/pallas_call | solution.py:411
  55.7 48.0 %attend.1 = (bf16[4096,128]{1,0:T(8,128)(2,1)}, bf16[2,4096,128]{2,1,0:T(8,128)(2,1)}) custom-call(s32[8]{0:T(128)} %get-tuple-element.79.lo_ref, s32[8]{0:T(128)} %get-tuple-element.78.hi_ref, bf16[2,4096,128]{2,1,0:T(8,128)(2,1)} %get-tuple-element.38.qe_ref, bf16[2,4096,128]{2,1,0:T(8,128)(2,1)} %get-tuple-element.39.ke_ref, ...), custom_call_target="tpu_custom_call" | custom-call | tf_op jit(solution)/shard_map/attend/pallas_call | solution.py:105
  103.7 4.6 all-to-all-start
  108.6 16.5 %all-to-all-done.att_ref = bf16[4,1024,128]{2,1,0:T(8,128)(2,1)S(1)} async-done(((bf16[4,1024,128]{2,1,0:T(8,128)(2,1)}), bf16[4,1024,128]{2,1,0:T(8,128)(2,1)S(1)}, u32[]{:S(2)}, u32[]{:S(2)}) %all-to-all-start) | async-done | bytes 1048608 | tf_op jit(solution)/shard_map/all_to_all | solution.py:766
  126.1 46.1 %middle.1 = (bf16[1024,512]{1,0:T(8,128)(2,1)}, f32[1024,512]{1,0:T(8,128)}, bf16[4,1024,128]{2,1,0:T(8,128)(2,1)}, bf16[25088,128]{1,0:T(8,128)(2,1)}, bf16[4,512,384]{2,1,0:T(8,128)(2,1)}) custom-call(s32[1]{0:T(128)} %bitcast.6.here_ref, s32[192]{0:T(256)} %get-tuple-element.70.row_ref, bf16[25088,128]{1,0:T(8,128)(2,1)} %all-gather.7.cloned.1.call-done.wire_ref, ...), custom_call_target="tpu_custom_call" | custom-call | tf_op jit(solution)/shard_map/middle/pallas_call | solution.py:549
  173.4 21.4 %all_to_all.20 = bf16[4,1024,128]{2,1,0:T(8,128)(2,1)} all-to-all(bf16[4,1024,128]{2,1,0:T(8,128)(2,1)S(1)} %copy-done.2), channel_id=1, replica_groups=mesh['wide'=8,'narrow'=4] {'narrow'}, dimensions={0} | all-to-all | bytes 2097152 | tf_op jit(solution)/shard_map/all_to_all | solution.py:838
  194.8 2.3 broadcast_in_dim.33
  197.1 4.9 all-to-all-start.2
  202.3 70.9 %attend_back.1.bm_ref = bf16[4096,384]{1,0:T(8,128)(2,1)} custom-call(s32[8]{0:T(128)} %get-tuple-element.79.lo_ref, s32[8]{0:T(128)} %get-tuple-element.78.hi_ref, bf16[2,4096,128]{2,1,0:T(8,128)(2,1)} %get-tuple-element.41.qb_ref, bf16[2,4096,128]{2,1,0:T(8,128)(2,1)} %get-tuple-element.39.ke_ref, bf16[2,4096,128]{2,1,0:T(8,128)(2,1)} %get-tuple-element.42.ve_ref, ...), custom_call_target="tpu_custom_call" | custom-call | tf_op jit(solution)/shard_map/attend_back/pallas_call | solution.py:197
  273.1 19.2 %all-to-all-done.2 = bf16[4,1024,512]{2,1,0:T(8,128)(2,1)} async-done(((bf16[4,1024,512]{2,1,0:T(8,128)(2,1)}), bf16[4,1024,512]{2,1,0:T(8,128)(2,1)}, u32[]{:S(2)}, u32[]{:S(2)}) %all-to-all-start.2) | async-done | bytes 4194336 | tf_op jit(solution)/shard_map/all_to_all | solution.py:840
  292.9 101.3 %finish.1 = (bf16[1040,512]{1,0:T(8,128)(2,1)}, f32[784,128]{1,0:T(8,128)}) custom-call(s32[192]{0:T(256)} %broadcast_minimum_fusion.sel_ref, bf16[512,384]{1,0:T(8,128)(2,1)} %get-tuple-element.50.mix_ref, bf16[4,512,384]{2,1,0:T(8,128)(2,1)} %get-tuple-element.51.full_ref, f32[1,512]{1,0:T(1,128)} %get-tuple-element.77.gain_ref, ...), custom_call_target="tpu_custom_call" | custom-call | tf_op jit(solution)/shard_map/finish/pallas_call | solution.py:731
  394.9 1.3 fusion.8
  397.0 1.5 broadcast_in_dim.34
  398.5 10.9 %all-to-all-start.3 = ((bf16[4,512,512]{2,1,0:T(8,128)(2,1)}), bf16[4,512,512]{2,1,0:T(8,128)(2,1)S(1)}, u32[]{:S(2)}, u32[]{:S(2)}) async-start(bf16[4,512,512]{2,1,0:T(8,128)(2,1)} %broadcast_in_dim.34), calls=%async_computation.4 | async-start | bytes 4194304 | tf_op jit(solution)/shard_map/all_to_all | solution.py:772
  409.4 28.6 %soap.1 = (f32[1,24,64,64]{3,2,1,0:T(8,128)}, f32[1,24,64,64]{3,2,1,0:T(8,128)}, f32[1,24,64,64]{3,2,1,0:T(8,128)}, f32[1,24,64,64]{3,2,1,0:T(8,128)}, f32[1,24,...) custom-call(bf16[784,128]{1,0:T(8,128)(2,1)} %reduce-scatter.5.cloned.1.call-done.ga_ref, ...), custom_call_target="tpu_custom_call" | custom-call | tf_op jit(solution)/shard_map/soap/pallas_call | solution.py:301
  438.1 50.4 %all-gather.9.cloned.1.call-done = bf16[2112,512]{1,0:T(8,128)(2,1)} async-done(((bf16[528,512]{1,0:T(8,128)(2,1)}), bf16[2112,512]{1,0:T(8,128)(2,1)}) %all-gather.9.cloned.1.call-update) | async-done | bytes 2162704 | tf_op jit(solution)/shard_map/all_gather | solution.py:771
  488.5 3.0 slice.59
  492.2 1.9 pad_maximum_fusion
  494.1 4.9 bitcast_convert_fusion
  499.0 1.2 add_multiply_fusion
  500.2 4.5 copy.32
  (53 shorter events, 11.5 us)
Async XLA Ops:
  7.2 31.9 %all-gather.5.cloned.1.call-start = ((), (), s32[]{:S(2)}) async-start(), calls=%async_computation.6 | async-start | bytes 1806336 | tf_op jit(solution)/shard_map/all_gather | solution.py:810
  9.1 22.9 %copy-start.3 = (s32[1,4096]{1,0:T(1,128)S(1)}, s32[1,4096]{1,0:T(1,128)}, u32[]{:S(2)}) copy-start(s32[1,4096]{1,0:T(1,128)} %seg_ref.1) | copy-start | bytes 49156
  9.1 23.1 %copy-start.4 = (s32[1,4096]{1,0:T(1,128)S(1)}, s32[1,4096]{1,0:T(1,128)}, u32[]{:S(2)}) copy-start(s32[1,4096]{1,0:T(1,128)} %param.18) | copy-start | bytes 49156
  9.1 24.0 %copy-start.5 = (s32[192]{0:T(256)S(1)}, s32[192]{0:T(256)}, u32[]{:S(2)}) copy-start(s32[192]{0:T(256)} %param.19) | copy-start | bytes 2308
  10.0 115.0 %all-gather.7.cloned.1.call-start = ((), (), s32[]{:S(2)}) async-start(), calls=%async_computation.7 | async-start | bytes 7225344 | tf_op jit(solution)/shard_map/all_gather | solution.py:811
  103.7 21.3 %all-to-all-start = ((bf16[4,1024,128]{2,1,0:T(8,128)(2,1)}), bf16[4,1024,128]{2,1,0:T(8,128)(2,1)S(1)}, u32[]{:S(2)}, u32[]{:S(2)}) async-start(bf16[4,1024,128]{2,1,0:T(8,128)(2,1)} %bitcast.29), calls=%async_computation | async-start | bytes 2097152 | tf_op jit(solution)/shard_map/all_to_all | solution.py:766
  108.4 183.9 %reduce-scatter.3.cloned.1.call-start = ((), (), s32[]{:S(2)}) async-start(), calls=%async_computation.8 | async-start | bytes 7225344 | tf_op jit(solution)/shard_map/reduce_scatter | solution.py:837
  125.0 1.1 copy-start
  172.2 1.2 copy-start.2
  172.2 22.6 %copy-start.1 = (bf16[1024,512]{1,0:T(8,128)(2,1)S(1)}, bf16[1024,512]{1,0:T(8,128)(2,1)}, u32[]{:S(2)}) copy-start(bf16[1024,512]{1,0:T(8,128)(2,1)} %get-tuple-element.48) | copy-start | bytes 3145732
  197.1 95.2 %all-to-all-start.2 = ((bf16[4,1024,512]{2,1,0:T(8,128)(2,1)}), bf16[4,1024,512]{2,1,0:T(8,128)(2,1)}, u32[]{:S(2)}, u32[]{:S(2)}) async-start(bf16[4,1024,512]{2,1,0:T(8,128)(2,1)} %broadcast_in_dim.33), calls=%async_computation.3 | async-start | bytes 8388608 | tf_op jit(solution)/shard_map/all_to_all | solution.py:840
  202.0 207.4 %reduce-scatter.5.cloned.1.call-start = ((), (), s32[]{:S(2)}) async-start(), calls=%async_computation.9 | async-start | bytes 1003520 | tf_op jit(solution)/shard_map/reduce_scatter | solution.py:843
  292.3 196.1 %all-gather.9.cloned.1.call-start = ((), (), s32[]{:S(2)}) async-start(), calls=%async_computation.10 | async-start | bytes 2703360 | tf_op jit(solution)/shard_map/all_gather | solution.py:771
  398.5 93.7 %all-to-all-start.3 = ((bf16[4,512,512]{2,1,0:T(8,128)(2,1)}), bf16[4,512,512]{2,1,0:T(8,128)(2,1)S(1)}, u32[]{:S(2)}, u32[]{:S(2)}) async-start(bf16[4,512,512]{2,1,0:T(8,128)(2,1)} %broadcast_in_dim.34), calls=%async_computation.4 | async-start | bytes 4194304 | tf_op jit(solution)/shard_map/all_to_all | solution.py:772
  494.1 4.9 copy-start.6
  494.1 4.9 copy-start.7
  494.1 4.9 copy-start.8
  494.1 4.9 copy-start.9
Sparse Core Ops, SparseCore 0:
  10.5 28.5 all-gather.4
  40.9 46.1 all-gather.6
  172.3 71.9 reduce-scatter.2
  292.4 65.9 reduce-scatter.4
  397.2 91.2 all-gather.8

commit v5 on v4

--- a/solution.py
+++ b/solution.py
@@ -227,43 +227,44 @@
     return lax.dot_general(a, b, ((dims[:1], dims[1:]), ((), ())), precision=highest, preferred_element_type=F32)
 
 
-def soap_kernel(group, ga_ref, gb_ref, w_ref, m1_ref, m2_ref, av_ref, st_ref, ba_ref,
-                nw_ref, n1_ref, n2_ref, na_ref, ns_ref, nb_ref, aug_ref):
+def soap_group(base, group, ga_ref, gb_ref, w_ref, m1_ref, m2_ref, av_ref, st_ref, ba_ref,
+               nw_ref, n1_ref, n2_ref, na_ref, ns_ref, nb_ref, aug_ref):
     size = w_ref.shape[-1]
     half = size // 2
     panel = 8
     every = range(group)
     grads, firsts = [], []
     for s in every:
-        wire = ga_ref[s * half : (s + 1) * half, :].astype(F32) + gb_ref[s * half : (s + 1) * half, :].astype(F32)
+        rows = slice((base + s) * half, (base + s + 1) * half)
+        wire = ga_ref[rows, :].astype(F32) + gb_ref[rows, :]
         grads.append(jnp.concatenate([wire[:, :size], wire[:, size:]], axis=0))
-        firsts.append(beta_one * m1_ref[0, s] + (1.0 - beta_one) * grads[s])
-        n1_ref[0, s] = firsts[s]
+        firsts.append(beta_one * m1_ref[0, base + s] + (1.0 - beta_one) * grads[s])
+        n1_ref[0, base + s] = firsts[s]
     sides = [(s, side) for s in every for side in range(2)]
     outers = [dot_f32(grads[s], grads[s], (1, 1) if side == 0 else (0, 0)) for s, side in sides]
-    both = [dot_f32(jnp.concatenate([grads[s], firsts[s]], axis=0), ba_ref[0, s, 1], (1, 0)) for s in every]
+    both = [dot_f32(jnp.concatenate([grads[s], firsts[s]], axis=0), ba_ref[0, base + s, 1], (1, 0)) for s in every]
     stats = []
     for (s, side), outer in zip(sides, outers):
-        stats.append(beta_two * st_ref[0, s, side] + (1.0 - beta_two) * outer)
-        ns_ref[0, s, side] = stats[-1]
-    pairs = [dot_f32(ba_ref[0, s, 0], jnp.concatenate([both[s][:size], both[s][size:]], axis=1), (0, 0)) for s in every]
-    mts = [dot_f32(ba_ref[0, s, side], stat, (0, 1)) for (s, side), stat in zip(sides, stats)]
+        stats.append(beta_two * st_ref[0, base + s, side] + (1.0 - beta_two) * outer)
+        ns_ref[0, base + s, side] = stats[-1]
+    pairs = [dot_f32(ba_ref[0, base + s, 0], jnp.concatenate([both[s][:size], both[s][size:]], axis=1), (0, 0)) for s in every]
+    mts = [dot_f32(ba_ref[0, base + s, side], stat, (0, 1)) for (s, side), stat in zip(sides, stats)]
     scaled = []
     for s in every:
         rotated, moment = pairs[s][:, :size], pairs[s][:, size:]
-        second = beta_two * m2_ref[0, s] + (1.0 - beta_two) * rotated * rotated
-        n2_ref[0, s] = second
+        second = beta_two * m2_ref[0, base + s] + (1.0 - beta_two) * rotated * rotated
+        n2_ref[0, base + s] = second
         scaled.append(moment / (jnp.sqrt(second) + step_eps))
     grams = [dot_f32(mt, mt, (1, 1)) for mt in mts]
-    inner = [dot_f32(scaled[s], ba_ref[0, s, 1], (1, 1)) for s in every]
+    inner = [dot_f32(scaled[s], ba_ref[0, base + s, 1], (1, 1)) for s in every]
     for m, (gram, mt) in enumerate(zip(grams, mts)):
         aug_ref[m] = jnp.concatenate([gram, mt], axis=1)
-    directions = [dot_f32(ba_ref[0, s, 0], inner[s], (1, 0)) for s in every]
+    directions = [dot_f32(ba_ref[0, base + s, 0], inner[s], (1, 0)) for s in every]
     for s in every:
-        weight = w_ref[0, s]
+        weight = w_ref[0, base + s]
         fresh = weight - step_rate * (directions[s] + weight_decay * weight)
-        nw_ref[0, s] = fresh
-        na_ref[0, s] = average_keep * av_ref[0, s] + (1.0 - average_keep) * fresh
+        nw_ref[0, base + s] = fresh
+        na_ref[0, base + s] = average_keep * av_ref[0, base + s] + (1.0 - average_keep) * fresh
     count = 2 * group
     row = lax.broadcasted_iota(jnp.int32, (count, panel, LANES), 1)
     for p in range(size // panel):
@@ -289,25 +290,7 @@
                 )
     for s in range(group):
         for side in range(2):
-            nb_ref[0, s, side] = aug_ref[2 * s + side][:, size:].T
-
-
-def soap(ga, gb, weights, first, second, average, stats, bases, group):
-    _, slots, size, _ = weights.shape
-    wire = pl.BlockSpec((group * size // 2, LANES), lambda i: (i, 0))
-    four = pl.BlockSpec((1, group, size, size), lambda i: (0, i, 0, 0))
-    five = pl.BlockSpec((1, group, 2, size, size), lambda i: (0, i, 0, 0, 0))
-    like = lambda a: jax.ShapeDtypeStruct(a.shape, a.dtype)
-    return pl.pallas_call(
-        functools.partial(soap_kernel, group),
-        grid=(slots // group,),
-        in_specs=[wire, wire, four, four, four, four, five, five],
-        out_specs=[four, four, four, four, five, five],
-        out_shape=[like(a) for a in (weights, first, second, average, stats, bases)],
-        scratch_shapes=[pltpu.VMEM((2 * group, size, LANES), F32)],
-        compiler_params=pltpu.CompilerParams(vmem_limit_bytes=60 << 20),
-        name="soap",
-    )(ga, gb, weights, first, second, average, stats, bases)
+            nb_ref[0, base + s, side] = aug_ref[2 * s + side][:, size:].T
 
 
 MESH = pl.DeviceIdType.MESH
@@ -588,13 +571,18 @@
     )(here, row_full, wire, att, tokens, cotangent, pad, gain_two)
 
 
-def finish_kernel(shards, wide, gain_row, gains_dev, sel_ref, mix_ref, full_ref, gain_ref, res_ref, bm_ref, norm_ref, tok_ref,
-                  out_ref, part_ref, own_ref, normed_ref, tokens_ref, got_ref, acc_ref, blk_ref, grads_ref, sums_ref,
-                  local_sem, send_z, recv_z, send_w, recv_w):
+PARTS = 4
+
+
+def finish_kernel(shards, wide, gain_row, gains_dev, group, sel_ref, mix_ref, full_ref, gain_ref, res_ref, bm_ref, norm_ref, tok_ref, *refs):
+    states, outs = refs[:7], refs[9:15]
+    grad_ref, line_ref = refs[7:9]
+    (own_ref, normed_ref, tokens_ref, got_ref, acc_ref, blk_ref, grads_ref, sums_ref, part_ref, aug_ref,
+     local_sem, send_z, recv_z, send_w, recv_w, send_a, recv_a, send_g, recv_g) = refs[15:]
     width = norm_ref.shape[1]
     rows, cols = bm_ref.shape
     own = rows // shards
-    hold = own // 2
+    hold = own // PARTS
     half = HD // 2
     grid_cols = cols // HD
     blocks = width // HD * grid_cols
@@ -634,7 +622,40 @@
             device_id_type=MESH,
         )
 
-    for part in range(2):
+    def hop_copy(c, part, step):
+        at = pl.ds(pl.multiple_of(c * own + part * hold, hold), hold)
+        return pltpu.make_async_remote_copy(
+            src_ref=grad_ref.at[at, :],
+            dst_ref=grad_ref.at[at, :],
+            send_sem=send_a.at[step, c, part],
+            recv_sem=recv_a.at[c, part],
+            device_id={"narrow": lax.rem(z + (1 if step == 0 else shards - 1), shards)},
+            device_id_type=MESH,
+        )
+
+    def pass_on(c, part, act):
+        for step, there in ((0, z < shards - 1), (1, z > 0)):
+            if c is None or step == c[0]:
+                chunk = z if c is None else c[1]
+                ok = there if c is None else there & c[2]
+
+                @pl.when(ok)
+                def _(chunk=chunk, step=step):
+                    act(hop_copy(chunk, part, step))
+
+    def line_to(d, mine):
+        peer = lax.rem(z + d, shards)
+        slot = z if mine else peer
+        return pltpu.make_async_remote_copy(
+            src_ref=line_ref.at[z],
+            dst_ref=line_ref.at[slot],
+            send_sem=send_g.at[d - 1],
+            recv_sem=recv_g.at[slot],
+            device_id={"narrow": peer},
+            device_id_type=MESH,
+        )
+
+    for part in range(PARTS):
         for d in range(1, shards):
             to_peer(d, part, True).start()
     mine = pl.ds(pl.multiple_of(z * own, own), own)
@@ -697,27 +718,59 @@
         for n in range(1, shards):
             back += nt(got_ref[n, at, :], full_ref[n])
         xhat, scale = normalize(tokens_ref[at, :].astype(F32))
-        out_ref[at, :] = (res_ref[at, :] + norm_back(back * gain_ref[...], xhat, scale)).astype(BF)
+        grad = res_ref[at, :] + norm_back(back * gain_ref[...], xhat, scale)
+        grad_ref[pl.ds(pl.multiple_of(z * own + i * tile, tile), tile), :] = grad.astype(BF)
         return 0
 
-    for part in range(2):
+    def norm_part(part):
         for d in range(1, shards):
             to_peer(d, part, False).wait_recv()
         lax.fori_loop(part * hold // tile, (part + 1) * hold // tile, norm_rows, 0)
+        pass_on(None, part, lambda copy: copy.start())
+
     for d in range(1, wide):
         to_owner(d, False).wait_recv()
     for d in range(1, wide):
         part_ref[...] += sums_ref[lax.rem(w + d, wide)].astype(F32)
-    out_ref[own:, :] = jnp.zeros((16, width), BF)
-    out_ref[own:, :LANES] = part_ref[gain_row : gain_row + 16, :].astype(BF)
-    for part in range(2):
+    line_ref[z] = part_ref[gain_row : gain_row + 16, :]
+    for d in range(1, shards):
+        line_to(d, True).start()
+    ready = 0
+    rounds = slots // group
+    for g in range(rounds):
+        soap_group(g * group, group, states[0], part_ref, *states[1:], *outs, aug_ref)
+        upto = PARTS * (g + 1) // rounds
+        while ready < upto:
+            norm_part(ready)
+            ready += 1
+    hops = [(s, part, step) for s in range(1, shards) for part in range(PARTS) for step in range(2)]
+    for s, part, step in hops:
+        chunk = z - s if step == 0 else z + s
+        there = chunk >= 0 if step == 0 else chunk < shards
+
+        @pl.when(there)
+        def _(chunk=chunk, part=part, step=step):
+            hop_copy(chunk, part, step).wait_recv()
+
+        pass_on((step, chunk, there), part, lambda copy: copy.start())
+    for d in range(1, shards):
+        line_to(d, False).wait_recv()
+    for part in range(PARTS):
+        pass_on(None, part, lambda copy: copy.wait_send())
+    for s, part, step in hops:
+        chunk = z - s if step == 0 else z + s
+        there = chunk >= 0 if step == 0 else chunk < shards
+        pass_on((step, chunk, there), part, lambda copy: copy.wait_send())
+    for d in range(1, shards):
+        line_to(d, True).wait_send()
+    for part in range(PARTS):
         for d in range(1, shards):
             to_peer(d, part, True).wait_send()
     for d in range(1, wide):
         to_owner(d, True).wait_send()
 
 
-def finish(sel, mix, mix_full, gain_one, res, bm, normed, tokens, wide, rows_dev, gain_row, gains_dev):
+def finish(sel, mix, mix_full, gain_one, res, bm, normed, tokens, states, group, wide, rows_dev, gain_row, gains_dev):
     shards = mix_full.shape[0]
     rows, cols = bm.shape
     width = normed.shape[1]
@@ -729,10 +782,11 @@
     hbm = pl.BlockSpec(memory_space=pl.ANY)
     dma = pltpu.SemaphoreType.DMA
     return pl.pallas_call(
-        functools.partial(finish_kernel, shards, wide, gain_row, gains_dev),
-        in_specs=[smem, vmem, vmem, vmem, vmem, hbm, hbm, hbm],
-        out_specs=[vmem, vmem],
-        out_shape=[jax.ShapeDtypeStruct((own + 16, width), BF), jax.ShapeDtypeStruct((rows_dev, LANES), F32)],
+        functools.partial(finish_kernel, shards, wide, gain_row, gains_dev, group),
+        in_specs=[smem, vmem, vmem, vmem, vmem, hbm, hbm, hbm] + [vmem] * 7,
+        out_specs=[vmem] * 8,
+        out_shape=[jax.ShapeDtypeStruct((rows, width), BF), jax.ShapeDtypeStruct((shards, 16, LANES), F32)]
+        + [jax.ShapeDtypeStruct(a.shape, a.dtype) for a in states[1:]],
         scratch_shapes=[
             pltpu.VMEM((rows, cols), BF),
             pltpu.VMEM((rows, width), BF),
@@ -742,15 +796,21 @@
             pltpu.VMEM((blocks + 1, half, LANES), BF),
             pltpu.VMEM((wide, rows_dev, LANES), BF),
             pltpu.VMEM((wide, rows_dev, LANES), BF),
+            pltpu.VMEM((rows_dev, LANES), F32),
+            pltpu.VMEM((2 * group, HD, LANES), F32),
             dma((4,)),
-            dma((shards - 1, 2)),
-            dma((shards, 2)),
+            dma((shards - 1, PARTS)),
+            dma((shards, PARTS)),
             dma((wide - 1,)),
             dma((wide,)),
+            dma((2, shards, PARTS)),
+            dma((shards, PARTS)),
+            dma((shards - 1,)),
+            dma((shards,)),
         ],
-        compiler_params=pltpu.CompilerParams(vmem_limit_bytes=60 << 20, collective_id=1, has_side_effects=True),
+        compiler_params=pltpu.CompilerParams(vmem_limit_bytes=62 << 20, collective_id=1, has_side_effects=True),
         name="finish",
-    )(sel, mix, mix_full, gain_one, res, bm, normed, tokens)
+    )(sel, mix, mix_full, gain_one, res, bm, normed, tokens, *states)
 
 
 def adam_gains(grad, gain, first, second, average):
@@ -764,13 +824,6 @@
 def to_shards(values, shards):
     rows, cols = values.shape
     return lax.all_to_all(values.reshape(shards, rows // shards, cols), "narrow", 0, 0)
-
-
-def spread(values, shards, own):
-    cut = own // 2
-    first = lax.all_gather(jnp.concatenate([values[:cut], values[own:]], axis=0), "narrow", axis=0, tiled=False)
-    rest = lax.all_to_all(jnp.broadcast_to(values[cut:own], (shards, own - cut, values.shape[1])), "narrow", 0, 0)
-    return jnp.concatenate([first[:, :cut], rest, first[:, cut:]], axis=1)
 
 
 def body(
@@ -834,24 +887,20 @@
     out_own, back_res, back_own, grads, mix_full = middle(
         here_of, row_full, wire_full, att_own, tokens, cotangent, pad, gain_two, wide, rows_dev, gain_row, gains_dev
     )
-    part_a = lax.psum_scatter(grads, "wide", scatter_dimension=0, tiled=True)
+    part_a = lax.psum_scatter(grads, ("wide", "narrow"), scatter_dimension=0, tiled=True)
     back_att = lax.all_to_all(back_own, "narrow", 0, 0).reshape(rows, span)
     out_own, back_att = lax.optimization_barrier((out_own, back_att))
     output = lax.all_to_all(jnp.broadcast_to(out_own, (narrow, own, width)), "narrow", 0, 0).reshape(rows, width)
     bm = attend_back(qb, ke, ve, back_att, attended, begin, end, block, block)
     bm, part_a, output = lax.optimization_barrier((bm, part_a, output))
-    part_a = lax.psum_scatter(part_a, "narrow", scatter_dimension=0, tiled=True)
     sel = jnp.minimum(owner_order, width // size * 3 * heads)
-    grad_own, part_b = finish(
-        sel, mix, mix_full, gain_one, back_res, bm, normed, tokens, wide, rows_dev, gain_row, gains_dev
+    group = next(g for g in range(min(12, slots), 0, -1) if slots % g == 0)
+    states = (part_a, weights, first_moment, second_moment, average, stats, bases)
+    grad_all, lines, new_weight, new_first, new_second, new_average, new_stats, new_bases = finish(
+        sel, mix, mix_full, gain_one, back_res, bm, normed, tokens, states, group, wide, rows_dev, gain_row, gains_dev
     )
-    grad_all = spread(grad_own, narrow, own)
-    input_grad = grad_all[:, :own].reshape(rows, width).astype(F32)
-    group = next(g for g in range(min(12, slots), 0, -1) if slots % g == 0)
-    new_weight, new_first, new_second, new_average, new_stats, new_bases = soap(
-        part_a, part_b, weights, first_moment, second_moment, average, stats, bases, group
-    )
-    line = part_a[gain_row].astype(F32) + jnp.sum(grad_all[:, own, :LANES].astype(F32), axis=0)
+    input_grad = grad_all.astype(F32)
+    line = part_a[gain_row].astype(F32) + jnp.sum(lines[:, 0], axis=0)
     offset = lax.axis_index("wide") * gains_dev % LANES
     own_gain = lax.dynamic_slice_in_dim(line, offset, gains_dev, 0)
     new_gains, gain_moment, gain_square, gain_mean = adam_gains(own_gain, gains, gain_first, gain_second, gain_average)

time: 516 us -> 596 us (1.16)
  waiting for transfers between devices: 90.3 us -> 151 us
  blocking collectives: 43.3 us -> 71.9 us
  starting transfers between devices: 20.9 us -> 10.4 us
    all_to_all x1, waiting for transfers between devices: 19.2 us -> 75.7 us  [body(): lax.all_to_all(jnp.broadcast_to(out_own, (narrow, own, width)), 'narrow',...]
    reduce_scatter x2 -> x1, waiting for transfers between devices: 0.02 us -> 53.2 us  [body(): lax.psum_scatter(grads, ('wide', 'narrow'), scatter_dimension=0, tiled=True)]
    all_gather x1 -> x0, waiting for transfers between devices: 50.4 us -> none  [spread(): lax.all_gather(jnp.concatenate([values[:cut], values[own:]], axis=0), 'na...]
    pallas_call x1, Pallas kernels: 101 us -> 132 us  [finish(): pl.pallas_call(functools.partial(finish_kernel, shards, wide, gain_row, g...]
    pallas_call x1 -> x0, Pallas kernels: 28.6 us -> none  [soap(): pl.pallas_call(functools.partial(soap_kernel, group), grid=(slots // grou...]
    all_to_all x1, blocking collectives: 21.4 us -> 50 us  [body(): back_att = lax.all_to_all(back_own, 'narrow', 0, 0).reshape(rows, span)]
    all_to_all x1 -> x0, starting transfers between devices: 10.9 us -> none  [spread(): lax.all_to_all(jnp.broadcast_to(values[cut:own], (shards, own - cut, valu...]
    unnamed x21 -> x39, local copies, waits for them, and re-layouts: 6.78 us -> 12.7 us
  transfers between devices with their start and end apart: 8 -> 5, of which waited for: 4 -> 4; matrix products, arithmetic and copies ran while one was open for 3% -> 1% of each run, Pallas kernels for 52% -> 23%
where the time goes in v5:
time: 596 us; the launch traced here: 591 us
  Pallas kernels  312 us (52%)
  waiting for transfers between devices  151 us (25%)
  blocking collectives  71.9 us (12%)
  local copies, waits for them, and re-layouts  16.5 us (3%)
  other arithmetic  14.7 us (2%)
  between operations  14.2 us (2%)
  starting transfers between devices  10.4 us (2%)
    pallas_call x1, Pallas kernels, finish(): pl.pallas_call(functools.partial(finish_kernel, shards, wide, gain_row, g...  132 us
    all_to_all x1, waiting for transfers between devices, body(): lax.all_to_all(jnp.broadcast_to(out_own, (narrow, own, width)), 'narrow',...  75.7 us
    pallas_call x1, Pallas kernels, attend_back(): pl.pallas_call(functools.partial(bwd_kernel, heads, bq, bk), grid_spec=pl...  70.9 us
    reduce_scatter x1, waiting for transfers between devices, body(): lax.psum_scatter(grads, ('wide', 'narrow'), scatter_dimension=0, tiled=True)  53.2 us
    all_to_all x1, blocking collectives, body(): back_att = lax.all_to_all(back_own, 'narrow', 0, 0).reshape(rows, span)  50 us
    pallas_call x1, Pallas kernels, attend(): pl.pallas_call(functools.partial(fwd_kernel, heads, bq, bk), grid_spec=pl...  48.1 us
    pallas_call x1, Pallas kernels, middle(): pl.pallas_call(functools.partial(middle_kernel, shards, span, units, rows...  46 us
    all_gather x1, blocking collectives, body(): lax.all_gather(wire, 'narrow', axis=0, tiled=True)  21.9 us
  transfers between devices with their start and end apart: 5, of which 4 were waited for; matrix products, arithmetic and copies ran while one was open for 1% of the time, Pallas kernels for 23%

profile of v5, /device:TPU:0, one launch (start us, length us, event | category | flops | bytes accessed | tf_op | source)
XLA Modules:
  0.0 591.5 jit_solution(12930926061772596258)
XLA Ops:
  7.9 1.2 convert_bitcast_fusion
  10.1 21.9 %all_gather.10 = bf16[3136,128]{1,0:T(8,128)(2,1)} all-gather(bf16[784,128]{1,0:T(8,128)(2,1)} %fusion.1), channel_id=1, replica_groups=mesh['wide'=8,'narrow'=4] {'narrow'}, dimensions={0}, use_global_device_ids=true | all-gather | bytes 1003520 | tf_op jit(solution)/shard_map/all_gather | solution.py:864
  34.9 4.1 all-gather.3.cloned.1.call-done.wire_ref
  40.4 15.3 %project.1 = (bf16[4096,512]{1,0:T(8,128)(2,1)}, bf16[2,4096,128]{2,1,0:T(8,128)(2,1)}, bf16[2,4096,128]{2,1,0:T(8,128)(2,1)}, bf16[2,4096,128]{2,1,0:T(8,128)(2...) custom-call(s32[192]{0:T(256)} %multiply_add_fusion.1.row_ref, ...), custom_call_target="tpu_custom_call" | custom-call | tf_op jit(solution)/shard_map/project/pallas_call | solution.py:394
  55.7 48.1 %attend.1 = (bf16[4096,128]{1,0:T(8,128)(2,1)}, bf16[2,4096,128]{2,1,0:T(8,128)(2,1)}) custom-call(s32[8]{0:T(128)} %get-tuple-element.77.lo_ref, s32[8]{0:T(128)} %get-tuple-element.76.hi_ref, bf16[2,4096,128]{2,1,0:T(8,128)(2,1)} %get-tuple-element.38.qe_ref, bf16[2,4096,128]{2,1,0:T(8,128)(2,1)} %get-tuple-element.39.ke_ref, ...), custom_call_target="tpu_custom_call" | custom-call | tf_op jit(solution)/shard_map/attend/pallas_call | solution.py:105
  103.7 4.7 all-to-all-start
  108.7 18.2 %all-to-all-done.att_ref = bf16[4,1024,128]{2,1,0:T(8,128)(2,1)S(1)} async-done(((bf16[4,1024,128]{2,1,0:T(8,128)(2,1)}), bf16[4,1024,128]{2,1,0:T(8,128)(2,1)S(1)}, u32[]{:S(2)}, u32[]{:S(2)}) %all-to-all-start) | async-done | bytes 1048608 | tf_op jit(solution)/shard_map/all_to_all | solution.py:826
  126.9 1.1 copy-done
  128.0 46.0 %middle.1 = (bf16[1024,512]{1,0:T(8,128)(2,1)}, f32[1024,512]{1,0:T(8,128)}, bf16[4,1024,128]{2,1,0:T(8,128)(2,1)}, bf16[25088,128]{1,0:T(8,128)(2,1)}, bf16[4,512,384]{2,1,0:T(8,128)(2,1)}) custom-call(s32[1]{0:T(128)} %bitcast.6.here_ref, s32[192]{0:T(256)} %get-tuple-element.70.row_ref, bf16[25088,128]{1,0:T(8,128)(2,1)} %all-gather.5.cloned.1.call-done.wire_ref, ...), custom_call_target="tpu_custom_call" | custom-call | tf_op jit(solution)/shard_map/middle/pallas_call | solution.py:532
  174.1 1.2 copy-done.4
  175.2 50.0 %all_to_all.15 = bf16[4,1024,128]{2,1,0:T(8,128)(2,1)} all-to-all(bf16[4,1024,128]{2,1,0:T(8,128)(2,1)S(1)} %copy-done.4), channel_id=1, replica_groups=mesh['wide'=8,'narrow'=4] {'narrow'}, dimensions={0} | all-to-all | bytes 2097152 | tf_op jit(solution)/shard_map/all_to_all | solution.py:891
  225.2 2.3 broadcast_in_dim.30
  227.5 5.4 all-to-all-start.2
  233.5 70.9 %attend_back.1.bm_ref = bf16[4096,384]{1,0:T(8,128)(2,1)} custom-call(s32[8]{0:T(128)} %get-tuple-element.77.lo_ref, s32[8]{0:T(128)} %get-tuple-element.76.hi_ref, bf16[2,4096,128]{2,1,0:T(8,128)(2,1)} %get-tuple-element.41.qb_ref, bf16[2,4096,128]{2,1,0:T(8,128)(2,1)} %get-tuple-element.39.ke_ref, bf16[2,4096,128]{2,1,0:T(8,128)(2,1)} %get-tuple-element.42.ve_ref, ...), custom_call_target="tpu_custom_call" | custom-call | tf_op jit(solution)/shard_map/attend_back/pallas_call | solution.py:197
  304.4 75.7 %all-to-all-done.2 = bf16[4,1024,512]{2,1,0:T(8,128)(2,1)} async-done(((bf16[4,1024,512]{2,1,0:T(8,128)(2,1)}), bf16[4,1024,512]{2,1,0:T(8,128)(2,1)}, u32[]{:S(2)}, u32[]{:S(2)}) %all-to-all-start.2) | async-done | bytes 4194336 | tf_op jit(solution)/shard_map/all_to_all | solution.py:893
  380.0 53.2 %reduce-scatter.2.cloned.1.call-done.refs_0_ = bf16[784,128]{1,0:T(8,128)(2,1)} async-done(((bf16[25088,128]{1,0:T(8,128)(2,1)}), bf16[784,128]{1,0:T(8,128)(2,1)}) %reduce-scatter.2.cloned.1.call-update) | async-done | bytes 200720 | tf_op jit(solution)/shard_map/reduce_scatter | solution.py:890
  433.3 132.2 %finish.1 = (bf16[4096,512]{1,0:T(8,128)(2,1)}, f32[4,16,128]{2,1,0:T(8,128)}, f32[1,24,64,64]{3,2,1,0:T(8,128)}, f32[1,24,64,64]{3,2,1,0:T(8,128)}, f32[1,24,64...) custom-call(s32[192]{0:T(256)} %broadcast_minimum_fusion.sel_ref, ...), custom_call_target="tpu_custom_call" | custom-call | tf_op jit(solution)/shard_map/finish/pallas_call | solution.py:784
  565.5 6.8 %convert_element_type.50 = f32[4096,512]{1,0:T(8,128)} convert(bf16[4096,512]{1,0:T(8,128)(2,1)} %get-tuple-element.56) | non-fusion elementwise | flops 2097152 | bytes 12582912 | tf_op jit(solution)/shard_map/convert_element_type | solution.py:902
  573.0 1.2 add_multiply_fusion
  574.2 4.6 copy.38
  578.8 0.9 copy.39
  579.7 0.9 copy.40
  582.4 1.1 copy.43
  583.5 1.1 copy.44
  (56 shorter events, 9.2 us)
Async XLA Ops:
  7.2 31.9 %all-gather.3.cloned.1.call-start = ((), (), s32[]{:S(2)}) async-start(), calls=%async_computation.4 | async-start | bytes 1806336 | tf_op jit(solution)/shard_map/all_gather | solution.py:863
  9.1 22.9 %copy-start.9 = (s32[1,4096]{1,0:T(1,128)S(1)}, s32[1,4096]{1,0:T(1,128)}, u32[]{:S(2)}) copy-start(s32[1,4096]{1,0:T(1,128)} %seg_ref.1) | copy-start | bytes 49156
  9.1 23.1 %copy-start.10 = (s32[1,4096]{1,0:T(1,128)S(1)}, s32[1,4096]{1,0:T(1,128)}, u32[]{:S(2)}) copy-start(s32[1,4096]{1,0:T(1,128)} %param.18) | copy-start | bytes 49156
  9.1 24.0 %copy-start.11 = (s32[192]{0:T(256)S(1)}, s32[192]{0:T(256)}, u32[]{:S(2)}) copy-start(s32[192]{0:T(256)} %param.19) | copy-start | bytes 2308
  10.0 116.9 %all-gather.5.cloned.1.call-start = ((), (), s32[]{:S(2)}) async-start(), calls=%async_computation.5 | async-start | bytes 7225344 | tf_op jit(solution)/shard_map/all_gather | solution.py:864
  103.7 23.1 %all-to-all-start = ((bf16[4,1024,128]{2,1,0:T(8,128)(2,1)}), bf16[4,1024,128]{2,1,0:T(8,128)(2,1)S(1)}, u32[]{:S(2)}, u32[]{:S(2)}) async-start(bf16[4,1024,128]{2,1,0:T(8,128)(2,1)} %bitcast.21), calls=%async_computation | async-start | bytes 2097152 | tf_op jit(solution)/shard_map/all_to_all | solution.py:826
  108.4 324.8 %reduce-scatter.2.cloned.1.call-start = ((), (), s32[]{:S(2)}) async-start(), calls=%async_computation.6 | async-start | bytes 6623232 | tf_op jit(solution)/shard_map/reduce_scatter | solution.py:890
  126.9 1.1 copy-start
  174.0 1.2 copy-start.4
  174.0 51.2 %copy-start.3 = (bf16[1024,512]{1,0:T(8,128)(2,1)S(1)}, bf16[1024,512]{1,0:T(8,128)(2,1)}, u32[]{:S(2)}) copy-start(bf16[1024,512]{1,0:T(8,128)(2,1)} %get-tuple-element.48) | copy-start | bytes 3145732
  227.5 152.5 %all-to-all-start.2 = ((bf16[4,1024,512]{2,1,0:T(8,128)(2,1)}), bf16[4,1024,512]{2,1,0:T(8,128)(2,1)}, u32[]{:S(2)}, u32[]{:S(2)}) async-start(bf16[4,1024,512]{2,1,0:T(8,128)(2,1)} %broadcast_in_dim.30), calls=%async_computation.3 | async-start | bytes 8388608 | tf_op jit(solution)/shard_map/all_to_all | solution.py:893
  565.4 7.6 %copy-start.12 = (f32[128]{0:T(128)S(1)}, f32[128]{0:T(128)}, u32[]{:S(2)}) copy-start(f32[128]{0:T(128)} %param.26) | copy-start | bytes 1540
  565.4 7.6 %copy-start.13 = (f32[128]{0:T(128)S(1)}, f32[128]{0:T(128)}, u32[]{:S(2)}) copy-start(f32[128]{0:T(128)} %param.29) | copy-start | bytes 1540
  565.4 7.6 %copy-start.14 = (f32[128]{0:T(128)S(1)}, f32[128]{0:T(128)}, u32[]{:S(2)}) copy-start(f32[128]{0:T(128)} %param.27) | copy-start | bytes 1540
  565.5 7.6 %copy-start.15 = (f32[128]{0:T(128)S(1)}, f32[128]{0:T(128)}, u32[]{:S(2)}) copy-start(f32[128]{0:T(128)} %param.28) | copy-start | bytes 1540
  574.2 4.6 copy-start.8
  574.2 5.5 copy-start.7
  578.8 1.8 copy-start.6
  578.8 2.7 copy-start.5
  579.7 2.7 copy-start.2
  581.5 2.0 copy-start.1
Sparse Core Ops, SparseCore 0:
  10.5 28.5 all-gather.2
  40.9 46.1 all-gather.4
  174.2 259.0 reduce-scatter.1

commit v6 on v5

--- a/solution.py
+++ b/solution.py
@@ -227,7 +227,7 @@
     return lax.dot_general(a, b, ((dims[:1], dims[1:]), ((), ())), precision=highest, preferred_element_type=F32)
 
 
-def soap_group(base, group, ga_ref, gb_ref, w_ref, m1_ref, m2_ref, av_ref, st_ref, ba_ref,
+def soap_group(base, group, gr_ref, w_ref, m1_ref, m2_ref, av_ref, st_ref, ba_ref,
                nw_ref, n1_ref, n2_ref, na_ref, ns_ref, nb_ref, aug_ref):
     size = w_ref.shape[-1]
     half = size // 2
@@ -236,7 +236,7 @@
     grads, firsts = [], []
     for s in every:
         rows = slice((base + s) * half, (base + s + 1) * half)
-        wire = ga_ref[rows, :].astype(F32) + gb_ref[rows, :]
+        wire = gr_ref[rows, :]
         grads.append(jnp.concatenate([wire[:, :size], wire[:, size:]], axis=0))
         firsts.append(beta_one * m1_ref[0, base + s] + (1.0 - beta_one) * grads[s])
         n1_ref[0, base + s] = firsts[s]
@@ -575,10 +575,10 @@
 
 
 def finish_kernel(shards, wide, gain_row, gains_dev, group, sel_ref, mix_ref, full_ref, gain_ref, res_ref, bm_ref, norm_ref, tok_ref, *refs):
-    states, outs = refs[:7], refs[9:15]
-    grad_ref, line_ref = refs[7:9]
-    (own_ref, normed_ref, tokens_ref, got_ref, acc_ref, blk_ref, grads_ref, sums_ref, part_ref, aug_ref,
-     local_sem, send_z, recv_z, send_w, recv_w, send_a, recv_a, send_g, recv_g) = refs[15:]
+    states, outs = refs[1:7], refs[9:15]
+    first_ref, grad_ref, line_ref = refs[0], refs[7], refs[8]
+    (own_ref, normed_ref, tokens_ref, got_ref, acc_ref, blk_ref, grads_ref, sums_ref, firsts_ref, part_ref, aug_ref,
+     local_sem, send_z, recv_z, send_w, recv_w, send_a, recv_a, send_g, recv_g, send_f, recv_f) = refs[15:]
     width = norm_ref.shape[1]
     rows, cols = bm_ref.shape
     own = rows // shards
@@ -655,6 +655,22 @@
             device_id_type=MESH,
         )
 
+    rows_dev = part_ref.shape[0]
+
+    def first_to(d, mine):
+        peer = lax.rem(z + d, shards)
+        slot = z if mine else peer
+        return pltpu.make_async_remote_copy(
+            src_ref=first_ref.at[pl.ds(pl.multiple_of(peer * rows_dev, 16), rows_dev), :],
+            dst_ref=firsts_ref.at[slot],
+            send_sem=send_f.at[d - 1],
+            recv_sem=recv_f.at[slot],
+            device_id={"narrow": peer},
+            device_id_type=MESH,
+        )
+
+    for d in range(1, shards):
+        first_to(d, True).start()
     for part in range(PARTS):
         for d in range(1, shards):
             to_peer(d, part, True).start()
@@ -664,6 +680,9 @@
         pltpu.make_async_copy(norm_ref, normed_ref, local_sem.at[1]),
         pltpu.make_async_copy(tok_ref.at[mine, :], tokens_ref, local_sem.at[2]),
         pltpu.make_async_copy(bm_ref.at[mine, :], got_ref.at[z], local_sem.at[3]),
+        pltpu.make_async_copy(
+            first_ref.at[pl.ds(pl.multiple_of(z * rows_dev, 16), rows_dev), :], firsts_ref.at[z], local_sem.at[4]
+        ),
     ]
     for copy in copies:
         copy.start()
@@ -735,10 +754,17 @@
     line_ref[z] = part_ref[gain_row : gain_row + 16, :]
     for d in range(1, shards):
         line_to(d, True).start()
+    for d in range(1, shards):
+        first_to(d, False).wait_recv()
+    total = firsts_ref[0].astype(F32)
+    for n in range(1, shards):
+        total += firsts_ref[n].astype(F32)
+    line_ref[shards] = total[gain_row : gain_row + 16, :]
+    part_ref[...] += total
     ready = 0
     rounds = slots // group
     for g in range(rounds):
-        soap_group(g * group, group, states[0], part_ref, *states[1:], *outs, aug_ref)
+        soap_group(g * group, group, part_ref, *states, *outs, aug_ref)
         upto = PARTS * (g + 1) // rounds
         while ready < upto:
             norm_part(ready)
@@ -763,6 +789,7 @@
         pass_on((step, chunk, there), part, lambda copy: copy.wait_send())
     for d in range(1, shards):
         line_to(d, True).wait_send()
+        first_to(d, True).wait_send()
     for part in range(PARTS):
         for d in range(1, shards):
             to_peer(d, part, True).wait_send()
@@ -783,9 +810,9 @@
     dma = pltpu.SemaphoreType.DMA
     return pl.pallas_call(
         functools.partial(finish_kernel, shards, wide, gain_row, gains_dev, group),
-        in_specs=[smem, vmem, vmem, vmem, vmem, hbm, hbm, hbm] + [vmem] * 7,
+        in_specs=[smem, vmem, vmem, vmem, vmem, hbm, hbm, hbm, hbm] + [vmem] * 6,
         out_specs=[vmem] * 8,
-        out_shape=[jax.ShapeDtypeStruct((rows, width), BF), jax.ShapeDtypeStruct((shards, 16, LANES), F32)]
+        out_shape=[jax.ShapeDtypeStruct((rows, width), BF), jax.ShapeDtypeStruct((shards + 1, 16, LANES), F32)]
         + [jax.ShapeDtypeStruct(a.shape, a.dtype) for a in states[1:]],
         scratch_shapes=[
             pltpu.VMEM((rows, cols), BF),
@@ -796,15 +823,18 @@
             pltpu.VMEM((blocks + 1, half, LANES), BF),
             pltpu.VMEM((wide, rows_dev, LANES), BF),
             pltpu.VMEM((wide, rows_dev, LANES), BF),
+            pltpu.VMEM((shards, rows_dev, LANES), BF),
             pltpu.VMEM((rows_dev, LANES), F32),
             pltpu.VMEM((2 * group, HD, LANES), F32),
-            dma((4,)),
+            dma((5,)),
             dma((shards - 1, PARTS)),
             dma((shards, PARTS)),
             dma((wide - 1,)),
             dma((wide,)),
             dma((2, shards, PARTS)),
             dma((shards, PARTS)),
+            dma((shards - 1,)),
+            dma((shards,)),
             dma((shards - 1,)),
             dma((shards,)),
         ],
@@ -887,7 +917,7 @@
     out_own, back_res, back_own, grads, mix_full = middle(
         here_of, row_full, wire_full, att_own, tokens, cotangent, pad, gain_two, wide, rows_dev, gain_row, gains_dev
     )
-    part_a = lax.psum_scatter(grads, ("wide", "narrow"), scatter_dimension=0, tiled=True)
+    part_a = lax.psum_scatter(grads, "wide", scatter_dimension=0, tiled=True)
     back_att = lax.all_to_all(back_own, "narrow", 0, 0).reshape(rows, span)
     out_own, back_att = lax.optimization_barrier((out_own, back_att))
     output = lax.all_to_all(jnp.broadcast_to(out_own, (narrow, own, width)), "narrow", 0, 0).reshape(rows, width)
@@ -900,7 +930,7 @@
         sel, mix, mix_full, gain_one, back_res, bm, normed, tokens, states, group, wide, rows_dev, gain_row, gains_dev
     )
     input_grad = grad_all.astype(F32)
-    line = part_a[gain_row].astype(F32) + jnp.sum(lines[:, 0], axis=0)
+    line = jnp.sum(lines[:, 0], axis=0)
     offset = lax.axis_index("wide") * gains_dev % LANES
     own_gain = lax.dynamic_slice_in_dim(line, offset, gains_dev, 0)
     new_gains, gain_moment, gain_square, gain_mean = adam_gains(own_gain, gains, gain_first, gain_second, gain_average)

time: 596 us -> 489 us (0.82)
  waiting for transfers between devices: 151 us -> 46.2 us
  Pallas kernels: 312 us -> 337 us
  blocking collectives: 71.9 us -> 50.3 us
    all_to_all x1, waiting for transfers between devices: 75.7 us -> 18.1 us  [body(): lax.all_to_all(jnp.broadcast_to(out_own, (narrow, own, width)), 'narrow',...]
    reduce_scatter x1, waiting for transfers between devices: 53.2 us -> 0.01 us  [body(): part_a = lax.psum_scatter(grads, 'wide', scatter_dimension=0, tiled=True)]
    all_to_all x1, blocking collectives: 50 us -> 28.4 us  [body(): back_att = lax.all_to_all(back_own, 'narrow', 0, 0).reshape(rows, span)]
    pallas_call x1, Pallas kernels: 132 us -> 152 us  [finish(): pl.pallas_call(functools.partial(finish_kernel, shards, wide, gain_row, g...]
  transfers between devices with their start and end apart: 5 -> 5, of which waited for: 4 -> 3; matrix products, arithmetic and copies ran while one was open for 1% -> 1% of each run, Pallas kernels for 23% -> 28%
where the time goes in v6:
time: 489 us; the launch traced here: 488 us
  Pallas kernels  337 us (69%)
  blocking collectives  50.3 us (10%)
  waiting for transfers between devices  46.2 us (9%)
  local copies, waits for them, and re-layouts  16.5 us (3%)
  between operations  14.2 us (3%)
  other arithmetic  14 us (3%)
  starting transfers between devices  10.4 us (2%)
    pallas_call x1, Pallas kernels, finish(): pl.pallas_call(functools.partial(finish_kernel, shards, wide, gain_row, g...  152 us
    pallas_call x1, Pallas kernels, attend_back(): pl.pallas_call(functools.partial(bwd_kernel, heads, bq, bk), grid_spec=pl...  73.6 us
    pallas_call x1, Pallas kernels, attend(): pl.pallas_call(functools.partial(fwd_kernel, heads, bq, bk), grid_spec=pl...  49.9 us
    pallas_call x1, Pallas kernels, middle(): pl.pallas_call(functools.partial(middle_kernel, shards, span, units, rows...  46.1 us
    all_to_all x1, blocking collectives, body(): back_att = lax.all_to_all(back_own, 'narrow', 0, 0).reshape(rows, span)  28.4 us
    all_to_all x1, waiting for transfers between devices, to_shards(): lax.all_to_all(values.reshape(shards, rows // shards, cols), 'narrow', 0, 0)  23.9 us
    all_gather x1, blocking collectives, body(): lax.all_gather(wire, 'narrow', axis=0, tiled=True)  21.9 us
    all_to_all x1, waiting for transfers between devices, body(): lax.all_to_all(jnp.broadcast_to(out_own, (narrow, own, width)), 'narrow',...  18.1 us
  transfers between devices with their start and end apart: 5, of which 3 were waited for; matrix products, arithmetic and copies ran while one was open for 1% of the time, Pallas kernels for 28%

profile of v6, /device:TPU:0, one launch (start us, length us, event | category | flops | bytes accessed | tf_op | source)
XLA Modules:
  0.0 488.2 jit_solution(11721573780200323986)
XLA Ops:
  7.9 1.2 convert_bitcast_fusion
  10.1 21.9 %all_gather.10 = bf16[3136,128]{1,0:T(8,128)(2,1)} all-gather(bf16[784,128]{1,0:T(8,128)(2,1)} %fusion.1), channel_id=1, replica_groups=mesh['wide'=8,'narrow'=4] {'narrow'}, dimensions={0}, use_global_device_ids=true | all-gather | bytes 1003520 | tf_op jit(solution)/shard_map/all_gather | solution.py:894
  34.9 4.1 all-gather.3.cloned.1.call-done.wire_ref
  40.4 15.3 %project.1 = (bf16[4096,512]{1,0:T(8,128)(2,1)}, bf16[2,4096,128]{2,1,0:T(8,128)(2,1)}, bf16[2,4096,128]{2,1,0:T(8,128)(2,1)}, bf16[2,4096,128]{2,1,0:T(8,128)(2...) custom-call(s32[192]{0:T(256)} %multiply_add_fusion.1.row_ref, ...), custom_call_target="tpu_custom_call" | custom-call | tf_op jit(solution)/shard_map/project/pallas_call | solution.py:394
  55.7 49.9 %attend.1 = (bf16[4096,128]{1,0:T(8,128)(2,1)}, bf16[2,4096,128]{2,1,0:T(8,128)(2,1)}) custom-call(s32[8]{0:T(128)} %get-tuple-element.77.lo_ref, s32[8]{0:T(128)} %get-tuple-element.76.hi_ref, bf16[2,4096,128]{2,1,0:T(8,128)(2,1)} %get-tuple-element.38.qe_ref, bf16[2,4096,128]{2,1,0:T(8,128)(2,1)} %get-tuple-element.39.ke_ref, ...), custom_call_target="tpu_custom_call" | custom-call | tf_op jit(solution)/shard_map/attend/pallas_call | solution.py:105
  105.6 4.7 all-to-all-start
  110.6 23.9 %all-to-all-done.att_ref = bf16[4,1024,128]{2,1,0:T(8,128)(2,1)S(1)} async-done(((bf16[4,1024,128]{2,1,0:T(8,128)(2,1)}), bf16[4,1024,128]{2,1,0:T(8,128)(2,1)S(1)}, u32[]{:S(2)}, u32[]{:S(2)}) %all-to-all-start) | async-done | bytes 1048608 | tf_op jit(solution)/shard_map/all_to_all | solution.py:856
  134.5 1.1 copy-done
  135.5 46.1 %middle.1 = (bf16[1024,512]{1,0:T(8,128)(2,1)}, f32[1024,512]{1,0:T(8,128)}, bf16[4,1024,128]{2,1,0:T(8,128)(2,1)}, bf16[25088,128]{1,0:T(8,128)(2,1)}, bf16[4,512,384]{2,1,0:T(8,128)(2,1)}) custom-call(s32[1]{0:T(128)} %bitcast.6.here_ref, s32[192]{0:T(256)} %get-tuple-element.70.row_ref, bf16[25088,128]{1,0:T(8,128)(2,1)} %all-gather.5.cloned.1.call-done.wire_ref, ...), custom_call_target="tpu_custom_call" | custom-call | tf_op jit(solution)/shard_map/middle/pallas_call | solution.py:532
  181.6 1.2 copy-done.4
  182.8 28.4 %all_to_all.15 = bf16[4,1024,128]{2,1,0:T(8,128)(2,1)} all-to-all(bf16[4,1024,128]{2,1,0:T(8,128)(2,1)S(1)} %copy-done.4), channel_id=1, replica_groups=mesh['wide'=8,'narrow'=4] {'narrow'}, dimensions={0} | all-to-all | bytes 2097152 | tf_op jit(solution)/shard_map/all_to_all | solution.py:921
  211.2 2.3 broadcast_in_dim.30
  213.5 5.4 %all-to-all-start.2 = ((bf16[4,1024,512]{2,1,0:T(8,128)(2,1)}), bf16[4,1024,512]{2,1,0:T(8,128)(2,1)}, u32[]{:S(2)}, u32[]{:S(2)}) async-start(bf16[4,1024,512]{2,1,0:T(8,128)(2,1)} %broadcast_in_dim.30), calls=%async_computation.3 | async-start | bytes 8388608 | tf_op jit(solution)/shard_map/all_to_all | solution.py:923
  219.5 73.6 %attend_back.1.bm_ref = bf16[4096,384]{1,0:T(8,128)(2,1)} custom-call(s32[8]{0:T(128)} %get-tuple-element.77.lo_ref, s32[8]{0:T(128)} %get-tuple-element.76.hi_ref, bf16[2,4096,128]{2,1,0:T(8,128)(2,1)} %get-tuple-element.41.qb_ref, bf16[2,4096,128]{2,1,0:T(8,128)(2,1)} %get-tuple-element.39.ke_ref, bf16[2,4096,128]{2,1,0:T(8,128)(2,1)} %get-tuple-element.42.ve_ref, ...), custom_call_target="tpu_custom_call" | custom-call | tf_op jit(solution)/shard_map/attend_back/pallas_call | solution.py:197
  293.1 18.1 %all-to-all-done.2 = bf16[4,1024,512]{2,1,0:T(8,128)(2,1)} async-done(((bf16[4,1024,512]{2,1,0:T(8,128)(2,1)}), bf16[4,1024,512]{2,1,0:T(8,128)(2,1)}, u32[]{:S(2)}, u32[]{:S(2)}) %all-to-all-start.2) | async-done | bytes 4194336 | tf_op jit(solution)/shard_map/all_to_all | solution.py:923
  311.2 151.6 %finish.1 = (bf16[4096,512]{1,0:T(8,128)(2,1)}, f32[5,16,128]{2,1,0:T(8,128)}, f32[1,24,64,64]{3,2,1,0:T(8,128)}, f32[1,24,64,64]{3,2,1,0:T(8,128)}, f32[1,24,64...) custom-call(s32[192]{0:T(256)} %broadcast_minimum_fusion.sel_ref, ...), custom_call_target="tpu_custom_call" | custom-call | tf_op jit(solution)/shard_map/finish/pallas_call | solution.py:811
  462.9 6.8 %convert_element_type.44 = f32[4096,512]{1,0:T(8,128)} convert(bf16[4096,512]{1,0:T(8,128)(2,1)} %get-tuple-element.56) | non-fusion elementwise | flops 2097152 | bytes 12582912 | tf_op jit(solution)/shard_map/convert_element_type | solution.py:932
  471.0 4.6 copy.38
  475.6 0.9 copy.39
  476.5 0.9 copy.40
  477.4 0.9 copy.41
  478.3 0.9 copy.42
  479.1 1.1 copy.43
  480.3 1.1 copy.44
  (56 shorter events, 8.0 us)
Async XLA Ops:
  7.2 31.9 %all-gather.3.cloned.1.call-start = ((), (), s32[]{:S(2)}) async-start(), calls=%async_computation.4 | async-start | bytes 1806336 | tf_op jit(solution)/shard_map/all_gather | solution.py:893
  9.1 22.9 %copy-start.9 = (s32[1,4096]{1,0:T(1,128)S(1)}, s32[1,4096]{1,0:T(1,128)}, u32[]{:S(2)}) copy-start(s32[1,4096]{1,0:T(1,128)} %seg_ref.1) | copy-start | bytes 49156
  9.1 23.1 %copy-start.10 = (s32[1,4096]{1,0:T(1,128)S(1)}, s32[1,4096]{1,0:T(1,128)}, u32[]{:S(2)}) copy-start(s32[1,4096]{1,0:T(1,128)} %param.18) | copy-start | bytes 49156
  9.1 24.0 %copy-start.11 = (s32[192]{0:T(256)S(1)}, s32[192]{0:T(256)}, u32[]{:S(2)}) copy-start(s32[192]{0:T(256)} %param.19) | copy-start | bytes 2308
  10.0 124.5 %all-gather.5.cloned.1.call-start = ((), (), s32[]{:S(2)}) async-start(), calls=%async_computation.5 | async-start | bytes 7225344 | tf_op jit(solution)/shard_map/all_gather | solution.py:894
  105.6 28.9 %all-to-all-start = ((bf16[4,1024,128]{2,1,0:T(8,128)(2,1)}), bf16[4,1024,128]{2,1,0:T(8,128)(2,1)S(1)}, u32[]{:S(2)}, u32[]{:S(2)}) async-start(bf16[4,1024,128]{2,1,0:T(8,128)(2,1)} %bitcast.12), calls=%async_computation | async-start | bytes 2097152 | tf_op jit(solution)/shard_map/all_to_all | solution.py:856
  110.3 200.9 %reduce-scatter.2.cloned.1.call-start = ((), (), s32[]{:S(2)}) async-start(), calls=%async_computation.6 | async-start | bytes 7225344 | tf_op jit(solution)/shard_map/reduce_scatter | solution.py:920
  134.5 1.1 copy-start
  181.6 1.2 copy-start.4
  181.6 29.5 %copy-start.3 = (bf16[1024,512]{1,0:T(8,128)(2,1)S(1)}, bf16[1024,512]{1,0:T(8,128)(2,1)}, u32[]{:S(2)}) copy-start(bf16[1024,512]{1,0:T(8,128)(2,1)} %get-tuple-element.48) | copy-start | bytes 3145732
  213.5 97.7 %all-to-all-start.2 = ((bf16[4,1024,512]{2,1,0:T(8,128)(2,1)}), bf16[4,1024,512]{2,1,0:T(8,128)(2,1)}, u32[]{:S(2)}, u32[]{:S(2)}) async-start(bf16[4,1024,512]{2,1,0:T(8,128)(2,1)} %broadcast_in_dim.30), calls=%async_computation.3 | async-start | bytes 8388608 | tf_op jit(solution)/shard_map/all_to_all | solution.py:923
  462.8 7.6 %copy-start.12 = (f32[128]{0:T(128)S(1)}, f32[128]{0:T(128)}, u32[]{:S(2)}) copy-start(f32[128]{0:T(128)} %param.26) | copy-start | bytes 1540
  462.9 7.6 %copy-start.13 = (f32[128]{0:T(128)S(1)}, f32[128]{0:T(128)}, u32[]{:S(2)}) copy-start(f32[128]{0:T(128)} %param.29) | copy-start | bytes 1540
  462.9 7.6 %copy-start.14 = (f32[128]{0:T(128)S(1)}, f32[128]{0:T(128)}, u32[]{:S(2)}) copy-start(f32[128]{0:T(128)} %param.27) | copy-start | bytes 1540
  462.9 7.6 %copy-start.15 = (f32[128]{0:T(128)S(1)}, f32[128]{0:T(128)}, u32[]{:S(2)}) copy-start(f32[128]{0:T(128)} %param.28) | copy-start | bytes 1540
  471.0 4.6 copy-start.8
  471.0 5.5 %copy-start.7 = (f32[1,24,64,64]{3,2,1,0:T(8,128)S(1)}, f32[1,24,64,64]{3,2,1,0:T(8,128)}, u32[]{:S(2)}) copy-start(f32[1,24,64,64]{3,2,1,0:T(8,128)} %get-tuple-element.93) | copy-start | bytes 1179652
  475.6 1.8 copy-start.6
  475.6 2.7 copy-start.5
  476.5 2.7 copy-start.2
  478.3 2.0 copy-start.1
Sparse Core Ops, SparseCore 0:
  10.5 28.5 all-gather.2
  40.9 46.1 all-gather.4
  181.8 59.6 reduce-scatter.1

commit v7 on v6

--- a/solution.py
+++ b/solution.py
@@ -426,149 +426,281 @@
     )(row_own, wire, tokens, seg, pad, gain_one)
 
 
-def middle_kernel(shards, span, units, rows_dev, wide, gain_row, gains_dev,
-                  here_ref, row_ref, wire_ref, att_ref, tok_ref, cot_ref, pad_ref, gain_ref,
-                  out_ref, res_ref, back_ref, grads_ref, mix_ref,
-                  wo_ref, wu_ref, wd_ref, go_ref, gu_ref, gd_ref, gg_ref):
-    width = tok_ref.shape[1]
+def middle_kernel(shards, span, units, wide, gain_row, gains_dev, inside,
+                  unit_ref, sel_ref, wire_ref, gain_ref, pad_ref, att_ref, tok_ref, cot_ref,
+                  outa_ref, outb_ref, res_ref, back_ref, grads_ref, mix_ref,
+                  tokens_ref, cots_ref, got_ref, give_ref, wo_ref, wu_ref, wd_ref, go_ref, gu_ref, gd_ref, gg_ref, blk_ref,
+                  local_sem, send_i, recv_i, send_b, recv_b, send_a, recv_a):
+    own, width = tokens_ref.shape
+    parts = recv_i.shape[1]
+    tb = own // parts
     half = HD // 2
+    rows_dev = grads_ref.shape[1]
+    z = lax.axis_index("narrow")
     kinds = (
         (mix_ref, None, width, 3 * span),
         (wo_ref, go_ref, span, width),
         (wu_ref, gu_ref, width, units),
         (wd_ref, gd_ref, units, width),
     )
-
-    @pl.when(pl.program_id(0) == 0)
-    def _():
-        base = 0
-        for ref, acc, rows, cols in kinds:
-            grid_cols = cols // HD
-
-            def fill(r, _, ref=ref, base=base, grid_cols=grid_cols):
+    mix_blocks = width // HD * (3 * span // HD)
+    per = blk_ref.shape[0] // shards
+
+    barrier = pltpu.get_barrier_semaphore()
+    for d in range(1, shards):
+        pl.semaphore_signal(barrier, inc=1, device_id={"narrow": lax.rem(z + d, shards)}, device_id_type=MESH)
+    pl.semaphore_wait(barrier, shards - 1)
+
+    def bring(d, t, mine):
+        peer = lax.rem(z + d, shards)
+        slot = z if mine else peer
+        return pltpu.make_async_remote_copy(
+            src_ref=att_ref.at[pl.ds(pl.multiple_of(peer * own + t * tb, tb), tb), :],
+            dst_ref=got_ref.at[slot, pl.ds(pl.multiple_of(t * tb, tb), tb), :],
+            send_sem=send_i.at[d - 1, t],
+            recv_sem=recv_i.at[slot, t],
+            device_id={"narrow": peer},
+            device_id_type=MESH,
+        )
+
+    def give(d, t, mine):
+        peer = lax.rem(z + d, shards)
+        slot = z if mine else peer
+        return pltpu.make_async_remote_copy(
+            src_ref=give_ref.at[peer, pl.ds(pl.multiple_of(t * tb, tb), tb), :],
+            dst_ref=back_ref.at[pl.ds(pl.multiple_of(slot * own + t * tb, tb), tb), :],
+            send_sem=send_b.at[d - 1, t],
+            recv_sem=recv_b.at[slot, t],
+            device_id={"narrow": peer},
+            device_id_type=MESH,
+        )
+
+    def hop_copy(c, t, step):
+        at = pl.ds(pl.multiple_of(t * tb, tb), tb)
+        return pltpu.make_async_remote_copy(
+            src_ref=outa_ref.at[c, at, :],
+            dst_ref=outa_ref.at[c, at, :],
+            send_sem=send_a.at[step, c, t],
+            recv_sem=recv_a.at[c, t],
+            device_id={"narrow": lax.rem(z + (1 if step == 0 else shards - 1), shards)},
+            device_id_type=MESH,
+        )
+
+    room = (z < shards - 1, z > 0)
+    for t in range(parts):
+        for d in range(1, shards):
+            bring(d, t, True).start()
+    mine = pl.ds(pl.multiple_of(z * own, own), own)
+    copies = [
+        pltpu.make_async_copy(att_ref.at[mine, :], got_ref.at[z], local_sem.at[0]),
+        pltpu.make_async_copy(tok_ref.at[mine, :], tokens_ref, local_sem.at[1]),
+        pltpu.make_async_copy(cot_ref.at[mine, :], cots_ref, local_sem.at[2]),
+    ]
+    for copy in copies:
+        copy.start()
+
+    base = 0
+    for ref, acc, rows, cols in kinds:
+        grid_cols = cols // HD
+
+        def fill(r, _, ref=ref, base=base, grid_cols=grid_cols):
+            low = pl.multiple_of(r * HD, HD)
+            for n in range(shards):
+                for c in range(grid_cols):
+                    unit = unit_ref[base + r * grid_cols + c] + n * (rows_dev // 16)
+                    t = jnp.concatenate([wire_ref[unit], wire_ref[unit + 1]], axis=0)
+                    for part in range(2):
+                        ref[n, pl.ds(low + part * half, half), c * HD : (c + 1) * HD] = t[:, part * HD : (part + 1) * HD]
+            return 0
+
+        lax.fori_loop(0, rows // HD, fill, 0)
+        base += rows // HD * grid_cols
+        if acc is not None:
+            acc[...] = jnp.zeros_like(acc)
+    gg_ref[...] = jnp.zeros_like(gg_ref)
+    for copy in copies:
+        copy.wait()
+
+    def block(t, _):
+        at = pl.ds(pl.multiple_of(t * tb, tb), tb)
+        for d in range(1, shards):
+            bring(d, t, False).wait_recv()
+        tokens = tokens_ref[at, :].astype(F32)
+        cot = cots_ref[at, :]
+        branch = nn(got_ref[0, at, :], wo_ref[0])
+        for n in range(1, shards):
+            branch += nn(got_ref[n, at, :], wo_ref[n])
+        residual = tokens + branch
+        xhat, scale = normalize(residual)
+        gain = gain_ref[...]
+        normed = (xhat * gain).astype(BF)
+        ups = [nn(normed, wu_ref[n]) for n in range(shards)]
+        downs = [nt(cot, wd_ref[n]) for n in range(shards)]
+        actives, back_ups = [], []
+        for n in range(shards):
+            value, slope = gelu_pair(ups[n])
+            actives.append(value.astype(BF))
+            back_ups.append((slope * downs[n]).astype(BF))
+        mlp = nn(actives[0], wd_ref[0])
+        back = nt(back_ups[0], wu_ref[0])
+        for n in range(1, shards):
+            mlp += nn(actives[n], wd_ref[n])
+            back += nt(back_ups[n], wu_ref[n])
+        out = (residual + mlp).astype(BF)
+
+        @pl.when(t < inside)
+        def _():
+            outa_ref[z, at, :] = out
+            for step in range(2):
+
+                @pl.when(room[step])
+                def _(step=step):
+                    hop_copy(z, t, step).start()
+
+        @pl.when(t >= inside)
+        def _():
+            outb_ref[pl.ds(pl.multiple_of((t - inside) * tb, tb), tb), :] = out
+
+        gg_ref[...] += jnp.sum(back * xhat, axis=0, keepdims=True)
+        back_res = cot.astype(F32) + norm_back(back * gain, xhat, scale)
+        res_ref[at, :] = back_res
+        branch_low = back_res.astype(BF)
+        line = pad_ref[:, pl.ds(pl.multiple_of(z * own + t * tb, LANES), tb)]
+        pad = jnp.broadcast_to(line, (8, tb)).T[:, :1]
+        for n in range(shards):
+            give_ref[n, at, :] = (nt(branch_low, wo_ref[n]) * pad).astype(BF)
+        for d in range(1, shards):
+            give(d, t, True).start()
+        for n in range(shards):
+            gd_ref[n] += tn(actives[n], cot)
+            gu_ref[n] += tn(normed, back_ups[n])
+            go_ref[n] += tn(got_ref[n, at, :], branch_low)
+        return 0
+
+    lax.fori_loop(0, parts, block, 0)
+    back_ref[mine, :] = give_ref[z]
+    base = 0
+    for ref, acc, rows, cols in kinds:
+        grid_cols = cols // HD
+        if acc is not None:
+
+            def cut(r, _, acc=acc, base=base, grid_cols=grid_cols):
                 low = pl.multiple_of(r * HD, HD)
                 for n in range(shards):
                     for c in range(grid_cols):
-                        t = block_rows(wire_ref, row_ref[base + r * grid_cols + c] + n * rows_dev, half)
-                        for part in range(2):
-                            ref[n, pl.ds(low + part * half, half), c * HD : (c + 1) * HD] = t[:, part * HD : (part + 1) * HD]
+                        lanes = slice(c * HD, (c + 1) * HD)
+                        value = jnp.concatenate([acc[n, pl.ds(low, half), lanes], acc[n, pl.ds(low + half, half), lanes]], axis=1)
+                        blk_ref[n * per + base - mix_blocks + r * grid_cols + c] = value.astype(BF)
                 return 0
 
-            lax.fori_loop(0, rows // HD, fill, 0)
-            base += rows // HD * grid_cols
-            if acc is not None:
-                acc[...] = jnp.zeros_like(acc)
-        gg_ref[...] = jnp.zeros_like(gg_ref)
-
-    tokens = tok_ref[...].astype(F32)
-    cot = cot_ref[...]
-    branch = nn(att_ref[0], wo_ref[0])
-    for n in range(1, shards):
-        branch += nn(att_ref[n], wo_ref[n])
-    residual = tokens + branch
-    xhat, scale = normalize(residual)
-    gain = gain_ref[...]
-    normed = (xhat * gain).astype(BF)
-    mlp = jnp.zeros_like(residual)
-    back = jnp.zeros_like(residual)
+            lax.fori_loop(0, rows // HD, cut, 0)
+        base += rows // HD * grid_cols
     for n in range(shards):
-        value, slope = gelu_pair(nn(normed, wu_ref[n]))
-        active = value.astype(BF)
-        mlp += nn(active, wd_ref[n])
-        gd_ref[n] += tn(active, cot)
-        back_up = (slope * nt(cot, wd_ref[n])).astype(BF)
-        gu_ref[n] += tn(normed, back_up)
-        back += nt(back_up, wu_ref[n])
-    out_ref[...] = (residual + mlp).astype(BF)
-    gg_ref[...] += jnp.sum(back * xhat, axis=0, keepdims=True)
-    back_res = cot.astype(F32) + norm_back(back * gain, xhat, scale)
-    res_ref[...] = back_res
-    branch_low = back_res.astype(BF)
-    pad = jnp.broadcast_to(pad_ref[...], (8, pad_ref.shape[1])).T[:, :1]
-    for n in range(shards):
-        go_ref[n] += tn(att_ref[n], branch_low)
-        back_ref[n] = (nt(branch_low, wo_ref[n]) * pad).astype(BF)
-
-    @pl.when(pl.program_id(0) == pl.num_programs(0) - 1)
-    def _():
-        grads_ref[...] = jnp.zeros_like(grads_ref)
-        base = 0
-        for ref, acc, rows, cols in kinds:
-            grid_cols = cols // HD
-            if acc is not None:
-
-                def scatter(r, _, acc=acc, base=base, grid_cols=grid_cols):
-                    low = pl.multiple_of(r * HD, HD)
-                    for n in range(shards):
-                        for c in range(grid_cols):
-                            at = row_ref[base + r * grid_cols + c] + n * rows_dev
-                            cut = slice(c * HD, (c + 1) * HD)
-                            value = jnp.concatenate([acc[n, pl.ds(low, half), cut], acc[n, pl.ds(low + half, half), cut]], axis=1)
-                            grads_ref[pl.ds(pl.multiple_of(at, 16), half), :] = value.astype(BF)
-                    return 0
-
-                lax.fori_loop(0, rows // HD, scatter, 0)
-            base += rows // HD * grid_cols
-        for w in range(wide):
-            piece = w * gains_dev // LANES - width // LANES
+        blk_ref[(n + 1) * per - 1] = jnp.zeros((half, LANES), BF)
+    slots = gain_row // half
+    top = lax.broadcasted_iota(jnp.int32, (16, LANES), 0) == 0
+
+    def place(v, _):
+        for n in range(shards):
+            for i in range(slots):
+                grads_ref[v * shards + n, i * half : (i + 1) * half, :] = blk_ref[sel_ref[v * slots + i] + n * per]
+        return 0
+
+    lax.fori_loop(0, wide, place, 0)
+    for v in range(wide):
+        piece = v * gains_dev // LANES - width // LANES
+        for n in range(shards):
             if piece >= 0:
-                for n in range(shards):
-                    at = (w * shards + n) * rows_dev + gain_row
-                    grads_ref[at : at + 1, :] = gg_ref[:, piece * LANES : (piece + 1) * LANES].astype(BF)
-
-
-def middle(here, row_full, wire, att, tokens, cotangent, pad, gain_two, wide, rows_dev, gain_row, gains_dev):
-    shards, own, span = att.shape
+                value = jnp.where(top, gg_ref[:, piece * LANES : (piece + 1) * LANES], 0.0).astype(BF)
+            else:
+                value = jnp.zeros((16, LANES), BF)
+            grads_ref[v * shards + n, gain_row:, :] = value
+
+    hops = [(s, t, step) for s in range(1, shards) for t in range(inside) for step in range(2)]
+    for s, t, step in hops:
+        chunk = z - s if step == 0 else z + s
+        there = chunk >= 0 if step == 0 else chunk < shards
+
+        @pl.when(there)
+        def _(chunk=chunk, t=t, step=step):
+            hop_copy(chunk, t, step).wait_recv()
+
+        @pl.when(there & room[step])
+        def _(chunk=chunk, t=t, step=step):
+            hop_copy(chunk, t, step).start()
+
+    for t in range(parts):
+        for d in range(1, shards):
+            give(d, t, False).wait_recv()
+    for t in range(parts):
+        for d in range(1, shards):
+            bring(d, t, True).wait_send()
+            give(d, t, True).wait_send()
+    for t in range(inside):
+        for step in range(2):
+
+            @pl.when(room[step])
+            def _(t=t, step=step):
+                hop_copy(z, t, step).wait_send()
+
+    for s, t, step in hops:
+        chunk = z - s if step == 0 else z + s
+        there = chunk >= 0 if step == 0 else chunk < shards
+
+        @pl.when(there & room[step])
+        def _(chunk=chunk, t=t, step=step):
+            hop_copy(chunk, t, step).wait_send()
+
+
+def middle(unit, sel, wire, gain_two, pad, att, tokens, cotangent, shards, wide, rows_dev, gain_row, gains_dev):
+    rows, span = att.shape
     width = tokens.shape[1]
     units = FF // shards
+    own = rows // shards
     tb = min(256, own)
-    steps = own // tb
-    full = lambda i, h, r: (0, 0)
-    full3 = lambda i, h, r: (0, 0, 0)
-    mine = lambda i, h, r: (h[0] * steps + i, 0)
-    blk = lambda i, h, r: (i, 0)
-    blk3 = lambda i, h, r: (0, i, 0)
-    once = pl.Buffered(1)
+    parts = own // tb
+    inside = parts // 2
+    blocks = unit.shape[0] - width // HD * (3 * span // HD)
+    vmem = pl.BlockSpec(memory_space=pltpu.VMEM)
+    smem = pl.BlockSpec(memory_space=pltpu.SMEM)
+    hbm = pl.BlockSpec(memory_space=pl.ANY)
+    dma = pltpu.SemaphoreType.DMA
     return pl.pallas_call(
-        functools.partial(middle_kernel, shards, span, units, rows_dev, wide, gain_row, gains_dev),
-        grid_spec=pltpu.PrefetchScalarGridSpec(
-            num_scalar_prefetch=2,
-            grid=(steps,),
-            in_specs=[
-                pl.BlockSpec(wire.shape, full, pipeline_mode=once),
-                pl.BlockSpec((shards, tb, span), blk3),
-                pl.BlockSpec((tb, width), mine),
-                pl.BlockSpec((tb, width), mine),
-                pl.BlockSpec((1, tb), lambda i, h, r: (0, h[0] * steps + i)),
-                pl.BlockSpec((1, width), full),
-            ],
-            out_specs=[
-                pl.BlockSpec((tb, width), blk),
-                pl.BlockSpec((tb, width), blk),
-                pl.BlockSpec((shards, tb, span), blk3),
-                pl.BlockSpec(wire.shape, full, pipeline_mode=once),
-                pl.BlockSpec((shards, width, 3 * span), full3, pipeline_mode=once),
-            ],
-            scratch_shapes=[
-                pltpu.VMEM((shards, span, width), BF),
-                pltpu.VMEM((shards, width, units), BF),
-                pltpu.VMEM((shards, units, width), BF),
-                pltpu.VMEM((shards, span, width), F32),
-                pltpu.VMEM((shards, width, units), F32),
-                pltpu.VMEM((shards, units, width), F32),
-                pltpu.VMEM((1, width), F32),
-            ],
-        ),
+        functools.partial(middle_kernel, shards, span, units, wide, gain_row, gains_dev, inside),
+        in_specs=[smem, smem, vmem, vmem, vmem, hbm, hbm, hbm],
+        out_specs=[vmem] * 6,
         out_shape=[
-            jax.ShapeDtypeStruct((own, width), BF),
+            jax.ShapeDtypeStruct((shards, inside * tb, width), BF),
+            jax.ShapeDtypeStruct((own - inside * tb, width), BF),
             jax.ShapeDtypeStruct((own, width), F32),
-            jax.ShapeDtypeStruct((shards, own, span), BF),
-            jax.ShapeDtypeStruct(wire.shape, BF),
+            jax.ShapeDtypeStruct((rows, span), BF),
+            jax.ShapeDtypeStruct((wide * shards, rows_dev, LANES), BF),
             jax.ShapeDtypeStruct((shards, width, 3 * span), BF),
         ],
-        compiler_params=pltpu.CompilerParams(vmem_limit_bytes=60 << 20),
+        scratch_shapes=[
+            pltpu.VMEM((own, width), BF),
+            pltpu.VMEM((own, width), BF),
+            pltpu.VMEM((shards, own, span), BF),
+            pltpu.VMEM((shards, own, span), BF),
+            pltpu.VMEM((shards, span, width), BF),
+            pltpu.VMEM((shards, width, units), BF),
+            pltpu.VMEM((shards, units, width), BF),
+            pltpu.VMEM((shards, span, width), F32),
+            pltpu.VMEM((shards, width, units), F32),
+            pltpu.VMEM((shards, units, width), F32),
+            pltpu.VMEM((1, width), F32),
+            pltpu.VMEM((shards * (blocks + 1), HD // 2, LANES), BF),
+            dma((3,)),
+            dma((shards - 1, parts)),
+            dma((shards, parts)),
+            dma((shards - 1, parts)),
+            dma((shards, parts)),
+            dma((2, shards, inside)),
+            dma((shards, inside)),
+        ],
+        compiler_params=pltpu.CompilerParams(vmem_limit_bytes=63 << 20, collective_id=2, has_side_effects=True),
         name="middle",
-    )(here, row_full, wire, att, tokens, cotangent, pad, gain_two)
+    )(unit, sel, wire, gain_two, pad, att, tokens, cotangent)
 
 
 PARTS = 4
@@ -851,11 +983,6 @@
     return (new_gain, new_first, new_second, new_average)
 
 
-def to_shards(values, shards):
-    rows, cols = values.shape
-    return lax.all_to_all(values.reshape(shards, rows // shards, cols), "narrow", 0, 0)
-
-
 def body(
     tokens,
     cotangent,
@@ -875,7 +1002,6 @@
 ):
     narrow = lax.axis_size("narrow")
     wide = lax.axis_size("wide")
-    here = lax.axis_index("narrow")
     heads = HEADS // narrow
     rows, width = tokens.shape
     span = heads * HD
@@ -898,7 +1024,6 @@
     device, place = slot_of // slots, slot_of % slots
     row_own = device * rows_dev + place * half
     row_full = device * (narrow * rows_dev) + place * half
-    here_of = jnp.full((1,), here, jnp.int32)
 
     gain_all = wire_own.reshape(wide, rows_dev, LANES)[:, gain_row, :gains_dev].astype(F32).reshape(1, 2 * width)
     gain_one, gain_two = gain_all[:, :width], gain_all[:, width:]
@@ -913,17 +1038,19 @@
 
     normed, qe, ke, ve, vt, mix = project(wire_own, row_own, tokens, seg, pad, gain_one, heads)
     attended, qb = attend(qe, ke, vt, pad, begin, end, block, block)
-    att_own = to_shards(attended, narrow)
-    out_own, back_res, back_own, grads, mix_full = middle(
-        here_of, row_full, wire_full, att_own, tokens, cotangent, pad, gain_two, wide, rows_dev, gain_row, gains_dev
+    unit = row_full // 16
+    mix_blocks = width // size * 3 * heads
+    sel_rest = jnp.where(owner_order >= mix_blocks, owner_order - mix_blocks, block_count - mix_blocks)
+    out_a, out_b, back_res, back_att, grads, mix_full = middle(
+        unit, sel_rest, wire_full.reshape(-1, 16, LANES), gain_two, pad, attended, tokens, cotangent,
+        narrow, wide, rows_dev, gain_row, gains_dev,
     )
-    part_a = lax.psum_scatter(grads, "wide", scatter_dimension=0, tiled=True)
-    back_att = lax.all_to_all(back_own, "narrow", 0, 0).reshape(rows, span)
-    out_own, back_att = lax.optimization_barrier((out_own, back_att))
-    output = lax.all_to_all(jnp.broadcast_to(out_own, (narrow, own, width)), "narrow", 0, 0).reshape(rows, width)
+    part_a = lax.psum_scatter(grads.reshape(-1, LANES), "wide", scatter_dimension=0, tiled=True)
+    out_b = lax.all_to_all(jnp.broadcast_to(out_b, (narrow, *out_b.shape)), "narrow", 0, 0)
     bm = attend_back(qb, ke, ve, back_att, attended, begin, end, block, block)
-    bm, part_a, output = lax.optimization_barrier((bm, part_a, output))
-    sel = jnp.minimum(owner_order, width // size * 3 * heads)
+    bm, part_a, out_b = lax.optimization_barrier((bm, part_a, out_b))
+    output = jnp.concatenate([out_a, out_b], axis=1).reshape(rows, width)
+    sel = jnp.minimum(owner_order, mix_blocks)
     group = next(g for g in range(min(12, slots), 0, -1) if slots % g == 0)
     states = (part_a, weights, first_moment, second_moment, average, stats, bases)
     grad_all, lines, new_weight, new_first, new_second, new_average, new_stats, new_bases = finish(

time: 489 us -> 457 us (0.935)
  Pallas kernels: 337 us -> 376 us
  waiting for transfers between devices: 46.2 us -> 9.16 us
  blocking collectives: 50.3 us -> 21.9 us
  local copies, waits for them, and re-layouts: 16.5 us -> 9.93 us
  starting transfers between devices: 10.4 us -> 5.05 us
    pallas_call x1, Pallas kernels: 46.1 us -> 89.1 us  [middle(): pl.pallas_call(functools.partial(middle_kernel, shards, span, units, wide...]
    all_to_all x2 -> x1, waiting for transfers between devices: 42 us -> 0.01 us  [body(): lax.all_to_all(jnp.broadcast_to(out_b, (narrow, *out_b.shape)), 'narrow',...]
    all_to_all x1 -> x0, blocking collectives: 28.4 us -> none  [body(): back_att = lax.all_to_all(back_own, 'narrow', 0, 0).reshape(rows, span)]
    pallas_call x1, Pallas kernels: 152 us -> 176 us  [finish(): pl.pallas_call(functools.partial(finish_kernel, shards, wide, gain_row, g...]
    pallas_call x1, Pallas kernels: 73.6 us -> 56.9 us  [attend_back(): pl.pallas_call(functools.partial(bwd_kernel, heads, bq, bk), grid_spec=pl...]
    pallas_call x1, Pallas kernels: 49.9 us -> 38.5 us  [attend(): pl.pallas_call(functools.partial(fwd_kernel, heads, bq, bk), grid_spec=pl...]
    unnamed x39 -> x36, local copies, waits for them, and re-layouts: 12.7 us -> 6.88 us
    reduce_scatter x1, waiting for transfers between devices: 0.01 us -> 5.58 us  [body(): lax.psum_scatter(grads.reshape(-1, LANES), 'wide', scatter_dimension=0, t...]
  transfers between devices with their start and end apart: 5 -> 4, of which waited for: 3 -> 2; matrix products, arithmetic and copies ran while one was open for 1% -> 1% of each run, Pallas kernels for 28% -> 24%
where the time goes in v7:
time: 457 us; the launch traced here: 454 us
  Pallas kernels  376 us (82%)
  blocking collectives  21.9 us (5%)
  other arithmetic  18.2 us (4%)
  between operations  14.4 us (3%)
  local copies, waits for them, and re-layouts  9.93 us (2%)
  waiting for transfers between devices  9.16 us (2%)
  starting transfers between devices  5.05 us (1%)
    pallas_call x1, Pallas kernels, finish(): pl.pallas_call(functools.partial(finish_kernel, shards, wide, gain_row, g...  176 us
    pallas_call x1, Pallas kernels, middle(): pl.pallas_call(functools.partial(middle_kernel, shards, span, units, wide...  89.1 us
    pallas_call x1, Pallas kernels, attend_back(): pl.pallas_call(functools.partial(bwd_kernel, heads, bq, bk), grid_spec=pl...  56.9 us
    pallas_call x1, Pallas kernels, attend(): pl.pallas_call(functools.partial(fwd_kernel, heads, bq, bk), grid_spec=pl...  38.5 us
    all_gather x1, blocking collectives, body(): lax.all_gather(wire, 'narrow', axis=0, tiled=True)  21.9 us
    pallas_call x1, Pallas kernels, project(): pl.pallas_call(functools.partial(project_kernel, heads, 0, 0), grid_spec=...  15.3 us
  transfers between devices with their start and end apart: 4, of which 2 were waited for; matrix products, arithmetic and copies ran while one was open for 1% of the time, Pallas kernels for 24%

profile of v7, /device:TPU:0, one launch (start us, length us, event | category | flops | bytes accessed | tf_op | source)
XLA Modules:
  0.0 454.2 jit_solution(14975961128143158946)
XLA Ops:
  7.2 0.7 convert_bitcast_fusion.1
  7.9 1.2 convert_bitcast_fusion
  9.3 0.7 fusion.1
  10.1 21.9 %all_gather.9 = bf16[3136,128]{1,0:T(8,128)(2,1)} all-gather(bf16[784,128]{1,0:T(8,128)(2,1)} %fusion.1), channel_id=1, replica_groups=mesh['wide'=8,'narrow'=4] {'narrow'}, dimensions={0}, use_global_device_ids=true | all-gather | bytes 1003520 | tf_op jit(solution)/shard_map/all_gather | solution.py:1020
  35.6 3.5 all-gather.5.cloned.1.call-done.wire_ref
  39.1 0.7 slice.34
  40.4 15.3 %project.1 = (bf16[4096,512]{1,0:T(8,128)(2,1)}, bf16[2,4096,128]{2,1,0:T(8,128)(2,1)}, bf16[2,4096,128]{2,1,0:T(8,128)(2,1)}, bf16[2,4096,128]{2,1,0:T(8,128)(2...) custom-call(s32[192]{0:T(256)} %multiply_add_fusion.row_ref, ...), custom_call_target="tpu_custom_call" | custom-call | tf_op jit(solution)/shard_map/project/pallas_call | solution.py:394
  55.7 38.5 %attend.1 = (bf16[4096,128]{1,0:T(8,128)(2,1)}, bf16[2,4096,128]{2,1,0:T(8,128)(2,1)}) custom-call(s32[8]{0:T(128)} %get-tuple-element.77.lo_ref, s32[8]{0:T(128)} %get-tuple-element.76.hi_ref, bf16[2,4096,128]{2,1,0:T(8,128)(2,1)} %get-tuple-element.37.qe_ref, bf16[2,4096,128]{2,1,0:T(8,128)(2,1)} %get-tuple-element.38.ke_ref, ...), custom_call_target="tpu_custom_call" | custom-call | tf_op jit(solution)/shard_map/attend/pallas_call | solution.py:105
  94.3 89.1 %middle.1 = (bf16[4,512,512]{2,1,0:T(8,128)(2,1)}, bf16[512,512]{1,0:T(8,128)(2,1)}, f32[1024,512]{1,0:T(8,128)}, bf16[4096,128]{1,0:T(8,128)(2,1)}, bf16[32,784...) custom-call(s32[192]{0:T(256)} %get-tuple-element.68.unit_ref, s32[192]{0:T(256)} %get-tuple-element.75.sel_ref, ...), custom_call_target="tpu_custom_call" | custom-call | tf_op jit(solution)/shard_map/middle/pallas_call | solution.py:668
  183.4 1.0 copy-done.7
  184.4 1.5 broadcast_in_dim.31
  185.9 4.9 %all-to-all-start = ((bf16[4,512,512]{2,1,0:T(8,128)(2,1)}), bf16[4,512,512]{2,1,0:T(8,128)(2,1)}, u32[]{:S(2)}, u32[]{:S(2)}) async-start(bf16[4,512,512]{2,1,0:T(8,128)(2,1)} %broadcast_in_dim.31), calls=%async_computation.1 | async-start | bytes 4194304 | tf_op jit(solution)/shard_map/all_to_all | solution.py:1049
  190.9 56.9 %attend_back.1.bm_ref = bf16[4096,384]{1,0:T(8,128)(2,1)} custom-call(s32[8]{0:T(128)} %get-tuple-element.77.lo_ref, s32[8]{0:T(128)} %get-tuple-element.76.hi_ref, bf16[2,4096,128]{2,1,0:T(8,128)(2,1)} %get-tuple-element.42.qb_ref, bf16[2,4096,128]{2,1,0:T(8,128)(2,1)} %get-tuple-element.38.ke_ref, bf16[2,4096,128]{2,1,0:T(8,128)(2,1)} %get-tuple-element.43.ve_ref, ...), custom_call_target="tpu_custom_call" | custom-call | tf_op jit(solution)/shard_map/attend_back/pallas_call | solution.py:197
  247.8 5.6 %reduce-scatter.2.cloned.1.call-done.refs_0_ = bf16[3136,128]{1,0:T(8,128)(2,1)} async-done(((bf16[25088,128]{1,0:T(8,128)(2,1)}), bf16[3136,128]{1,0:T(8,128)(2,1)}) %reduce-scatter.2.cloned.1.call-update) | async-done | bytes 802832 | tf_op jit(solution)/shard_map/reduce_scatter | solution.py:1048
  253.4 175.8 %finish.1 = (bf16[4096,512]{1,0:T(8,128)(2,1)}, f32[5,16,128]{2,1,0:T(8,128)}, f32[1,24,64,64]{3,2,1,0:T(8,128)}, f32[1,24,64,64]{3,2,1,0:T(8,128)}, f32[1,24,64...) custom-call(s32[192]{0:T(256)} %get-tuple-element.74.sel_ref, ...), custom_call_target="tpu_custom_call" | custom-call | tf_op jit(solution)/shard_map/finish/pallas_call | solution.py:943
  429.2 0.7 slice_reduce_fusion
  429.9 6.9 %convert_element_type.44 = f32[4096,512]{1,0:T(8,128)} convert(bf16[4096,512]{1,0:T(8,128)(2,1)} %get-tuple-element.54) | non-fusion elementwise | flops 2097152 | bytes 12582912 | tf_op jit(solution)/shard_map/convert_element_type | solution.py:1059
  436.9 4.0 pad_maximum_fusion
  441.4 0.9 copy.37
  442.3 0.9 copy.38
  443.2 0.9 copy.39
  444.1 0.9 copy.40
  445.0 1.1 copy.41
  446.1 1.1 copy.42
  (51 shorter events, 5.0 us)
Async XLA Ops:
  7.2 31.9 %all-gather.5.cloned.1.call-start = ((), (), s32[]{:S(2)}) async-start(), calls=%async_computation.3 | async-start | bytes 1806336 | tf_op jit(solution)/shard_map/all_gather | solution.py:1019
  9.1 23.0 %copy-start.8 = (s32[1,4096]{1,0:T(1,128)S(1)}, s32[1,4096]{1,0:T(1,128)}, u32[]{:S(2)}) copy-start(s32[1,4096]{1,0:T(1,128)} %seg_ref.1) | copy-start | bytes 49156
  9.1 23.2 %copy-start.9 = (s32[1,4096]{1,0:T(1,128)S(1)}, s32[1,4096]{1,0:T(1,128)}, u32[]{:S(2)}) copy-start(s32[1,4096]{1,0:T(1,128)} %param.18) | copy-start | bytes 49156
  9.1 24.0 %copy-start.10 = (s32[192]{0:T(256)S(1)}, s32[192]{0:T(256)}, u32[]{:S(2)}) copy-start(s32[192]{0:T(256)} %param.19) | copy-start | bytes 2308
  10.0 84.3 %all-gather.3.cloned.1.call-start = ((), (), s32[]{:S(2)}) async-start(), calls=%async_computation.2 | async-start | bytes 7225344 | tf_op jit(solution)/shard_map/all_gather | solution.py:1020
  32.0 221.4 %reduce-scatter.2.cloned.1.call-start = ((), (), s32[]{:S(2)}) async-start(), calls=%async_computation.4 | async-start | bytes 7225344 | tf_op jit(solution)/shard_map/reduce_scatter | solution.py:1048
  183.4 1.0 copy-start.7
  185.9 61.9 %all-to-all-start = ((bf16[4,512,512]{2,1,0:T(8,128)(2,1)}), bf16[4,512,512]{2,1,0:T(8,128)(2,1)}, u32[]{:S(2)}, u32[]{:S(2)}) async-start(bf16[4,512,512]{2,1,0:T(8,128)(2,1)} %broadcast_in_dim.31), calls=%async_computation.1 | async-start | bytes 4194304 | tf_op jit(solution)/shard_map/all_to_all | solution.py:1049
  429.9 6.9 %copy-start = (bf16[4,512,512]{2,1,0:T(8,128)(2,1)S(1)}, bf16[4,512,512]{2,1,0:T(8,128)(2,1)}, u32[]{:S(2)}) copy-start(bf16[4,512,512]{2,1,0:T(8,128)(2,1)} %get-tuple-element.41) | copy-start | bytes 6291460
  436.9 4.0 copy-start.11
  436.9 4.0 copy-start.12
  436.9 4.0 copy-start.13
  436.9 4.0 copy-start.14
  436.9 4.5 %copy-start.6 = (f32[1,24,64,64]{3,2,1,0:T(8,128)S(1)}, f32[1,24,64,64]{3,2,1,0:T(8,128)}, u32[]{:S(2)}) copy-start(f32[1,24,64,64]{3,2,1,0:T(8,128)} %get-tuple-element.92) | copy-start | bytes 1179652
  440.9 1.4 copy-start.5
  440.9 2.3 copy-start.4
  441.4 2.7 copy-start.3
  442.3 2.7 copy-start.2
  444.1 2.0 copy-start.1
Sparse Core Ops, SparseCore 0:
  10.5 28.5 all-gather.4
  41.0 46.0 all-gather.2
  183.5 69.8 reduce-scatter.1

commit v8 on v7

--- a/solution.py
+++ b/solution.py
@@ -57,6 +57,26 @@
 
 
 VT = 80
+UNIT = 256
+
+
+def in_steps(begin, end, block, step):
+    per = block // UNIT
+    count = end - begin
+    whole = count // per
+
+    def long(i, _):
+        step((begin + i * per) * UNIT, block)
+        return 0
+
+    def short(i, _):
+        step((begin + whole * per + i) * UNIT, UNIT)
+        return 0
+
+    lax.fori_loop(0, whole, long, 0)
+    lax.fori_loop(0, count - whole * per, short, 0)
+
+
 QC, AHEAD, QB, BAHEAD = 512, 1, 256, 1
 
 
@@ -71,8 +91,8 @@
         m_ref[h] = jnp.where(real, NEG, own)
         acc_ref[h] = jnp.where(real, 0.0, vt_ref[h, :, pl.ds(row0, bq)].astype(F32))
 
-    def step(j, _):
-        col0 = pl.multiple_of(j * bk, bk)
+    def step(at, bk):
+        col0 = pl.multiple_of(at, UNIT)
         work = [(h, slice(c, c + QC)) for c in range(0, bq, QC) for h in range(heads)]
         score = lambda h, c: nt(ke_ref[h, pl.ds(col0, bk), :], qe_ref[h, c, :])
         ss = [score(*w) for w in work[:AHEAD]]
@@ -86,9 +106,8 @@
             alpha = jnp.exp(m_old - m_new)
             acc_ref[h, :, c] = acc_ref[h, :, c] * alpha + nn(vt_ref[h, :, pl.ds(col0, bk)], p)
             m_ref[h, :, c] = m_new
-        return 0
-
-    lax.fori_loop(lo_ref[i], hi_ref[i], step, 0)
+
+    in_steps(lo_ref[i], hi_ref[i], bk, step)
     outs = []
     for h in range(heads):
         acc = acc_ref[h]
@@ -154,8 +173,8 @@
 
     zero = jnp.zeros((HD, bk), F32)
 
-    def step(i, carry):
-        row0 = pl.multiple_of(i * bq, bq)
+    def step(at, bq):
+        row0 = pl.multiple_of(at, UNIT)
         work = [(h, pl.ds(row0 + c, QB)) for c in range(0, bq, QB) for h in range(heads)]
         score = lambda h, c: (nt(ke_ref[h], qb_ref[h, c, :]), nt(ve_ref[h], ge_ref[h, c, :]))
         ss = [score(*w) for w in work[:BAHEAD]]
@@ -169,12 +188,11 @@
             dvt_ref[h] += nt(got_ref[h, :, c], pb)
             dkt_ref[h] += nt(qt_ref[h, :, c], ds)
             dqt_ref[h, :, c] += nn(kt_ref[h], ds)
-        return 0
 
     for h in range(heads):
         dkt_ref[h] = zero
         dvt_ref[h] = zero
-    lax.fori_loop(lo_ref[j], hi_ref[j], step, 0)
+    in_steps(lo_ref[j], hi_ref[j], bq, step)
     for h in range(heads):
         for part, ref in ((1, dkt_ref), (2, dvt_ref)):
             at = (part * heads + h) * HD
@@ -659,7 +677,7 @@
     own = rows // shards
     tb = min(256, own)
     parts = own // tb
-    inside = parts // 2
+    inside = max(1, parts // 4)
     blocks = unit.shape[0] - width // HD * (3 * span // HD)
     vmem = pl.BlockSpec(memory_space=pltpu.VMEM)
     smem = pl.BlockSpec(memory_space=pltpu.SMEM)
@@ -893,24 +911,35 @@
         total += firsts_ref[n].astype(F32)
     line_ref[shards] = total[gain_row : gain_row + 16, :]
     part_ref[...] += total
+    hops = [(s, part, step) for part in range(PARTS) for s in range(1, shards) for step in range(2)]
+    hops.sort(key=lambda hop: hop[0] + hop[1])
+
+    def wave(done, upto):
+        for s, part, step in hops:
+            if done < s + part <= upto:
+                chunk = z - s if step == 0 else z + s
+                there = chunk >= 0 if step == 0 else chunk < shards
+
+                @pl.when(there)
+                def _(chunk=chunk, part=part, step=step):
+                    hop_copy(chunk, part, step).wait_recv()
+
+                pass_on((step, chunk, there), part, lambda copy: copy.start())
+
+    rounds = slots // group
     ready = 0
-    rounds = slots // group
     for g in range(rounds):
-        soap_group(g * group, group, part_ref, *states, *outs, aug_ref)
-        upto = PARTS * (g + 1) // rounds
+        upto = PARTS * (g + 1) // (2 * rounds)
         while ready < upto:
             norm_part(ready)
+            wave(ready - 1, ready)
             ready += 1
-    hops = [(s, part, step) for s in range(1, shards) for part in range(PARTS) for step in range(2)]
-    for s, part, step in hops:
-        chunk = z - s if step == 0 else z + s
-        there = chunk >= 0 if step == 0 else chunk < shards
-
-        @pl.when(there)
-        def _(chunk=chunk, part=part, step=step):
-            hop_copy(chunk, part, step).wait_recv()
-
-        pass_on((step, chunk, there), part, lambda copy: copy.start())
+        soap_group(g * group, group, part_ref, *states, *outs, aug_ref)
+    while ready < PARTS:
+        norm_part(ready)
+        wave(ready - 1, ready)
+        ready += 1
+    wave(PARTS - 1, PARTS + shards)
     for d in range(1, shards):
         line_to(d, False).wait_recv()
     for part in range(PARTS):
@@ -975,6 +1004,47 @@
     )(sel, mix, mix_full, gain_one, res, bm, normed, tokens, *states)
 
 
+def wrap_kernel(count, inside, grad_ref, outa_ref, outb_ref, *refs):
+    shards = outa_ref.shape[0]
+    olds, wide_ref, out_ref, news, sem = refs[:count], refs[count], refs[count + 1], refs[count + 2 : -1], refs[-1]
+    copies = [pltpu.make_async_copy(old, new, sem.at[k]) for k, (old, new) in enumerate(zip(olds, news))]
+    for n in range(shards):
+        copies.append(pltpu.make_async_copy(outa_ref.at[n], out_ref.at[n, :inside], sem.at[count + 2 * n]))
+        copies.append(pltpu.make_async_copy(outb_ref.at[n], out_ref.at[n, inside:], sem.at[count + 2 * n + 1]))
+
+    @pl.when(pl.program_id(0) == 0)
+    def _():
+        for copy in copies:
+            copy.start()
+
+    wide_ref[...] = grad_ref[...].astype(F32)
+
+    @pl.when(pl.program_id(0) == pl.num_programs(0) - 1)
+    def _():
+        for copy in copies:
+            copy.wait()
+
+
+def wrap(grad, out_a, out_b, olds):
+    rows, width = grad.shape
+    shards, inside, _ = out_a.shape
+    own = inside + out_b.shape[1]
+    tb = min(512, rows)
+    hbm = pl.BlockSpec(memory_space=pl.ANY)
+    blk = pl.BlockSpec((tb, width), lambda i: (i, 0))
+    return pl.pallas_call(
+        functools.partial(wrap_kernel, len(olds), inside),
+        grid=(rows // tb,),
+        in_specs=[blk, hbm, hbm] + [hbm] * len(olds),
+        out_specs=[blk, hbm] + [hbm] * len(olds),
+        out_shape=[jax.ShapeDtypeStruct((rows, width), F32), jax.ShapeDtypeStruct((shards, own, width), BF)]
+        + [jax.ShapeDtypeStruct(a.shape, a.dtype) for a in olds],
+        scratch_shapes=[pltpu.SemaphoreType.DMA((len(olds) + 2 * shards,))],
+        compiler_params=pltpu.CompilerParams(vmem_limit_bytes=60 << 20),
+        name="wrap",
+    )(grad, out_a, out_b, *olds)
+
+
 def adam_gains(grad, gain, first, second, average):
     new_first = beta_one * first + (1.0 - beta_one) * grad
     new_second = beta_two * second + (1.0 - beta_two) * grad * grad
@@ -1033,8 +1103,8 @@
     block = min(512, rows)
     low_seg = seg_row[::block]
     high_seg = seg_row[block - 1 :: block]
-    begin = jnp.sum((seg_row[None, :] < low_seg[:, None]).astype(jnp.int32), axis=1) // block
-    end = (jnp.sum((seg_row[None, :] <= high_seg[:, None]).astype(jnp.int32), axis=1) + block - 1) // block
+    begin = jnp.sum((seg_row[None, :] < low_seg[:, None]).astype(jnp.int32), axis=1) // UNIT
+    end = (jnp.sum((seg_row[None, :] <= high_seg[:, None]).astype(jnp.int32), axis=1) + UNIT - 1) // UNIT
 
     normed, qe, ke, ve, vt, mix = project(wire_own, row_own, tokens, seg, pad, gain_one, heads)
     attended, qb = attend(qe, ke, vt, pad, begin, end, block, block)
@@ -1049,14 +1119,16 @@
     out_b = lax.all_to_all(jnp.broadcast_to(out_b, (narrow, *out_b.shape)), "narrow", 0, 0)
     bm = attend_back(qb, ke, ve, back_att, attended, begin, end, block, block)
     bm, part_a, out_b = lax.optimization_barrier((bm, part_a, out_b))
-    output = jnp.concatenate([out_a, out_b], axis=1).reshape(rows, width)
     sel = jnp.minimum(owner_order, mix_blocks)
     group = next(g for g in range(min(12, slots), 0, -1) if slots % g == 0)
     states = (part_a, weights, first_moment, second_moment, average, stats, bases)
-    grad_all, lines, new_weight, new_first, new_second, new_average, new_stats, new_bases = finish(
+    grad_all, lines, *fresh = finish(
         sel, mix, mix_full, gain_one, back_res, bm, normed, tokens, states, group, wide, rows_dev, gain_row, gains_dev
     )
-    input_grad = grad_all.astype(F32)
+    input_grad, output, new_weight, new_first, new_second, new_average, new_stats, new_bases = wrap(
+        grad_all, out_a, out_b, fresh
+    )
+    output = output.reshape(rows, width)
     line = jnp.sum(lines[:, 0], axis=0)
     offset = lax.axis_index("wide") * gains_dev % LANES
     own_gain = lax.dynamic_slice_in_dim(line, offset, gains_dev, 0)

time: 457 us -> 758 us (1.66)
  Pallas kernels: 376 us -> 691 us
  other arithmetic: 18.2 us -> 6.6 us
    pallas_call x0 -> x1, Pallas kernels: none -> 321 us  [wrap(): pl.pallas_call(functools.partial(wrap_kernel, len(olds), inside), grid=(r...]
    pallas_call x1, Pallas kernels: 89.1 us -> 66.9 us  [middle(): pl.pallas_call(functools.partial(middle_kernel, shards, span, units, wide...]
    pallas_call x1, Pallas kernels: 56.9 us -> 68.3 us  [attend_back(): pl.pallas_call(functools.partial(bwd_kernel, heads, bq, bk), grid_spec=pl...]
  transfers between devices with their start and end apart: 4 -> 4, of which waited for: 2 -> 1; matrix products, arithmetic and copies ran while one was open for 1% -> 1% of each run, Pallas kernels for 24% -> 17%
where the time goes in v8:
time: 758 us; the launch traced here: 748 us
  Pallas kernels  691 us (91%)
  blocking collectives  22 us (3%)
  between operations  14.4 us (2%)
    pallas_call x1, Pallas kernels, wrap(): pl.pallas_call(functools.partial(wrap_kernel, len(olds), inside), grid=(r...  321 us
    pallas_call x1, Pallas kernels, finish(): pl.pallas_call(functools.partial(finish_kernel, shards, wide, gain_row, g...  173 us
    pallas_call x1, Pallas kernels, attend_back(): pl.pallas_call(functools.partial(bwd_kernel, heads, bq, bk), grid_spec=pl...  68.3 us
    pallas_call x1, Pallas kernels, middle(): pl.pallas_call(functools.partial(middle_kernel, shards, span, units, wide...  66.9 us
    pallas_call x1, Pallas kernels, attend(): pl.pallas_call(functools.partial(fwd_kernel, heads, bq, bk), grid_spec=pl...  46.1 us
    all_gather x1, blocking collectives, body(): lax.all_gather(wire, 'narrow', axis=0, tiled=True)  22 us
    pallas_call x1, Pallas kernels, project(): pl.pallas_call(functools.partial(project_kernel, heads, 0, 0), grid_spec=...  15.3 us
  transfers between devices with their start and end apart: 4, of which 1 were waited for; matrix products, arithmetic and copies ran while one was open for 1% of the time, Pallas kernels for 17%

profile of v8, /device:TPU:0, one launch (start us, length us, event | category | flops | bytes accessed | tf_op | source)
XLA Modules:
  0.0 747.8 jit_solution(17031957708920767696)
XLA Ops:
  7.2 0.7 convert_bitcast_fusion.1
  7.9 1.2 convert_bitcast_fusion
  9.2 0.1 pad_maximum_fusion
  9.3 0.7 fusion.1
  10.1 22.0 %all_gather.10 = bf16[3136,128]{1,0:T(8,128)(2,1)} all-gather(bf16[784,128]{1,0:T(8,128)(2,1)} %fusion.1), channel_id=1, replica_groups=mesh['wide'=8,'narrow'=4] {'narrow'}, dimensions={0}, use_global_device_ids=true | all-gather | bytes 1003520 | tf_op jit(solution)/shard_map/all_gather | solution.py:1090
  32.3 0.6 convert_element_type.36.pad_ref
  32.9 0.2 convert_reduce_fusion
  33.3 0.5 and_select_fusion
  33.8 0.5 compare_select_fusion
  34.4 0.6 multiply_add_fusion.row_ref
  34.9 4.2 all-gather.3.cloned.1.call-done.wire_ref
  39.1 0.7 slice.34
  39.8 0.6 fusion.6
  40.4 15.3 %project.1 = (bf16[4096,512]{1,0:T(8,128)(2,1)}, bf16[2,4096,128]{2,1,0:T(8,128)(2,1)}, bf16[2,4096,128]{2,1,0:T(8,128)(2,1)}, bf16[2,4096,128]{2,1,0:T(8,128)(2...) custom-call(s32[192]{0:T(256)} %multiply_add_fusion.row_ref, ...), custom_call_target="tpu_custom_call" | custom-call | tf_op jit(solution)/shard_map/project/pallas_call | solution.py:412
  55.8 46.1 %attend.1 = (bf16[4096,128]{1,0:T(8,128)(2,1)}, bf16[2,4096,128]{2,1,0:T(8,128)(2,1)}) custom-call(s32[8]{0:T(128)} %get-tuple-element.93.lo_ref, s32[8]{0:T(128)} %get-tuple-element.92.hi_ref, bf16[2,4096,128]{2,1,0:T(8,128)(2,1)} %get-tuple-element.46.qe_ref, bf16[2,4096,128]{2,1,0:T(8,128)(2,1)} %get-tuple-element.47.ke_ref, ...), custom_call_target="tpu_custom_call" | custom-call | tf_op jit(solution)/shard_map/attend/pallas_call | solution.py:124
  101.9 66.9 %middle.1 = (bf16[4,256,512]{2,1,0:T(8,128)(2,1)}, bf16[768,512]{1,0:T(8,128)(2,1)}, f32[1024,512]{1,0:T(8,128)}, bf16[4096,128]{1,0:T(8,128)(2,1)}, bf16[32,784...) custom-call(s32[192]{0:T(256)} %get-tuple-element.94.unit_ref, s32[192]{0:T(256)} %get-tuple-element.90.sel_ref, ...), custom_call_target="tpu_custom_call" | custom-call | tf_op jit(solution)/shard_map/middle/pallas_call | solution.py:686
  168.8 1.1 copy-done
  169.9 1.9 broadcast_in_dim.31
  171.8 5.3 all-to-all-start
  177.1 68.3 %attend_back.1.bm_ref = bf16[4096,384]{1,0:T(8,128)(2,1)} custom-call(s32[8]{0:T(128)} %get-tuple-element.93.lo_ref, s32[8]{0:T(128)} %get-tuple-element.92.hi_ref, bf16[2,4096,128]{2,1,0:T(8,128)(2,1)} %get-tuple-element.52.qb_ref, bf16[2,4096,128]{2,1,0:T(8,128)(2,1)} %get-tuple-element.47.ke_ref, bf16[2,4096,128]{2,1,0:T(8,128)(2,1)} %get-tuple-element.53.ve_ref, ...), custom_call_target="tpu_custom_call" | custom-call | tf_op jit(solution)/shard_map/attend_back/pallas_call | solution.py:215
  245.5 173.0 %finish.1 = (bf16[4096,512]{1,0:T(8,128)(2,1)}, f32[5,16,128]{2,1,0:T(8,128)}, f32[1,24,64,64]{3,2,1,0:T(8,128)}, f32[1,24,64,64]{3,2,1,0:T(8,128)}, f32[1,24,64...) custom-call(s32[192]{0:T(256)} %get-tuple-element.91.sel_ref, ...), custom_call_target="tpu_custom_call" | custom-call | tf_op jit(solution)/shard_map/finish/pallas_call | solution.py:972
  418.6 0.7 slice_reduce_fusion
  419.4 0.5 add_multiply_fusion
  419.9 320.9 %wrap.1 = (f32[4096,512]{1,0:T(8,128)}, bf16[4,1024,512]{2,1,0:T(8,128)(2,1)}, f32[1,24,64,64]{3,2,1,0:T(8,128)}, f32[1,24,64,64]{3,2,1,0:T(8,128)}, f32[1,24,64...) custom-call(bf16[4096,512]{1,0:T(8,128)(2,1)} %get-tuple-element.60.g, ...), custom_call_target="tpu_custom_call" | custom-call | tf_op jit(solution)/shard_map/wrap/pallas_call | solution.py:1035
  (29 shorter events, 0.6 us)
Async XLA Ops:
  7.2 31.9 %all-gather.3.cloned.1.call-start = ((), (), s32[]{:S(2)}) async-start(), calls=%async_computation.2 | async-start | bytes 1806336 | tf_op jit(solution)/shard_map/all_gather | solution.py:1089
  9.1 23.0 %copy-start.1 = (s32[1,4096]{1,0:T(1,128)S(1)}, s32[1,4096]{1,0:T(1,128)}, u32[]{:S(2)}) copy-start(s32[1,4096]{1,0:T(1,128)} %seg_ref.1) | copy-start | bytes 49156
  9.1 23.2 %copy-start.2 = (s32[1,4096]{1,0:T(1,128)S(1)}, s32[1,4096]{1,0:T(1,128)}, u32[]{:S(2)}) copy-start(s32[1,4096]{1,0:T(1,128)} %param.18) | copy-start | bytes 49156
  9.1 24.0 %copy-start.3 = (s32[192]{0:T(256)S(1)}, s32[192]{0:T(256)}, u32[]{:S(2)}) copy-start(s32[192]{0:T(256)} %param.19) | copy-start | bytes 2308
  10.0 91.9 %all-gather.5.cloned.1.call-start = ((), (), s32[]{:S(2)}) async-start(), calls=%async_computation.3 | async-start | bytes 7225344 | tf_op jit(solution)/shard_map/all_gather | solution.py:1090
  32.0 213.4 %reduce-scatter.2.cloned.1.call-start = ((), (), s32[]{:S(2)}) async-start(), calls=%async_computation.4 | async-start | bytes 7225344 | tf_op jit(solution)/shard_map/reduce_scatter | solution.py:1118
  168.7 1.1 copy-start
  171.8 73.7 %all-to-all-start = ((bf16[4,768,512]{2,1,0:T(8,128)(2,1)}), bf16[4,768,512]{2,1,0:T(8,128)(2,1)}, u32[]{:S(2)}, u32[]{:S(2)}) async-start(bf16[4,768,512]{2,1,0:T(8,128)(2,1)} %broadcast_in_dim.31), calls=%async_computation.1 | async-start | bytes 6291456 | tf_op jit(solution)/shard_map/all_to_all | solution.py:1119
  245.5 173.8 %copy-start.4 = (f32[128]{0:T(128)S(1)}, f32[128]{0:T(128)}, u32[]{:S(2)}) copy-start(f32[128]{0:T(128)} %param.26) | copy-start | bytes 1540
  245.5 173.8 %copy-start.5 = (f32[128]{0:T(128)S(1)}, f32[128]{0:T(128)}, u32[]{:S(2)}) copy-start(f32[128]{0:T(128)} %param.29) | copy-start | bytes 1540
  245.5 173.8 %copy-start.6 = (f32[128]{0:T(128)S(1)}, f32[128]{0:T(128)}, u32[]{:S(2)}) copy-start(f32[128]{0:T(128)} %param.27) | copy-start | bytes 1540
  245.5 173.8 %copy-start.7 = (f32[128]{0:T(128)S(1)}, f32[128]{0:T(128)}, u32[]{:S(2)}) copy-start(f32[128]{0:T(128)} %param.28) | copy-start | bytes 1540
Sparse Core Ops, SparseCore 0:
  10.5 28.5 all-gather.2
  41.0 46.0 all-gather.4
  168.9 62.5 reduce-scatter.1
